TPU v7x, 128 devices: a whole 4x4x4 slice. The times are simulated.
128 devices in a mesh: patch: 16 (over x, z_lo, core), tensor: 8 (over y, z_hi).
Axes of the slice: x: 4, y: 4, z: 4 (z_hi: 2, z_lo: 2; z = z_hi * 2 + z_lo), core: 2. Of those that a mesh axis runs over, the one named last changes fastest.
Arguments:
- query: bfloat16 [8192, 5120], P('patch', 'tensor'), may hold values from -6 to 6
- key_fresh: bfloat16 [8192, 5120], P('patch', 'tensor'), may hold values from -6 to 6
- value_fresh: bfloat16 [8192, 5120], P('patch', 'tensor'), may hold values from -6 to 6
- key_stale: bfloat16 [8192, 5120], P('patch', 'tensor'), may hold values from -6 to 6
- value_stale: bfloat16 [8192, 5120], P('patch', 'tensor'), may hold values from -6 to 6
- out_weight: bfloat16 [5120, 5120], P('tensor'), may hold values from -0.078125 to 0.078125
- residual: bfloat16 [8192, 5120], P('patch', 'tensor'), may hold values from -6 to 6
- gate: float32 [5120], P('tensor'), may hold values from 0.5 to 1.5
Outputs:
- block_out: bfloat16 [8192, 5120], P('patch', 'tensor')
All inputs are finite; a program needn't handle non-finite values.
Results may differ from a plain program's by a relative error of at most 0.006.
Values may be sent and summed in bfloat16 or wider, within the bound.
No kernel may reach another device: no remote copies, remote signals or barrier semaphores. Data moves between devices by JAX's collectives and lax.ppermute only.
A program may use at most 128 MiB of HBM per device.

v0:
```python
import math

import jax
import jax.numpy as jnp
from jax import lax
from jax.sharding import PartitionSpec as P

HD = 128


def softmax_step(carry, query3, keys, values):
    run_max, run_total, accum = carry
    count = keys.shape[0]
    heads = query3.shape[1]
    keys3 = keys.reshape(count, heads, HD)
    values3 = values.reshape(count, heads, HD)
    scores = jnp.einsum("qhd,khd->qhk", query3, keys3, preferred_element_type=jnp.float32) * HD ** (
        -0.5
    )
    new_max = jnp.maximum(run_max, jnp.max(scores, axis=-1))
    factor = jnp.exp(run_max - new_max)
    expo = jnp.exp(scores - new_max[..., None])
    new_total = run_total * factor + jnp.sum(expo, axis=-1)
    mixed = jnp.einsum(
        "qhk,khd->qhd", expo.astype(jnp.bfloat16), values3, preferred_element_type=jnp.float32
    )
    return (new_max, new_total, accum * factor[..., None] + mixed)


def fold_keys(carry, pieces, query3, fresh_pair, own_first):
    keys, values = pieces
    count = keys.shape[0]
    local = query3.shape[0]
    block = math.gcd(count, 1024)

    def inner(step, state):
        first = step * block
        key_rows = lax.dynamic_slice_in_dim(keys, first, block, 0)
        value_rows = lax.dynamic_slice_in_dim(values, first, block, 0)
        position = first + jnp.arange(block, dtype=jnp.int32)
        inside = (position >= own_first) & (position < own_first + local)
        within = jnp.clip(position - own_first, 0, local - 1)
        key_rows = jnp.where(inside[:, None], fresh_pair[0][within], key_rows)
        value_rows = jnp.where(inside[:, None], fresh_pair[1][within], value_rows)
        return softmax_step(state, query3, key_rows, value_rows)

    return lax.fori_loop(0, count // block, inner, carry)


def body(query, key_fresh, value_fresh, key_stale, value_stale, out_weight, residual, gate):
    local = query.shape[0]
    heads = query.shape[1] // HD
    own_first = lax.axis_index("patch") * local
    query3 = query.reshape(local, heads, HD)
    start_carry = (
        jnp.full((local, heads), -1e30, jnp.float32),
        jnp.zeros((local, heads), jnp.float32),
        jnp.zeros((local, heads, HD), jnp.float32),
    )
    run_max, run_total, accum = fold_keys(
        start_carry,
        (
            lax.all_gather(key_stale, "patch", axis=0, tiled=True),
            lax.all_gather(value_stale, "patch", axis=0, tiled=True),
        ),
        query3,
        (key_fresh, value_fresh),
        own_first,
    )
    attended = (accum / run_total[..., None]).astype(jnp.bfloat16).reshape(local, heads * HD)
    width = out_weight.shape[1]
    share = width // lax.axis_size("tensor")
    whole = lax.psum(
        jnp.dot(attended, out_weight, preferred_element_type=jnp.float32).astype(jnp.bfloat16),
        "tensor",
    ).astype(jnp.float32)
    mine = lax.dynamic_slice_in_dim(whole, lax.axis_index("tensor") * share, share, 1)
    return (residual.astype(jnp.float32) + gate[None, :] * mine).astype(jnp.bfloat16)


def solution(mesh):
    in_specs = (
        P("patch", "tensor"),
        P("patch", "tensor"),
        P("patch", "tensor"),
        P("patch", "tensor"),
        P("patch", "tensor"),
        P("tensor", None),
        P("patch", "tensor"),
        P("tensor"),
    )
    out_specs = P("patch", "tensor")
    return jax.shard_map(body, mesh=mesh, in_specs=in_specs, out_specs=out_specs, check_vma=False)
```

profile of v0, /device:TPU:18, one launch (start us, length us, event | category | flops | bytes accessed | tf_op | source)
XLA Modules:
  0.0 579.2 jit_solution(12198199217972934188)
XLA Ops:
  8.7 64.3 %all-gather.3.cloned.1.call-done = bf16[8192,640]{1,0:T(8,128)(2,1)} async-done(((bf16[512,640]{1,0:T(8,128)(2,1)}), bf16[8192,640]{1,0:T(8,128)(2,1)}) %all-gather.3.cloned.1.call-update) | async-done | bytes 10485776 | tf_op jit(solution)/shard_map/all_gather | solution.py:63
  73.0 64.5 %all-gather.5.cloned.1.call-done = bf16[8192,640]{1,0:T(8,128)(2,1)} async-done(((bf16[512,640]{1,0:T(8,128)(2,1)}), bf16[8192,640]{1,0:T(8,128)(2,1)}) %all-gather.5.cloned.1.call-update) | async-done | bytes 10485776 | tf_op jit(solution)/shard_map/all_gather | solution.py:64
  137.5 195.4 %while.19 = (s32[]{:T(128)}, f32[512,5]{0,1:T(8,128)S(1)}, f32[512,5]{0,1:T(8,128)S(1)}, f32[512,5,128]{0,2,1:T(8,128)}, s32[]{:T(128)}, /*index=5*/s32[]{:T(128...) while((s32[]{:T(128)}, f32[512,5]{0,1:T(8,128)S(1)}, ...), condition=%wide.region_3.4_spmd.clone, body=%wide.region_0.3_spmd.clone.sunk | while | flops 1365466624 | bytes 71620920 | solution.py:47
  137.6 4.0 gather_fusion.1
  141.6 5.2 gather_fusion
  146.8 4.3 dynamic-slice_select_fusion.3
  152.7 2.5 copy.23
  158.6 2.3 fusion.38
  162.0 4.0 gather_fusion.1
  166.0 5.2 gather_fusion
  171.2 4.3 dynamic-slice_select_fusion.3
  177.1 2.5 copy.23
  181.2 1.7 fusion.36
  183.0 2.3 fusion.38
  186.4 4.0 gather_fusion.1
  190.5 5.2 gather_fusion
  195.6 4.3 dynamic-slice_select_fusion.3
  201.5 2.5 copy.23
  205.7 1.7 fusion.36
  207.4 2.3 fusion.38
  210.8 4.0 gather_fusion.1
  214.9 5.2 gather_fusion
  220.1 4.3 dynamic-slice_select_fusion.3
  226.0 2.5 copy.23
  231.8 2.3 fusion.38
  235.3 4.0 gather_fusion.1
  239.3 5.2 gather_fusion
  244.5 4.3 dynamic-slice_select_fusion.3
  250.4 2.5 copy.23
  256.3 2.3 fusion.38
  259.7 4.0 gather_fusion.1
  263.7 5.2 gather_fusion
  268.9 4.3 dynamic-slice_select_fusion.3
  274.8 2.5 copy.23
  280.7 2.3 fusion.38
  284.1 4.0 gather_fusion.1
  288.2 5.2 gather_fusion
  293.3 4.3 dynamic-slice_select_fusion.3
  299.3 2.5 copy.23
  305.1 2.3 fusion.38
  308.6 4.0 gather_fusion.1
  312.6 5.2 gather_fusion
  317.8 4.3 dynamic-slice_select_fusion.3
  323.7 2.5 copy.23
  329.6 2.3 fusion.38
  334.4 8.9 %convolution_convert_fusion = bf16[512,5120]{1,0:T(8,128)(2,1)} fusion(bf16[512,640]{0,1:T(8,128)(2,1)S(1)} %bitcast.51, bf16[640,5120]{1,0:T(8,128)(2,1)} %param.15), kind=kOutput, calls=%fused_computation.26 | convolution fusion | flops 3358064640 | bytes 12451840 | tf_op jit(solution)/shard_map/dot_general | solution.py:74
  343.4 227.2 %all-reduce.2.cloned.1.call-done = bf16[512,5120]{1,0:T(8,128)(2,1)} async-done(((bf16[512,5120]{1,0:T(8,128)(2,1)}), bf16[512,5120]{1,0:T(8,128)(2,1)}) %all-reduce.2.cloned.1.call-update) | async-done | bytes 5242896 | tf_op jit(solution)/shard_map/psum | solution.py:73
  570.6 2.1 add_convert_fusion
  (140 shorter events, 48.4 us)
Async XLA Ops:
  6.5 1.6 copy-start.5
  6.5 66.5 %all-gather.3.cloned.1.call-start = ((), (), s32[]{:S(2)}) async-start(), calls=%async_computation | async-start | bytes 11141120 | tf_op jit(solution)/shard_map/all_gather | solution.py:63
  7.3 130.3 %all-gather.5.cloned.1.call-start = ((), (), s32[]{:S(2)}) async-start(), calls=%async_computation.1 | async-start | bytes 11141120 | tf_op jit(solution)/shard_map/all_gather | solution.py:64
  8.0 562.5 %all-reduce.2.cloned.1.call-start = ((), (), s32[]{:S(2)}) async-start(), calls=%async_computation.2 | async-start | bytes 10485760 | tf_op jit(solution)/shard_map/psum | solution.py:73
  8.1 129.4 %copy-start = (bf16[512,640]{1,0:T(8,128)(2,1)S(1)}, bf16[512,640]{1,0:T(8,128)(2,1)}, u32[]{:S(2)}) copy-start(bf16[512,640]{1,0:T(8,128)(2,1)} %param.11) | copy-start | bytes 1966084
  8.1 129.4 %copy-start.1 = (bf16[512,640]{1,0:T(8,128)(2,1)S(1)}, bf16[512,640]{1,0:T(8,128)(2,1)}, u32[]{:S(2)}) copy-start(bf16[512,640]{1,0:T(8,128)(2,1)} %param.12) | copy-start | bytes 1966084
  156.8 1.8 copy-start.2
  156.8 1.8 copy-start.3
  160.9 1.1 copy-start.4
  181.2 1.8 copy-start.2
  181.2 1.8 copy-start.3
  185.3 1.1 copy-start.4
  205.6 1.8 copy-start.2
  205.7 1.8 copy-start.3
  209.7 1.1 copy-start.4
  230.1 1.8 copy-start.2
  230.1 1.8 copy-start.3
  234.1 1.1 copy-start.4
  254.5 1.8 copy-start.2
  254.5 1.8 copy-start.3
  258.6 1.1 copy-start.4
  278.9 1.8 copy-start.2
  278.9 1.8 copy-start.3
  283.0 1.1 copy-start.4
  303.4 1.8 copy-start.2
  303.4 1.8 copy-start.3
  307.4 1.1 copy-start.4
  327.8 1.8 copy-start.2
  327.8 1.8 copy-start.3
  331.9 1.1 copy-start.4
  343.4 227.2 %copy-start.6 = (bf16[512,640]{1,0:T(8,128)(2,1)S(1)}, bf16[512,640]{1,0:T(8,128)(2,1)}, u32[]{:S(2)}) copy-start(bf16[512,640]{1,0:T(8,128)(2,1)} %param.16) | copy-start | bytes 1966084
  343.4 227.2 %copy-start.7 = (f32[640]{0:T(1024)S(1)}, f32[640]{0:T(1024)}, u32[]{:S(2)}) copy-start(f32[640]{0:T(1024)} %param.17) | copy-start | bytes 7684
Sparse Core Ops, SparseCore 0:
  9.0 63.9 all-gather.2
  74.7 62.7 all-gather.4
  343.5 226.9 all-reduce.1
where the time goes:
time: 580 us; the launch traced here: 579 us
  waiting for transfers between devices  357 us (62%)
  local copies, waits for them, and re-layouts  116 us (20%)
  other arithmetic  52.1 us (9%)
  matrix products  39.8 us (7%)
  between operations  13.2 us (2%)
    psum x1, waiting for transfers between devices, body(): lax.psum(jnp.dot(attended, out_weight, preferred_element_type=jnp.float32...  227 us
    all_gather x1, waiting for transfers between devices, body(): lax.all_gather(value_stale, 'patch', axis=0, tiled=True)  64.5 us
    all_gather x1, waiting for transfers between devices, body(): lax.all_gather(key_stale, 'patch', axis=0, tiled=True)  64.3 us
    gather x8, local copies, waits for them, and re-layouts, inner(): value_rows = jnp.where(inside[:, None], fresh_pair[1][within], value_rows)  41.4 us
    select_n x8, other arithmetic, inner(): value_rows = jnp.where(inside[:, None], fresh_pair[1][within], value_rows)  34.4 us
    gather x8, local copies, waits for them, and re-layouts, inner(): key_rows = jnp.where(inside[:, None], fresh_pair[0][within], key_rows)  32.2 us
    select_n x8, local copies, waits for them, and re-layouts, inner(): value_rows = jnp.where(inside[:, None], fresh_pair[1][within], value_rows)  20 us
    dot_general x8, matrix products, softmax_step(): jnp.einsum('qhk,khd->qhd', expo.astype(jnp.bfloat16), values3, preferred_...  18.2 us
  transfers between devices with their start and end apart: 3, of which 3 were waited for; matrix products, arithmetic and copies ran while one was open for 0% of the time, Pallas kernels for 0%

commit v1 on v0

v1 whole, which is shorter than its diff:
```python
import functools
import math

import jax
import jax.numpy as jnp
from jax import lax
from jax.experimental import pallas as pl
from jax.experimental.pallas import tpu as pltpu
from jax.sharding import PartitionSpec as P


HD = 128
STAT = 16
TO_LOG2 = math.log2(math.e) / math.sqrt(HD)
AXES = ("x", "zl", "c", "y", "zh")
NT = (((1,), (1,)), ((), ()))
TN = (((0,), (0,)), ((), ()))


def ring(n, k):
    return [(i, (i + k) % n) for i in range(n)]


def dot(a, b, dims):
    return lax.dot_general(a, b, dims, preferred_element_type=jnp.float32)


def attend(q, pieces):
    scores = [dot(k, q, NT) for k, _ in pieces]
    top = functools.reduce(jnp.maximum, [jnp.max(s, axis=0, keepdims=True) for s in scores])
    total, mixed = None, None
    for s, (_, v) in zip(scores, pieces, strict=True):
        expo = jnp.exp2((s - top) * TO_LOG2)
        part = jnp.sum(expo, axis=0, keepdims=True)
        out = dot(v, expo.astype(jnp.bfloat16), TN)
        total = part if total is None else total + part
        mixed = out if mixed is None else mixed + out
    return mixed * (1.0 / total), top * TO_LOG2 + jnp.log2(total)


def flash_kernel(own, qa_ref, qb_ref, kv_ref, sib_ref, z_ref, zs_ref, *refs):
    if own:
        kf_ref, vf_ref, oa_ref, ob_ref, stat = refs
    else:
        oa_ref, ob_ref, stat = refs
    h = pl.program_id(0)
    n = qa_ref.shape[0]

    def halves(ref):
        return ref[0:n, :], ref[n : 2 * n, :]

    shared = [halves(sib_ref), halves(z_ref), halves(zs_ref)]
    rows = pl.ds(pl.multiple_of(h * HD, HD), HD)
    for index, (q_ref, o_ref) in enumerate(((qa_ref, oa_ref), (qb_ref, ob_ref))):
        first = (kf_ref[...], vf_ref[...]) if own and index == 1 else halves(kv_ref)
        out, lse = attend(q_ref[...], [first, *shared])
        o_ref[rows, :] = out.astype(jnp.bfloat16)
        stat[index, pl.ds(h, 1), :] = lse

    @pl.when(h == pl.num_programs(0) - 1)
    def _():
        for index, o_ref in enumerate((oa_ref, ob_ref)):
            lse = stat[index]
            high = lse.astype(jnp.bfloat16)
            low = (lse - high.astype(jnp.float32)).astype(jnp.bfloat16)
            o_ref[pl.num_programs(0) * HD : pl.num_programs(0) * HD + STAT, :] = jnp.concatenate([high, low], axis=0)


def flash(qa, qb, kvs, fresh):
    n, width = qa.shape
    heads = width // HD
    q_spec = pl.BlockSpec((n, HD), lambda h: (0, h))
    kv_spec = pl.BlockSpec((2 * n, HD), lambda h: (0, h))
    o_spec = pl.BlockSpec((width + STAT, n), lambda h: (0, 0))
    o_shape = jax.ShapeDtypeStruct((width + STAT, n), jnp.bfloat16)
    return pl.pallas_call(
        functools.partial(flash_kernel, bool(fresh)),
        out_shape=(o_shape, o_shape),
        grid=(heads,),
        in_specs=[q_spec] * 2 + [kv_spec] * len(kvs) + [q_spec] * len(fresh),
        out_specs=(o_spec, o_spec),
        scratch_shapes=[pltpu.VMEM((2, 8, n), jnp.float32)],
        compiler_params=pltpu.CompilerParams(vmem_limit_bytes=56 << 20),
        cost_estimate=pl.CostEstimate(
            flops=4 * 2 * n * 4 * n * width, bytes_accessed=24 * n * width, transcendentals=8 * n * n * heads
        ),
    )(qa, qb, *kvs, *fresh)


def merge_kernel(*refs):
    *parts, out_ref = refs
    width = out_ref.shape[1]
    stats = []
    for ref in parts:
        both = ref[width : width + STAT, :].astype(jnp.float32)
        stats.append(both[0:8] + both[8:16])
    top = functools.reduce(jnp.maximum, stats)
    weights = [jnp.exp2(s - top) for s in stats]
    total = functools.reduce(jnp.add, weights)
    weights = [w * (1.0 / total) for w in weights]
    for h in range(width // HD):
        mixed = None
        for ref, w in zip(parts, weights, strict=True):
            term = ref[h * HD : (h + 1) * HD, :].astype(jnp.float32) * w[h : h + 1, :]
            mixed = term if mixed is None else mixed + term
        out_ref[:, h * HD : (h + 1) * HD] = mixed.T.astype(jnp.bfloat16)


def merge(parts):
    rows, n = parts[0].shape
    return pl.pallas_call(
        merge_kernel,
        out_shape=jax.ShapeDtypeStruct((n, rows - STAT), jnp.bfloat16),
        compiler_params=pltpu.CompilerParams(vmem_limit_bytes=32 << 20),
        cost_estimate=pl.CostEstimate(flops=8 * rows * n, bytes_accessed=10 * rows * n, transcendentals=0),
    )(*parts)


def project_kernel(where, att_ref, other_ref, w_ref, wz_ref, ws_ref, *outs):
    j = pl.program_id(0)
    target = lax.rem(where[0] + j, 4)
    mine = lax.div(target, 2) == where[2]
    other_w = jnp.where(mine, wz_ref[...], ws_ref[...])
    total = jnp.dot(att_ref[...], w_ref[...], preferred_element_type=jnp.float32)
    total = total + jnp.dot(other_ref[...], other_w, preferred_element_type=jnp.float32)
    result = total.astype(jnp.bfloat16)
    for index, out_ref in enumerate(outs):

        @pl.when(j == index)
        def _():
            out_ref[...] = result


def project(where, att, other, w, wz, ws):
    n, width = att.shape
    act = pl.BlockSpec((n, width), lambda j, where: (0, 0))
    half = pl.BlockSpec((width, width), lambda j, where: (lax.rem(where[0] + j, 2), 0))
    out = jax.ShapeDtypeStruct((n, width), jnp.bfloat16)
    return pl.pallas_call(
        project_kernel,
        out_shape=(out,) * 4,
        grid_spec=pltpu.PrefetchScalarGridSpec(
            num_scalar_prefetch=1,
            grid=(4,),
            in_specs=[
                act,
                act,
                pl.BlockSpec((width, width), lambda j, where: (0, lax.rem(where[0] + j, 4) * 2 + where[1])),
                half,
                half,
            ],
            out_specs=(pl.BlockSpec((n, width), lambda j, where: (0, 0)),) * 4,
        ),
        compiler_params=pltpu.CompilerParams(vmem_limit_bytes=40 << 20),
        cost_estimate=pl.CostEstimate(
            flops=16 * n * width * width, bytes_accessed=24 * width * width + 12 * n * width, transcendentals=0
        ),
    )(where, att, other, w, wz, ws)


def block(query, key_fresh, value_fresh, key_stale, value_stale, out_weight, residual, gate):
    width = query.shape[1]
    y, zh, c = lax.axis_index("y"), lax.axis_index("zh"), lax.axis_index("c")
    swap = ring(2, 1)

    kv = jnp.concatenate([key_stale, value_stale], axis=0)
    kv_z = lax.ppermute(kv, "zl", swap)
    q1 = lax.ppermute(query, "x", ring(4, 1))
    q3 = lax.ppermute(query, "x", ring(4, 3))
    q2 = lax.ppermute(query, "x", ring(4, 2))
    kv_s = lax.ppermute(kv, "c", swap)
    kv_zs = lax.ppermute(kv_z, "c", swap)

    sent = [
        lax.dynamic_slice_in_dim(out_weight, ((2 * c + i) * 2 + 1 - zh) * width, width, 1) for i in range(2)
    ]
    w_z = lax.ppermute(jnp.concatenate(sent, axis=0), ("zl", "zh"), [(0, 3), (3, 0), (1, 2), (2, 1)])
    w_s = lax.ppermute(w_z, "c", swap)

    kvs = (kv, kv_s, kv_z, kv_zs)
    o1, o2 = flash(q1, q2, kvs, ())
    o3, o0 = flash(q3, query, kvs, (key_fresh, value_fresh))
    parts = (
        o0, lax.ppermute(o1, "x", ring(4, 3)), lax.ppermute(o2, "x", ring(4, 2)), lax.ppermute(o3, "x", ring(4, 1))
    )
    attended = merge(parts)
    other = lax.ppermute(attended, "zh", swap)
    where = jnp.stack([y, zh, c]).astype(jnp.int32)
    pieces = project(where, attended, other, out_weight, w_z, w_s)
    whole = pieces[0].astype(jnp.float32)
    for j in range(1, 4):
        whole = whole + lax.ppermute(pieces[j], "y", ring(4, j)).astype(jnp.float32)
    return (residual.astype(jnp.float32) + gate[None, :] * whole).astype(jnp.bfloat16)


def solution(mesh):
    fine = jax.sharding.Mesh(mesh.devices.reshape(4, 2, 2, 4, 2), AXES)
    rows, cols = ("x", "zl", "c"), ("y", "zh")
    spec = P(rows, cols)
    in_specs = (spec, spec, spec, spec, spec, P(cols, None), spec, P(cols))
    return jax.shard_map(block, mesh=fine, in_specs=in_specs, out_specs=spec, check_vma=False)
```

time: 580 us -> 192 us (0.33)
  waiting for transfers between devices: 357 us -> 111 us
  local copies, waits for them, and re-layouts: 116 us -> 11.7 us
  other arithmetic: 52.1 us -> 1.51 us
  Pallas kernels: 0 us -> 47.1 us
  matrix products: 39.8 us -> 0 us
  starting transfers between devices: 0.08 us -> 17.2 us
  between operations: 13.2 us -> 0.07 us
    psum x1 -> x0, waiting for transfers between devices: 227 us -> none  [body(): lax.psum(jnp.dot(attended, out_weight, preferred_element_type=jnp.float32...]
    all_gather x2 -> x0, waiting for transfers between devices: 129 us -> none  [the longest x1 64.5 us: body(): lax.all_gather(value_stale, 'patch', axis=0, tiled=True)]
    ppermute x0 -> x15, waiting for transfers between devices: none -> 111 us  [the longest x3 27.4 us: block(): whole = whole + lax.ppermute(pieces[j], 'y', ring(4, j)).astype(jnp.float32)]
    gather x16 -> x0, local copies, waits for them, and re-layouts: 73.6 us -> none  [the longest x8 41.4 us: inner(): value_rows = jnp.where(inside[:, None], fresh_pair[1][within], value_rows)]
    pallas_call x0 -> x4, Pallas kernels: none -> 47.1 us  [the longest x2 38.7 us: flash(): pl.pallas_call(functools.partial(flash_kernel, bool(fresh)), out_shape=(o...]
    dot_general x17 -> x0, matrix products: 39.8 us -> none  [the longest x8 18.2 us: softmax_step(): jnp.einsum('qhk,khd->qhd', expo.astype(jnp.bfloat16), values3, preferred_...]
    select_n x16 -> x0, other arithmetic: 34.5 us -> none  [the longest x8 34.4 us: inner(): value_rows = jnp.where(inside[:, None], fresh_pair[1][within], value_rows)]
    select_n x16 -> x0, local copies, waits for them, and re-layouts: 32.8 us -> none  [the longest x8 20 us: inner(): value_rows = jnp.where(inside[:, None], fresh_pair[1][within], value_rows)]
  transfers between devices with their start and end apart: 3 -> 15, of which waited for: 3 -> 8; matrix products, arithmetic and copies ran while one was open for 0% -> 1% of each run, Pallas kernels for 0% -> 21%
where the time goes in v1:
time: 192 us; the launch traced here: 189 us
  waiting for transfers between devices  111 us (58%)
  Pallas kernels  47.1 us (25%)
  starting transfers between devices  17.2 us (9%)
  local copies, waits for them, and re-layouts  11.7 us (6%)
    pallas_call x2, Pallas kernels, flash(): pl.pallas_call(functools.partial(flash_kernel, bool(fresh)), out_shape=(o...  38.7 us
    ppermute x3, waiting for transfers between devices, block(): whole = whole + lax.ppermute(pieces[j], 'y', ring(4, j)).astype(jnp.float32)  27.4 us
    ppermute x1, waiting for transfers between devices, block(): kv_z = lax.ppermute(kv, 'zl', swap)  24.8 us
    ppermute x1, waiting for transfers between devices, block(): q2 = lax.ppermute(query, 'x', ring(4, 2))  16.5 us
    ppermute x1, waiting for transfers between devices, block(): other = lax.ppermute(attended, 'zh', swap)  13.3 us
    ppermute x1, waiting for transfers between devices, block(): q1 = lax.ppermute(query, 'x', ring(4, 1))  13.1 us
    unnamed x23, local copies, waits for them, and re-layouts  9.24 us
    ppermute x1, waiting for transfers between devices, block(): lax.ppermute(o2, 'x', ring(4, 2))  8.46 us
  transfers between devices with their start and end apart: 15, of which 8 were waited for; matrix products, arithmetic and copies ran while one was open for 1% of the time, Pallas kernels for 21%

profile of v1, /device:TPU:18, one launch (start us, length us, event | category | flops | bytes accessed | tf_op | source)
XLA Modules:
  0.0 188.9 jit_solution(3607902990175914522)
XLA Ops:
  0.0 2.1 %constant_dynamic-update-slice_fusion.1 = bf16[1024,640]{1,0:T(8,128)(2,1)} fusion(bf16[512,640]{1,0:T(8,128)(2,1)} %param.11), kind=kLoop, calls=%fused_computation.3 | loop fusion | bytes 1310720
  2.1 0.9 constant_dynamic-update-slice_fusion.kv_ref
  3.0 1.9 %collective-permute-start.2 = (bf16[1024,640]{1,0:T(8,128)(2,1)}, bf16[1024,640]{1,0:T(8,128)(2,1)}, u32[]{:S(2)}, u32[]{:S(2)}) collective-permute-start(bf16[1024,640]{1,0:T(8,128)(2,1)} %constant_dynamic-update-slice_fusion.kv_ref), channel_id=1, source_target_pairs={{0,16},{16,0},{1,17},{17,1},{2,18},{18,2},{3,19},{19,3},{4,20},{20... | collective-permute-start | bytes 3932168 | tf_op jit(solution)/shard_map/ppermute | solution.py:167
  4.9 1.5 constant_dynamic-slice_fusion.1
  6.4 0.0 copy-start.7
  6.5 0.1 pad_maximum_fusion
  6.6 2.6 %collective-permute-start.10 = (bf16[1280,640]{1,0:T(8,128)(2,1)S(1)}, bf16[1280,640]{1,0:T(8,128)(2,1)S(1)}, u32[]{:S(2)}, u32[]{:S(2)}) collective-permute-start(bf16[1280,640]{1,0:T(8,128)(2,1)S(1)} %pad_maximum_fusion), channel_id=1, source_target_pairs={{0,17},{17,0},{1,16},{16,1},{2,19},{19,2},{3,18},{18,3},{4,21},{21... | collective-permute-start | bytes 4915208 | tf_op jit(solution)/shard_map/ppermute | solution.py:177
  9.2 0.0 collective-permute-start.1
  9.2 24.8 %collective-permute-done.2.z_ref = bf16[1024,640]{1,0:T(8,128)(2,1)} collective-permute-done((bf16[1024,640]{1,0:T(8,128)(2,1)}, bf16[1024,640]{1,0:T(8,128)(2,1)}, u32[]{:S(2)}, u32[]{:S(2)}) %collective-permute-start.2) | collective-permute-done | bytes 1310752 | tf_op jit(solution)/shard_map/ppermute | solution.py:167
  34.0 0.0 collective-permute-start.3
  34.0 2.1 %collective-permute-start.5 = (bf16[512,640]{1,0:T(8,128)(2,1)S(1)}, bf16[512,640]{1,0:T(8,128)(2,1)S(1)}, u32[]{:S(2)}, u32[]{:S(2)}) collective-permute-start(bf16[512,640]{1,0:T(8,128)(2,1)S(1)} %copy-done.7), channel_id=1, source_target_pairs={{0,64},{32,96},{64,0},{96,32},{1,65},{33,97},{65,1},{97,33},{2,66}... | collective-permute-start | bytes 1966088 | tf_op jit(solution)/shard_map/ppermute | solution.py:170
  36.1 0.0 collective-permute-start.4
  36.1 16.5 %collective-permute-done.5.qb_ref = bf16[512,640]{1,0:T(8,128)(2,1)S(1)} collective-permute-done((bf16[512,640]{1,0:T(8,128)(2,1)S(1)}, bf16[512,640]{1,0:T(8,128)(2,1)S(1)}, u32[]{:S(2)}, u32[]{:S(2)}) %collective-permute-start.5) | collective-permute-done | bytes 655392 | tf_op jit(solution)/shard_map/ppermute | solution.py:170
  52.6 1.0 collective-permute-start
  53.7 0.0 collective-permute-done.10.wz_ref
  53.7 0.0 collective-permute-start.11
  53.7 13.1 %collective-permute-done.4.qa_ref = bf16[512,640]{1,0:T(8,128)(2,1)S(1)} collective-permute-done((bf16[512,640]{1,0:T(8,128)(2,1)S(1)}, bf16[512,640]{1,0:T(8,128)(2,1)S(1)}, u32[]{:S(2)}, u32[]{:S(2)}) %collective-permute-start.4) | collective-permute-done | bytes 655392 | tf_op jit(solution)/shard_map/ppermute | solution.py:168
  66.8 0.0 collective-permute-done.1.sib_ref
  66.8 0.0 collective-permute-done.3.zs_ref
  66.8 0.0 copy-done.9
  66.8 0.8 copy-done.10
  67.6 0.4 copy-done.5
  68.0 1.1 copy-done.6
  69.2 19.3 %shard_map.83 = (bf16[656,512]{1,0:T(8,128)(2,1)}, bf16[656,512]{1,0:T(8,128)(2,1)}) custom-call(bf16[512,640]{1,0:T(8,128)(2,1)} %copy-done.10, bf16[512,640]{1,0:T(8,128)(2,1)} %copy-done.9, bf16[1024,640]{1,0:T(8,128)(2,1)} %constant_dynamic-update-slice_fusion.kv_ref, bf16[1024,640]{1,0:T(8,128)(2,1)} %copy-done.5, ...), custom_call_target="tpu_custom_call" | custom-call | flops 5368709120 | bytes 7864320 | tf_op jit(solution)/shard_map/pallas_call | solution.py:76
  88.5 0.5 collective-permute-start.6
  88.9 1.5 collective-permute-start.7
  90.5 0.0 collective-permute-done.qa_ref
  90.5 0.8 copy-done.8
  91.3 19.4 %shard_map.82 = (bf16[656,512]{1,0:T(8,128)(2,1)}, bf16[656,512]{1,0:T(8,128)(2,1)}) custom-call(bf16[512,640]{1,0:T(8,128)(2,1)} %copy-done.8, bf16[512,640]{1,0:T(8,128)(2,1)} %qb_ref.1, bf16[1024,640]{1,0:T(8,128)(2,1)} %constant_dynamic-update-slice_fusion.kv_ref, bf16[1024,640]{1,0:T(8,128)(2,1)} %copy-done.5, ...), custom_call_target="tpu_custom_call" | custom-call | flops 5368709120 | bytes 7864320 | tf_op jit(solution)/shard_map/pallas_call | solution.py:76
  110.7 0.5 collective-permute-start.8
  111.2 0.0 collective-permute-done.6.refs_1_
  111.2 8.5 %collective-permute-done.7.refs_2_ = bf16[656,512]{1,0:T(8,128)(2,1)S(1)} collective-permute-done((bf16[656,512]{1,0:T(8,128)(2,1)}, bf16[656,512]{1,0:T(8,128)(2,1)S(1)}, u32[]{:S(2)}, u32[]{:S(2)}) %collective-permute-start.7) | collective-permute-done | bytes 671776 | tf_op jit(solution)/shard_map/ppermute | solution.py:184
  119.7 7.6 %collective-permute-done.8.refs_3_ = bf16[656,512]{1,0:T(8,128)(2,1)S(1)} collective-permute-done((bf16[656,512]{1,0:T(8,128)(2,1)}, bf16[656,512]{1,0:T(8,128)(2,1)S(1)}, u32[]{:S(2)}, u32[]{:S(2)}) %collective-permute-start.8) | collective-permute-done | bytes 671776 | tf_op jit(solution)/shard_map/ppermute | solution.py:184
  127.4 1.1 copy-done
  128.4 0.6 shard_map.84.att_ref
  129.1 4.0 %collective-permute-start.9 = (bf16[512,640]{1,0:T(8,128)(2,1)S(1)}, bf16[512,640]{1,0:T(8,128)(2,1)S(1)}, u32[]{:S(2)}, u32[]{:S(2)}) collective-permute-start(bf16[512,640]{1,0:T(8,128)(2,1)S(1)} %shard_map.84.att_ref), channel_id=1, source_target_pairs={{0,1},{1,0},{2,3},{3,2},{4,5},{5,4},{6,7},{7,6},{8,9},{9,8},{10,11... | collective-permute-start | bytes 1966088 | tf_op jit(solution)/shard_map/ppermute | solution.py:187
  133.1 0.1 pad_add_fusion.where
  133.1 0.0 collective-permute-done.11.ws_ref
  133.1 13.3 %collective-permute-done.9.other_ref = bf16[512,640]{1,0:T(8,128)(2,1)S(1)} collective-permute-done((bf16[512,640]{1,0:T(8,128)(2,1)S(1)}, bf16[512,640]{1,0:T(8,128)(2,1)S(1)}, u32[]{:S(2)}, u32[]{:S(2)}) %collective-permute-start.9) | collective-permute-done | bytes 655392 | tf_op jit(solution)/shard_map/ppermute | solution.py:187
  146.5 2.9 %copy-done.1 = bf16[640,5120]{1,0:T(8,128)(2,1)S(1)} copy-done((bf16[640,5120]{1,0:T(8,128)(2,1)S(1)}, bf16[640,5120]{1,0:T(8,128)(2,1)}, u32[]{:S(2)}) %copy-start.1) | copy-done | bytes 6553624
  149.3 7.8 %shard_map.85 = (bf16[512,640]{1,0:T(8,128)(2,1)S(1)}, bf16[512,640]{1,0:T(8,128)(2,1)S(1)}, bf16[512,640]{1,0:T(8,128)(2,1)S(1)}, bf16[512,640]{1,0:T(8,128)(2,1)S(1)}) custom-call(s32[3]{0:T(128)S(1)} %pad_add_fusion.where, bf16[512,640]{1,0:T(8,128)(2,1)S(1)} %shard_map.84.att_ref, bf16[512,640]{1,0:T(8,128)(2,1)S(1)} %collective-permute-done.9.other_ref, ...), custom_call_target="tpu_custom_call" | custom-call | flops 3355443200 | bytes 13762560 | tf_op jit(solution)/shard_map/pallas_call | solution.py:139
  157.1 1.4 collective-permute-start.12
  158.4 0.6 collective-permute-start.13
  159.1 1.1 collective-permute-start.14
  160.2 25.6 %collective-permute-done.12 = bf16[512,640]{1,0:T(8,128)(2,1)S(1)} collective-permute-done((bf16[512,640]{1,0:T(8,128)(2,1)S(1)}, bf16[512,640]{1,0:T(8,128)(2,1)S(1)}, u32[]{:S(2)}, u32[]{:S(2)}) %collective-permute-start.12) | collective-permute-done | bytes 655392 | tf_op jit(solution)/shard_map/ppermute | solution.py:192
  185.8 0.0 collective-permute-done.13
  185.8 1.8 collective-permute-done.14
  187.6 1.3 add_convert_fusion
  (14 shorter events, 0.0 us)
Async XLA Ops:
  0.0 2.1 %copy-start.2 = (bf16[512,640]{1,0:T(8,128)(2,1)S(1)}, bf16[512,640]{1,0:T(8,128)(2,1)}, u32[]{:S(2)}) copy-start(bf16[512,640]{1,0:T(8,128)(2,1)} %param.12) | copy-start | bytes 1966084
  3.0 31.0 %collective-permute-start.2 = (bf16[1024,640]{1,0:T(8,128)(2,1)}, bf16[1024,640]{1,0:T(8,128)(2,1)}, u32[]{:S(2)}, u32[]{:S(2)}) collective-permute-start(bf16[1024,640]{1,0:T(8,128)(2,1)} %constant_dynamic-update-slice_fusion.kv_ref), channel_id=1, source_target_pairs={{0,16},{16,0},{1,17},{17,1},{2,18},{18,2},{3,19},{19,3},{4,20},{20... | collective-permute-start | bytes 3932168 | tf_op jit(solution)/shard_map/ppermute | solution.py:167
  6.4 27.6 %copy-start.7 = (bf16[512,640]{1,0:T(8,128)(2,1)S(1)}, bf16[512,640]{1,0:T(8,128)(2,1)}, u32[]{:S(2)}) copy-start(bf16[512,640]{1,0:T(8,128)(2,1)} %qb_ref.1) | copy-start | bytes 1966084
  6.6 47.1 %collective-permute-start.10 = (bf16[1280,640]{1,0:T(8,128)(2,1)S(1)}, bf16[1280,640]{1,0:T(8,128)(2,1)S(1)}, u32[]{:S(2)}, u32[]{:S(2)}) collective-permute-start(bf16[1280,640]{1,0:T(8,128)(2,1)S(1)} %pad_maximum_fusion), channel_id=1, source_target_pairs={{0,17},{17,0},{1,16},{16,1},{2,19},{19,2},{3,18},{18,3},{4,21},{21... | collective-permute-start | bytes 4915208 | tf_op jit(solution)/shard_map/ppermute | solution.py:177
  9.2 57.6 %collective-permute-start.1 = (bf16[1024,640]{1,0:T(8,128)(2,1)}, bf16[1024,640]{1,0:T(8,128)(2,1)S(1)}, u32[]{:S(2)}, u32[]{:S(2)}) collective-permute-start(bf16[1024,640]{1,0:T(8,128)(2,1)} %constant_dynamic-update-slice_fusion.kv_ref), channel_id=1, source_target_pairs={{0,8},{8,0},{1,9},{9,1},{2,10},{10,2},{3,11},{11,3},{4,12},{12,4},... | collective-permute-start | bytes 3932168 | tf_op jit(solution)/shard_map/ppermute | solution.py:171
  34.0 32.8 %collective-permute-start.3 = (bf16[1024,640]{1,0:T(8,128)(2,1)}, bf16[1024,640]{1,0:T(8,128)(2,1)S(1)}, u32[]{:S(2)}, u32[]{:S(2)}) collective-permute-start(bf16[1024,640]{1,0:T(8,128)(2,1)} %collective-permute-done.2.z_ref), channel_id=1, source_target_pairs={{0,8},{8,0},{1,9},{9,1},{2,10},{10,2},{3,11},{11,3},{4,12},{12,4},... | collective-permute-start | bytes 3932168 | tf_op jit(solution)/shard_map/ppermute | solution.py:172
  34.0 18.6 %collective-permute-start.5 = (bf16[512,640]{1,0:T(8,128)(2,1)S(1)}, bf16[512,640]{1,0:T(8,128)(2,1)S(1)}, u32[]{:S(2)}, u32[]{:S(2)}) collective-permute-start(bf16[512,640]{1,0:T(8,128)(2,1)S(1)} %copy-done.7), channel_id=1, source_target_pairs={{0,64},{32,96},{64,0},{96,32},{1,65},{33,97},{65,1},{97,33},{2,66}... | collective-permute-start | bytes 1966088 | tf_op jit(solution)/shard_map/ppermute | solution.py:170
  36.1 30.6 %collective-permute-start.4 = (bf16[512,640]{1,0:T(8,128)(2,1)S(1)}, bf16[512,640]{1,0:T(8,128)(2,1)S(1)}, u32[]{:S(2)}, u32[]{:S(2)}) collective-permute-start(bf16[512,640]{1,0:T(8,128)(2,1)S(1)} %copy-done.7), channel_id=1, source_target_pairs={{0,32},{32,64},{64,96},{96,0},{1,33},{33,65},{65,97},{97,1},{2,34}... | collective-permute-start | bytes 1966088 | tf_op jit(solution)/shard_map/ppermute | solution.py:168
  52.6 14.1 %copy-start.9 = (bf16[512,640]{1,0:T(8,128)(2,1)}, bf16[512,640]{1,0:T(8,128)(2,1)S(1)}, u32[]{:S(2)}) copy-start(bf16[512,640]{1,0:T(8,128)(2,1)S(1)} %collective-permute-done.5.qb_ref) | copy-start | bytes 1966084
  52.6 37.8 %collective-permute-start = (bf16[512,640]{1,0:T(8,128)(2,1)S(1)}, bf16[512,640]{1,0:T(8,128)(2,1)S(1)}, u32[]{:S(2)}, u32[]{:S(2)}) collective-permute-start(bf16[512,640]{1,0:T(8,128)(2,1)S(1)} %copy-done.7), channel_id=1, source_target_pairs={{0,96},{32,0},{64,32},{96,64},{1,97},{33,1},{65,33},{97,65},{2,98}... | collective-permute-start | bytes 1966088 | tf_op jit(solution)/shard_map/ppermute | solution.py:169
  53.7 79.4 %collective-permute-start.11 = (bf16[1280,640]{1,0:T(8,128)(2,1)S(1)}, bf16[1280,640]{1,0:T(8,128)(2,1)}, u32[]{:S(2)}, u32[]{:S(2)}) collective-permute-start(bf16[1280,640]{1,0:T(8,128)(2,1)S(1)} %collective-permute-done.10.wz_ref), channel_id=1, source_target_pairs={{0,8},{8,0},{1,9},{9,1},{2,10},{10,2},{3,11},{11,3},{4,12},{12,4},... | collective-permute-start | bytes 4915208 | tf_op jit(solution)/shard_map/ppermute | solution.py:178
  66.8 0.8 copy-start.10
  66.8 1.3 copy-start.5
  68.0 1.1 copy-start.6
  88.5 22.8 %collective-permute-start.6 = (bf16[656,512]{1,0:T(8,128)(2,1)}, bf16[656,512]{1,0:T(8,128)(2,1)S(1)}, u32[]{:S(2)}, u32[]{:S(2)}) collective-permute-start(bf16[656,512]{1,0:T(8,128)(2,1)} %get-tuple-element.14), channel_id=1, source_target_pairs={{0,96},{32,0},{64,32},{96,64},{1,97},{33,1},{65,33},{97,65},{2,98}... | collective-permute-start | bytes 2015240 | tf_op jit(solution)/shard_map/ppermute | solution.py:184
  88.9 30.8 %collective-permute-start.7 = (bf16[656,512]{1,0:T(8,128)(2,1)}, bf16[656,512]{1,0:T(8,128)(2,1)S(1)}, u32[]{:S(2)}, u32[]{:S(2)}) collective-permute-start(bf16[656,512]{1,0:T(8,128)(2,1)} %get-tuple-element.15), channel_id=1, source_target_pairs={{0,64},{32,96},{64,0},{96,32},{1,65},{33,97},{65,1},{97,33},{2,66}... | collective-permute-start | bytes 2015240 | tf_op jit(solution)/shard_map/ppermute | solution.py:184
  90.5 0.8 copy-start.8
  110.7 16.6 %collective-permute-start.8 = (bf16[656,512]{1,0:T(8,128)(2,1)}, bf16[656,512]{1,0:T(8,128)(2,1)S(1)}, u32[]{:S(2)}, u32[]{:S(2)}) collective-permute-start(bf16[656,512]{1,0:T(8,128)(2,1)} %get-tuple-element.16), channel_id=1, source_target_pairs={{0,32},{32,64},{64,96},{96,0},{1,33},{33,65},{65,97},{97,1},{2,34}... | collective-permute-start | bytes 2015240 | tf_op jit(solution)/shard_map/ppermute | solution.py:184
  127.4 1.1 copy-start
  129.1 17.4 %collective-permute-start.9 = (bf16[512,640]{1,0:T(8,128)(2,1)S(1)}, bf16[512,640]{1,0:T(8,128)(2,1)S(1)}, u32[]{:S(2)}, u32[]{:S(2)}) collective-permute-start(bf16[512,640]{1,0:T(8,128)(2,1)S(1)} %shard_map.84.att_ref), channel_id=1, source_target_pairs={{0,1},{1,0},{2,3},{3,2},{4,5},{5,4},{6,7},{7,6},{8,9},{9,8},{10,11... | collective-permute-start | bytes 1966088 | tf_op jit(solution)/shard_map/ppermute | solution.py:187
  146.5 2.9 %copy-start.1 = (bf16[640,5120]{1,0:T(8,128)(2,1)S(1)}, bf16[640,5120]{1,0:T(8,128)(2,1)}, u32[]{:S(2)}) copy-start(bf16[640,5120]{1,0:T(8,128)(2,1)} %w_ref.1) | copy-start | bytes 19660804
  149.3 38.3 %copy-start.3 = (bf16[512,640]{1,0:T(8,128)(2,1)S(1)}, bf16[512,640]{1,0:T(8,128)(2,1)}, u32[]{:S(2)}) copy-start(bf16[512,640]{1,0:T(8,128)(2,1)} %param.14) | copy-start | bytes 1966084
  149.3 38.3 %copy-start.4 = (f32[640]{0:T(1024)S(1)}, f32[640]{0:T(1024)}, u32[]{:S(2)}) copy-start(f32[640]{0:T(1024)} %param.15) | copy-start | bytes 7684
  157.1 28.7 %collective-permute-start.12 = (bf16[512,640]{1,0:T(8,128)(2,1)S(1)}, bf16[512,640]{1,0:T(8,128)(2,1)S(1)}, u32[]{:S(2)}, u32[]{:S(2)}) collective-permute-start(bf16[512,640]{1,0:T(8,128)(2,1)S(1)} %get-tuple-element.18), channel_id=1, source_target_pairs={{0,2},{2,4},{4,6},{6,0},{1,3},{3,5},{5,7},{7,1},{8,10},{10,12},{12... | collective-permute-start | bytes 1966088 | tf_op jit(solution)/shard_map/ppermute | solution.py:192
  158.4 27.3 %collective-permute-start.13 = (bf16[512,640]{1,0:T(8,128)(2,1)S(1)}, bf16[512,640]{1,0:T(8,128)(2,1)S(1)}, u32[]{:S(2)}, u32[]{:S(2)}) collective-permute-start(bf16[512,640]{1,0:T(8,128)(2,1)S(1)} %get-tuple-element.19), channel_id=1, source_target_pairs={{0,4},{2,6},{4,0},{6,2},{1,5},{3,7},{5,1},{7,3},{8,12},{10,14},{12... | collective-permute-start | bytes 1966088 | tf_op jit(solution)/shard_map/ppermute | solution.py:192
  159.1 28.5 %collective-permute-start.14 = (bf16[512,640]{1,0:T(8,128)(2,1)S(1)}, bf16[512,640]{1,0:T(8,128)(2,1)S(1)}, u32[]{:S(2)}, u32[]{:S(2)}) collective-permute-start(bf16[512,640]{1,0:T(8,128)(2,1)S(1)} %get-tuple-element.20), channel_id=1, source_target_pairs={{0,6},{2,0},{4,2},{6,4},{1,7},{3,1},{5,3},{7,5},{8,14},{10,8},{12,... | collective-permute-start | bytes 1966088 | tf_op jit(solution)/shard_map/ppermute | solution.py:192

commit v2 on v1

v2 whole, which is shorter than its diff:
```python
import functools
import math

import jax
import jax.numpy as jnp
from jax import lax
from jax.experimental import pallas as pl
from jax.experimental.pallas import tpu as pltpu
from jax.sharding import PartitionSpec as P


HD = 128
STAT = 16
CHUNKS = 2
TO_LOG2 = math.log2(math.e) / math.sqrt(HD)
AXES = ("x", "zl", "c", "y", "zh")
NT = (((1,), (1,)), ((), ()))
TN = (((0,), (0,)), ((), ()))


def ring(n, k):
    return [(i, (i + k) % n) for i in range(n)]


def dot(a, b, dims):
    return lax.dot_general(a, b, dims, preferred_element_type=jnp.float32)


def attend(q, k, v):
    scores = dot(k, q, NT)
    top = jnp.max(scores, axis=0, keepdims=True)
    expo = jnp.exp2((scores - top) * TO_LOG2)
    return dot(v, expo.astype(jnp.bfloat16), TN), jnp.sum(expo, axis=0, keepdims=True), top * TO_LOG2


def attend_all(q, pieces, extra=()):
    raw = [attend(q, k, v) for k, v in pieces]
    tops = [t for _, _, t in raw] + [lse for _, lse in extra]
    top = functools.reduce(jnp.maximum, tops)
    scaled = [(o, total, jnp.exp2(t - top)) for o, total, t in raw] + [(o, 1.0, jnp.exp2(lse - top)) for o, lse in extra]
    total = functools.reduce(jnp.add, [part * w for _, part, w in scaled])
    inverse = 1.0 / total
    out = functools.reduce(jnp.add, [o * (w * inverse) for o, _, w in scaled])
    return out, top + jnp.log2(total)


def halves(ref):
    n = ref.shape[0] // 2
    return ref[0:n, :], ref[n : 2 * n, :]


def early_kernel(n_q, fresh, *refs):
    q_refs, refs = refs[:n_q], refs[n_q:]
    if fresh:
        own, refs = (refs[0][...], refs[1][...]), refs[2:]
    else:
        own, refs = halves(refs[0]), refs[1:]
    pieces = [own, halves(refs[0])]
    outs = refs[1:]
    h = pl.program_id(0)
    for index, q_ref in enumerate(q_refs):
        out, lse = attend_all(q_ref[...], pieces)
        outs[2 * index][...] = out
        outs[2 * index + 1][pl.ds(h, 1), :] = lse


def early(queries, own, sibling):
    n, width = queries[0].shape
    heads = width // HD
    q_spec = pl.BlockSpec((n, HD), lambda h: (0, h))
    kv_spec = pl.BlockSpec((2 * n, HD), lambda h: (0, h))
    count = len(queries)
    return pl.pallas_call(
        functools.partial(early_kernel, count, len(own) == 2),
        out_shape=(
            jax.ShapeDtypeStruct((width, n), jnp.float32),
            jax.ShapeDtypeStruct((8, n), jnp.float32),
        )
        * count,
        grid=(heads,),
        in_specs=[q_spec] * count + ([q_spec] * 2 if len(own) == 2 else [kv_spec]) + [kv_spec],
        out_specs=(pl.BlockSpec((HD, n), lambda h: (h, 0)), pl.BlockSpec((8, n), lambda h: (0, 0))) * count,
        compiler_params=pltpu.CompilerParams(vmem_limit_bytes=40 << 20),
        cost_estimate=pl.CostEstimate(
            flops=count * 8 * n * n * width, bytes_accessed=16 * n * width, transcendentals=count * 2 * n * n * heads
        ),
    )(*queries, *own, sibling)


def late_kernel(qa_ref, qb_ref, z_ref, zs_ref, ea_ref, la_ref, eb_ref, lb_ref, oa_ref, ob_ref, stat):
    h = pl.program_id(0)
    heads = pl.num_programs(0)
    n = qa_ref.shape[0]
    q = jnp.concatenate([qa_ref[...], qb_ref[...]], axis=0)
    before = jnp.concatenate([ea_ref[...], eb_ref[...]], axis=1)
    before_lse = jnp.concatenate([la_ref[pl.ds(h, 1), :], lb_ref[pl.ds(h, 1), :]], axis=1)
    out, lse = attend_all(q, [halves(z_ref), halves(zs_ref)], [(before, before_lse)])
    out = out.astype(jnp.bfloat16)
    rows = pl.ds(pl.multiple_of(h * HD, HD), HD)
    oa_ref[rows, :] = out[:, 0:n]
    ob_ref[rows, :] = out[:, n : 2 * n]
    stat[pl.ds(h, 1), :] = lse

    @pl.when(h == heads - 1)
    def _():
        high = stat[...].astype(jnp.bfloat16)
        low = (stat[...] - high.astype(jnp.float32)).astype(jnp.bfloat16)
        both = jnp.concatenate([high, low], axis=0)
        base = heads * HD
        oa_ref[base : base + STAT, :] = both[:, 0:n]
        ob_ref[base : base + STAT, :] = both[:, n : 2 * n]


def late(chunk, qa, qb, z, zs, ea, eb):
    whole, width = qa.shape
    n = whole // CHUNKS
    heads = width // HD
    q_spec = pl.BlockSpec((n, HD), lambda h: (chunk, h))
    kv_spec = pl.BlockSpec((2 * whole, HD), lambda h: (0, h))
    e_specs = [pl.BlockSpec((HD, n), lambda h: (h, chunk)), pl.BlockSpec((8, n), lambda h: (0, chunk))]
    o_shape = jax.ShapeDtypeStruct((width + STAT, n), jnp.bfloat16)
    return pl.pallas_call(
        late_kernel,
        out_shape=(o_shape, o_shape),
        grid=(heads,),
        in_specs=[q_spec] * 2 + [kv_spec] * 2 + e_specs * 2,
        out_specs=(pl.BlockSpec((width + STAT, n), lambda h: (0, 0)),) * 2,
        scratch_shapes=[pltpu.VMEM((8, 2 * n), jnp.float32)],
        compiler_params=pltpu.CompilerParams(vmem_limit_bytes=40 << 20),
        cost_estimate=pl.CostEstimate(
            flops=16 * n * whole * width, bytes_accessed=20 * n * width, transcendentals=4 * n * whole * heads
        ),
    )(qa, qb, z, zs, *ea, *eb)


def merge_kernel(*refs):
    *parts, out_ref = refs
    width = out_ref.shape[1]
    stats = []
    for ref in parts:
        both = ref[width : width + STAT, :].astype(jnp.float32)
        stats.append(both[0:8] + both[8:16])
    top = functools.reduce(jnp.maximum, stats)
    weights = [jnp.exp2(s - top) for s in stats]
    total = functools.reduce(jnp.add, weights)
    weights = [w * (1.0 / total) for w in weights]
    for h in range(width // HD):
        mixed = None
        for ref, w in zip(parts, weights, strict=True):
            term = ref[h * HD : (h + 1) * HD, :].astype(jnp.float32) * w[h : h + 1, :]
            mixed = term if mixed is None else mixed + term
        out_ref[:, h * HD : (h + 1) * HD] = mixed.T.astype(jnp.bfloat16)


def merge(parts):
    rows, n = parts[0].shape
    return pl.pallas_call(
        merge_kernel,
        out_shape=jax.ShapeDtypeStruct((n, rows - STAT), jnp.bfloat16),
        compiler_params=pltpu.CompilerParams(vmem_limit_bytes=16 << 20),
        cost_estimate=pl.CostEstimate(flops=8 * rows * n, bytes_accessed=10 * rows * n, transcendentals=0),
    )(*parts)


def project_kernel(where, att_ref, other_ref, w_ref, wz_ref, ws_ref, *outs):
    j = pl.program_id(0)
    target = lax.rem(where[0] + j, 4)
    mine = lax.div(target, 2) == where[2]
    other_w = jnp.where(mine, wz_ref[...], ws_ref[...])
    total = jnp.dot(att_ref[...], w_ref[...], preferred_element_type=jnp.float32)
    total = total + jnp.dot(other_ref[...], other_w, preferred_element_type=jnp.float32)
    result = total.astype(jnp.bfloat16)
    for index, out_ref in enumerate(outs):

        @pl.when(j == index)
        def _():
            out_ref[...] = result


def project(where, att, other, w, wz, ws):
    n, width = att.shape
    act = pl.BlockSpec((n, width), lambda j, where: (0, 0))
    half = pl.BlockSpec((width, width), lambda j, where: (lax.rem(where[0] + j, 2), 0))
    out = jax.ShapeDtypeStruct((n, width), jnp.bfloat16)
    return pl.pallas_call(
        project_kernel,
        out_shape=(out,) * 4,
        grid_spec=pltpu.PrefetchScalarGridSpec(
            num_scalar_prefetch=1,
            grid=(4,),
            in_specs=[
                act,
                act,
                pl.BlockSpec((width, width), lambda j, where: (0, lax.rem(where[0] + j, 4) * 2 + where[1])),
                half,
                half,
            ],
            out_specs=(pl.BlockSpec((n, width), lambda j, where: (0, 0)),) * 4,
        ),
        compiler_params=pltpu.CompilerParams(vmem_limit_bytes=40 << 20),
        cost_estimate=pl.CostEstimate(
            flops=16 * n * width * width, bytes_accessed=24 * width * width + 12 * n * width, transcendentals=0
        ),
    )(where, att, other, w, wz, ws)


def block(query, key_fresh, value_fresh, key_stale, value_stale, out_weight, residual, gate):
    width = query.shape[1]
    y, zh, c = lax.axis_index("y"), lax.axis_index("zh"), lax.axis_index("c")
    where = jnp.stack([y, zh, c]).astype(jnp.int32)
    swap = ring(2, 1)

    kv = jnp.concatenate([key_stale, value_stale], axis=0)
    kv_z = lax.ppermute(kv, "zl", swap)
    kv_s = lax.ppermute(kv, "c", swap)
    q1 = lax.ppermute(query, "x", ring(4, 1))
    q3 = lax.ppermute(query, "x", ring(4, 3))
    q2 = lax.ppermute(query, "x", ring(4, 2))
    kv_zs = lax.ppermute(kv_z, "c", swap)

    sent = [
        lax.dynamic_slice_in_dim(out_weight, ((2 * c + i) * 2 + 1 - zh) * width, width, 1) for i in range(2)
    ]
    w_z = lax.ppermute(jnp.concatenate(sent, axis=0), ("zl", "zh"), [(0, 3), (3, 0), (1, 2), (2, 1)])
    w_s = lax.ppermute(w_z, "c", swap)

    e0 = early((query,), (key_fresh, value_fresh), kv_s)
    e1, l1, e3, l3 = early((q1, q3), (kv,), kv_s)
    e2 = early((q2,), (kv,), kv_s)

    results = []
    for i in range(CHUNKS):
        o2, o1 = late(i, q2, q1, kv_z, kv_zs, e2, (e1, l1))
        o3, o0 = late(i, q3, query, kv_z, kv_zs, (e3, l3), e0)
        parts = (
            o0, lax.ppermute(o1, "x", ring(4, 3)), lax.ppermute(o2, "x", ring(4, 2)), lax.ppermute(o3, "x", ring(4, 1))
        )
        attended = merge(parts)
        other = lax.ppermute(attended, "zh", swap)
        pieces = project(where, attended, other, out_weight, w_z, w_s)
        whole = pieces[0].astype(jnp.float32)
        for j in range(1, 4):
            whole = whole + lax.ppermute(pieces[j], "y", ring(4, j)).astype(jnp.float32)
        results.append(whole)
    whole = jnp.concatenate(results, axis=0)
    return (residual.astype(jnp.float32) + gate[None, :] * whole).astype(jnp.bfloat16)


def solution(mesh):
    fine = jax.sharding.Mesh(mesh.devices.reshape(4, 2, 2, 4, 2), AXES)
    rows, cols = ("x", "zl", "c"), ("y", "zh")
    spec = P(rows, cols)
    in_specs = (spec, spec, spec, spec, spec, P(cols, None), spec, P(cols))
    return jax.shard_map(block, mesh=fine, in_specs=in_specs, out_specs=spec, check_vma=False)
```

time: 192 us -> 169 us (0.88); the launches traced: 189 us -> 168 us
  waiting for transfers between devices: 111 us -> 61.4 us
  Pallas kernels: 47.1 us -> 68.3 us
  starting transfers between devices: 17.2 us -> 29.2 us
  local copies, waits for them, and re-layouts: 11.7 us -> 7.4 us
    ppermute x1, waiting for transfers between devices: 16.5 us -> 0.01 us  [block(): q2 = lax.ppermute(query, 'x', ring(4, 2))]
    pallas_call x2 -> x7, Pallas kernels: 38.7 us -> 55.1 us  [the longest x4 28.6 us: late(): pl.pallas_call(late_kernel, out_shape=(o_shape, o_shape), grid=(heads,),...]
    ppermute x1 -> x2, waiting for transfers between devices: 13.3 us -> 0.01 us  [block(): other = lax.ppermute(attended, 'zh', swap)]
    ppermute x1, waiting for transfers between devices: 13.1 us -> 0.01 us  [block(): q1 = lax.ppermute(query, 'x', ring(4, 1))]
    ppermute x3 -> x6, waiting for transfers between devices: 27.4 us -> 17.6 us  [block(): whole = whole + lax.ppermute(pieces[j], 'y', ring(4, j)).astype(jnp.float32)]
    ppermute x1, waiting for transfers between devices: 0.01 us -> 9.26 us  [block(): lax.ppermute(jnp.concatenate(sent, axis=0), ('zl', 'zh'), [(0, 3), (3, 0)...]
    ppermute x1 -> x2, waiting for transfers between devices: 7.64 us -> 0.01 us  [block(): lax.ppermute(o3, 'x', ring(4, 1))]
    ppermute x1 -> x2, waiting for transfers between devices: 0.01 us -> 4.68 us  [block(): lax.ppermute(o1, 'x', ring(4, 3))]
  transfers between devices with their start and end apart: 15 -> 22, of which waited for: 8 -> 10; matrix products, arithmetic and copies ran while one was open for 1% -> 1% of each run, Pallas kernels for 21% -> 41%
where the time goes in v2:
time: 169 us; the launch traced here: 168 us
  Pallas kernels  68.3 us (40%)
  waiting for transfers between devices  61.4 us (36%)
  starting transfers between devices  29.2 us (17%)
  local copies, waits for them, and re-layouts  7.4 us (4%)
    pallas_call x4, Pallas kernels, late(): pl.pallas_call(late_kernel, out_shape=(o_shape, o_shape), grid=(heads,),...  28.6 us
    pallas_call x3, Pallas kernels, early(): pl.pallas_call(functools.partial(early_kernel, count, len(own) == 2), out...  26.5 us
    ppermute x1, waiting for transfers between devices, block(): kv_z = lax.ppermute(kv, 'zl', swap)  22.5 us
    ppermute x6, waiting for transfers between devices, block(): whole = whole + lax.ppermute(pieces[j], 'y', ring(4, j)).astype(jnp.float32)  17.6 us
    pallas_call x2, Pallas kernels, project(): pl.pallas_call(project_kernel, out_shape=(out,) * 4, grid_spec=pltpu.Pref...  11.4 us
    ppermute x1, waiting for transfers between devices, block(): lax.ppermute(jnp.concatenate(sent, axis=0), ('zl', 'zh'), [(0, 3), (3, 0)...  9.26 us
    ppermute x6, starting transfers between devices, block(): whole = whole + lax.ppermute(pieces[j], 'y', ring(4, j)).astype(jnp.float32)  7.71 us
    ppermute x2, waiting for transfers between devices, block(): lax.ppermute(o2, 'x', ring(4, 2))  7.36 us
  transfers between devices with their start and end apart: 22, of which 10 were waited for; matrix products, arithmetic and copies ran while one was open for 1% of the time, Pallas kernels for 41%

profile of v2, /device:TPU:18, one launch (start us, length us, event | category | flops | bytes accessed | tf_op | source)
XLA Modules:
  0.0 168.0 jit_solution(3170195140555317565)
XLA Ops:
  0.0 2.1 %constant_dynamic-update-slice_fusion.1 = bf16[1024,640]{1,0:T(8,128)(2,1)} fusion(bf16[512,640]{1,0:T(8,128)(2,1)} %param.11), kind=kLoop, calls=%fused_computation.7 | loop fusion | bytes 1310720
  2.1 0.9 constant_dynamic-update-slice_fusion.refs_2_.refs_1_
  3.0 1.9 %collective-permute-start.1 = (bf16[1024,640]{1,0:T(8,128)(2,1)}, bf16[1024,640]{1,0:T(8,128)(2,1)S(1)}, u32[]{:S(2)}, u32[]{:S(2)}) collective-permute-start(bf16[1024,640]{1,0:T(8,128)(2,1)} %constant_dynamic-update-slice_fusion.refs_2_.refs_1_), channel_id=1, source_target_pairs={{0,16},{16,0},{1,17},{17,1},{2,18},{18,2},{3,19},{19,3},{4,20},{20... | collective-permute-start | bytes 3932168 | tf_op jit(solution)/shard_map/ppermute | solution.py:214
  4.9 1.5 constant_dynamic-slice_fusion.1
  6.4 0.1 pad_maximum_fusion
  6.6 2.6 %collective-permute-start.10 = (bf16[1280,640]{1,0:T(8,128)(2,1)S(1)}, bf16[1280,640]{1,0:T(8,128)(2,1)S(1)}, u32[]{:S(2)}, u32[]{:S(2)}) collective-permute-start(bf16[1280,640]{1,0:T(8,128)(2,1)S(1)} %pad_maximum_fusion), channel_id=1, source_target_pairs={{0,17},{17,0},{1,16},{16,1},{2,19},{19,2},{3,18},{18,3},{4,21},{21... | collective-permute-start | bytes 4915208 | tf_op jit(solution)/shard_map/ppermute | solution.py:224
  9.2 2.1 %collective-permute-start.5 = (bf16[512,640]{1,0:T(8,128)(2,1)S(1)}, bf16[512,640]{1,0:T(8,128)(2,1)S(1)}, u32[]{:S(2)}, u32[]{:S(2)}) collective-permute-start(bf16[512,640]{1,0:T(8,128)(2,1)S(1)} %copy-done.1), channel_id=1, source_target_pairs={{0,64},{32,96},{64,0},{96,32},{1,65},{33,97},{65,1},{97,33},{2,66}... | collective-permute-start | bytes 1966088 | tf_op jit(solution)/shard_map/ppermute | solution.py:218
  11.4 22.5 %collective-permute-done.1.z_ref = bf16[1024,640]{1,0:T(8,128)(2,1)S(1)} collective-permute-done((bf16[1024,640]{1,0:T(8,128)(2,1)}, bf16[1024,640]{1,0:T(8,128)(2,1)S(1)}, u32[]{:S(2)}, u32[]{:S(2)}) %collective-permute-start.1) | collective-permute-done | bytes 1310752 | tf_op jit(solution)/shard_map/ppermute | solution.py:214
  33.9 1.5 collective-permute-start.3
  35.4 0.5 collective-permute-start
  35.9 9.3 %collective-permute-done.10.wz_ref = bf16[1280,640]{1,0:T(8,128)(2,1)S(1)} collective-permute-done((bf16[1280,640]{1,0:T(8,128)(2,1)S(1)}, bf16[1280,640]{1,0:T(8,128)(2,1)S(1)}, u32[]{:S(2)}, u32[]{:S(2)}) %collective-permute-start.10) | collective-permute-done | bytes 1638432 | tf_op jit(solution)/shard_map/ppermute | solution.py:224
  45.2 7.3 %shard_map.85 = (f32[640,512]{1,0:T(8,128)S(1)}, f32[8,512]{1,0:T(8,128)S(1)}) custom-call(bf16[512,640]{1,0:T(8,128)(2,1)S(1)} %collective-permute-done.5.refs_0_.qa_ref, bf16[1024,640]{1,0:T(8,128)(2,1)} %constant_dynamic-update-slice_fusion.refs_2_.refs_1_, bf16[1024,640]{1,0:T(8,128)(2,1)S(1)} %collective-permute-done.4.refs_3_.refs_2_), custom_call_target="tpu_custom_call" | custom-call | flops 1342177280 | bytes 5242880 | tf_op jit(solution)/shard_map/pallas_call | solution.py:73
  52.5 6.6 %shard_map.83 = (f32[640,512]{1,0:T(8,128)S(1)}, f32[8,512]{1,0:T(8,128)S(1)}) custom-call(bf16[512,640]{1,0:T(8,128)(2,1)S(1)} %copy-done.1, bf16[512,640]{1,0:T(8,128)(2,1)S(1)} %copy-done.2, bf16[512,640]{1,0:T(8,128)(2,1)S(1)} %copy-done.3, bf16[1024,640]{1,0:T(8,128)(2,1)S(1)} %collective-permute-done.4.refs_3_.refs_2_), custom_call_target="tpu_custom_call" | custom-call | flops 1342177280 | bytes 5242880 | tf_op jit(solution)/shard_map/pallas_call | solution.py:73
  59.2 12.5 %shard_map.82 = (f32[640,512]{1,0:T(8,128)S(1)}, f32[8,512]{1,0:T(8,128)S(1)}, f32[640,512]{1,0:T(8,128)S(1)}, f32[8,512]{1,0:T(8,128)S(1)}) custom-call(bf16[512,640]{1,0:T(8,128)(2,1)S(1)} %collective-permute-done.3.refs_0_.qb_ref, bf16[512,640]{1,0:T(8,128)(2,1)S(1)} %collective-permute-done.refs_1_.qa_ref, ...), custom_call_target="tpu_custom_call" | custom-call | flops 2684354560 | bytes 5242880 | tf_op jit(solution)/shard_map/pallas_call | solution.py:73
  71.7 6.8 %shard_map.89 = (bf16[656,256]{1,0:T(8,128)(2,1)S(1)}, bf16[656,256]{1,0:T(8,128)(2,1)S(1)}) custom-call(bf16[512,640]{1,0:T(8,128)(2,1)S(1)} %collective-permute-done.refs_1_.qa_ref, bf16[512,640]{1,0:T(8,128)(2,1)S(1)} %copy-done.1, bf16[1024,640]{1,0:T(8,128)(2,1)S(1)} %collective-permute-done.1.z_ref, ...), custom_call_target="tpu_custom_call" | custom-call | flops 1342177280 | bytes 3276800 | tf_op jit(solution)/shard_map/pallas_call | solution.py:122
  78.5 1.6 collective-permute-start.17
  80.1 6.8 %shard_map.90 = (bf16[656,256]{1,0:T(8,128)(2,1)S(1)}, bf16[656,256]{1,0:T(8,128)(2,1)S(1)}) custom-call(bf16[512,640]{1,0:T(8,128)(2,1)S(1)} %collective-permute-done.5.refs_0_.qa_ref, bf16[512,640]{1,0:T(8,128)(2,1)S(1)} %collective-permute-done.3.refs_0_.qb_ref, bf16[1024,640]{1,0:T(8,128)(2,1)S(1)} %collective-permute-done.1.z_ref, ...), custom_call_target="tpu_custom_call" | custom-call | flops 1342177280 | bytes 3276800 | tf_op jit(solution)/shard_map/pallas_call | solution.py:122
  86.9 0.6 collective-permute-start.15
  87.5 2.1 %collective-permute-start.16 = (bf16[656,256]{1,0:T(8,128)(2,1)S(1)}, bf16[656,256]{1,0:T(8,128)(2,1)S(1)}, u32[]{:S(2)}, u32[]{:S(2)}) collective-permute-start(bf16[656,256]{1,0:T(8,128)(2,1)S(1)} %get-tuple-element.47), channel_id=1, source_target_pairs={{0,64},{32,96},{64,0},{96,32},{1,65},{33,97},{65,1},{97,33},{2,66}... | collective-permute-start | bytes 1007624 | tf_op jit(solution)/shard_map/ppermute | solution.py:236
  89.6 7.5 %shard_map.84 = (bf16[656,256]{1,0:T(8,128)(2,1)}, bf16[656,256]{1,0:T(8,128)(2,1)S(1)}) custom-call(bf16[512,640]{1,0:T(8,128)(2,1)S(1)} %collective-permute-done.refs_1_.qa_ref, bf16[512,640]{1,0:T(8,128)(2,1)S(1)} %copy-done.1, bf16[1024,640]{1,0:T(8,128)(2,1)S(1)} %collective-permute-done.1.z_ref, bf16[1024,640]{1,0:T(8,128)(2,1)S(1)} %collective-permute-done.2.zs_ref, ...), custom_call_target="tpu_custom_call" | custom-call | flops 1342177280 | bytes 3276800 | tf_op jit(solution)/shard_map/pallas_call | solution.py:122
  97.1 1.1 collective-permute-start.8
  98.2 7.6 %shard_map.86 = (bf16[656,256]{1,0:T(8,128)(2,1)}, bf16[656,256]{1,0:T(8,128)(2,1)}) custom-call(bf16[512,640]{1,0:T(8,128)(2,1)S(1)} %collective-permute-done.5.refs_0_.qa_ref, bf16[512,640]{1,0:T(8,128)(2,1)S(1)} %collective-permute-done.3.refs_0_.qb_ref, bf16[1024,640]{1,0:T(8,128)(2,1)S(1)} %collective-permute-done.1.z_ref, ...), custom_call_target="tpu_custom_call" | custom-call | flops 1342177280 | bytes 3276800 | tf_op jit(solution)/shard_map/pallas_call | solution.py:122
  105.7 1.0 collective-permute-start.6
  106.7 1.6 collective-permute-start.7
  108.3 0.4 shard_map.91.att_ref
  108.6 2.5 %collective-permute-start.18 = (bf16[256,640]{1,0:T(8,128)(2,1)S(1)}, bf16[256,640]{1,0:T(8,128)(2,1)}, u32[]{:S(2)}, u32[]{:S(2)}) collective-permute-start(bf16[256,640]{1,0:T(8,128)(2,1)S(1)} %shard_map.91.att_ref), channel_id=1, source_target_pairs={{0,1},{1,0},{2,3},{3,2},{4,5},{5,4},{6,7},{7,6},{8,9},{9,8},{10,11... | collective-permute-start | bytes 983048 | tf_op jit(solution)/shard_map/ppermute | solution.py:239
  111.1 4.7 %collective-permute-done.6.refs_1_ = bf16[656,256]{1,0:T(8,128)(2,1)S(1)} collective-permute-done((bf16[656,256]{1,0:T(8,128)(2,1)}, bf16[656,256]{1,0:T(8,128)(2,1)S(1)}, u32[]{:S(2)}, u32[]{:S(2)}) %collective-permute-start.6) | collective-permute-done | bytes 335904 | tf_op jit(solution)/shard_map/ppermute | solution.py:236
  115.8 7.4 %collective-permute-done.7.refs_2_ = bf16[656,256]{1,0:T(8,128)(2,1)} collective-permute-done((bf16[656,256]{1,0:T(8,128)(2,1)}, bf16[656,256]{1,0:T(8,128)(2,1)}, u32[]{:S(2)}, u32[]{:S(2)}) %collective-permute-start.7) | collective-permute-done | bytes 335904 | tf_op jit(solution)/shard_map/ppermute | solution.py:236
  123.1 1.4 shard_map.87.att_ref
  124.6 2.5 %collective-permute-start.9 = (bf16[256,640]{1,0:T(8,128)(2,1)S(1)}, bf16[256,640]{1,0:T(8,128)(2,1)S(1)}, u32[]{:S(2)}, u32[]{:S(2)}) collective-permute-start(bf16[256,640]{1,0:T(8,128)(2,1)S(1)} %shard_map.87.att_ref), channel_id=1, source_target_pairs={{0,1},{1,0},{2,3},{3,2},{4,5},{5,4},{6,7},{7,6},{8,9},{9,8},{10,11... | collective-permute-start | bytes 983048 | tf_op jit(solution)/shard_map/ppermute | solution.py:239
  127.1 2.9 %copy-done = bf16[640,5120]{1,0:T(8,128)(2,1)S(1)} copy-done((bf16[640,5120]{1,0:T(8,128)(2,1)S(1)}, bf16[640,5120]{1,0:T(8,128)(2,1)}, u32[]{:S(2)}) %copy-start) | copy-done | bytes 6553624
  130.0 5.7 %shard_map.92 = (bf16[256,640]{1,0:T(8,128)(2,1)S(1)}, bf16[256,640]{1,0:T(8,128)(2,1)S(1)}, bf16[256,640]{1,0:T(8,128)(2,1)S(1)}, bf16[256,640]{1,0:T(8,128)(2,1)S(1)}) custom-call(s32[3]{0:T(128)S(1)} %pad_add_fusion.where, bf16[256,640]{1,0:T(8,128)(2,1)S(1)} %shard_map.91.att_ref, bf16[256,640]{1,0:T(8,128)(2,1)} %collective-permute-done.18.other_ref, ...), custom_call_target="tpu_custom_call" | custom-call | flops 1677721600 | bytes 11796480 | tf_op jit(solution)/shard_map/pallas_call | solution.py:185
  135.7 1.4 collective-permute-start.19
  137.1 0.6 collective-permute-start.20
  137.7 1.1 collective-permute-start.21
  138.8 5.7 %shard_map.88 = (bf16[256,640]{1,0:T(8,128)(2,1)S(1)}, bf16[256,640]{1,0:T(8,128)(2,1)S(1)}, bf16[256,640]{1,0:T(8,128)(2,1)S(1)}, bf16[256,640]{1,0:T(8,128)(2,1)S(1)}) custom-call(s32[3]{0:T(128)S(1)} %pad_add_fusion.where, bf16[256,640]{1,0:T(8,128)(2,1)S(1)} %shard_map.87.att_ref, bf16[256,640]{1,0:T(8,128)(2,1)S(1)} %collective-permute-done.9.other_ref, ...), custom_call_target="tpu_custom_call" | custom-call | flops 1677721600 | bytes 11796480 | tf_op jit(solution)/shard_map/pallas_call | solution.py:185
  144.4 1.2 collective-permute-start.12
  145.6 2.7 %collective-permute-start.13 = (bf16[256,640]{1,0:T(8,128)(2,1)S(1)}, bf16[256,640]{1,0:T(8,128)(2,1)S(1)}, u32[]{:S(2)}, u32[]{:S(2)}) collective-permute-start(bf16[256,640]{1,0:T(8,128)(2,1)S(1)} %get-tuple-element.43), channel_id=1, source_target_pairs={{0,4},{2,6},{4,0},{6,2},{1,5},{3,7},{5,1},{7,3},{8,12},{10,14},{12... | collective-permute-start | bytes 983048 | tf_op jit(solution)/shard_map/ppermute | solution.py:243
  148.4 1.2 collective-permute-done.19
  149.6 0.7 collective-permute-start.14
  150.3 3.0 %collective-permute-done.20 = bf16[256,640]{1,0:T(8,128)(2,1)S(1)} collective-permute-done((bf16[256,640]{1,0:T(8,128)(2,1)S(1)}, bf16[256,640]{1,0:T(8,128)(2,1)S(1)}, u32[]{:S(2)}, u32[]{:S(2)}) %collective-permute-start.20) | collective-permute-done | bytes 327712 | tf_op jit(solution)/shard_map/ppermute | solution.py:243
  153.3 2.1 %collective-permute-done.21 = bf16[256,640]{1,0:T(8,128)(2,1)S(1)} collective-permute-done((bf16[256,640]{1,0:T(8,128)(2,1)S(1)}, bf16[256,640]{1,0:T(8,128)(2,1)S(1)}, u32[]{:S(2)}, u32[]{:S(2)}) %collective-permute-start.21) | collective-permute-done | bytes 327712 | tf_op jit(solution)/shard_map/ppermute | solution.py:243
  155.5 0.2 convert_add_fusion
  155.6 4.8 %collective-permute-done.12 = bf16[256,640]{1,0:T(8,128)(2,1)S(1)} collective-permute-done((bf16[256,640]{1,0:T(8,128)(2,1)S(1)}, bf16[256,640]{1,0:T(8,128)(2,1)S(1)}, u32[]{:S(2)}, u32[]{:S(2)}) %collective-permute-start.12) | collective-permute-done | bytes 327712 | tf_op jit(solution)/shard_map/ppermute | solution.py:243
  160.4 4.6 %collective-permute-done.13 = bf16[256,640]{1,0:T(8,128)(2,1)S(1)} collective-permute-done((bf16[256,640]{1,0:T(8,128)(2,1)S(1)}, bf16[256,640]{1,0:T(8,128)(2,1)S(1)}, u32[]{:S(2)}, u32[]{:S(2)}) %collective-permute-start.13) | collective-permute-done | bytes 327712 | tf_op jit(solution)/shard_map/ppermute | solution.py:243
  165.0 1.9 %collective-permute-done.14 = bf16[256,640]{1,0:T(8,128)(2,1)S(1)} collective-permute-done((bf16[256,640]{1,0:T(8,128)(2,1)S(1)}, bf16[256,640]{1,0:T(8,128)(2,1)S(1)}, u32[]{:S(2)}, u32[]{:S(2)}) %collective-permute-start.14) | collective-permute-done | bytes 327712 | tf_op jit(solution)/shard_map/ppermute | solution.py:243
  166.9 0.2 convert_add_fusion.1
  167.0 1.0 fusion.1
  (29 shorter events, 0.2 us)
Async XLA Ops:
  0.0 2.1 %copy-start.5 = (bf16[512,640]{1,0:T(8,128)(2,1)S(1)}, bf16[512,640]{1,0:T(8,128)(2,1)}, u32[]{:S(2)}) copy-start(bf16[512,640]{1,0:T(8,128)(2,1)} %param.12) | copy-start | bytes 1966084
  3.0 30.9 %collective-permute-start.1 = (bf16[1024,640]{1,0:T(8,128)(2,1)}, bf16[1024,640]{1,0:T(8,128)(2,1)S(1)}, u32[]{:S(2)}, u32[]{:S(2)}) collective-permute-start(bf16[1024,640]{1,0:T(8,128)(2,1)} %constant_dynamic-update-slice_fusion.refs_2_.refs_1_), channel_id=1, source_target_pairs={{0,16},{16,0},{1,17},{17,1},{2,18},{18,2},{3,19},{19,3},{4,20},{20... | collective-permute-start | bytes 3932168 | tf_op jit(solution)/shard_map/ppermute | solution.py:214
  6.4 2.8 %copy-start.1 = (bf16[512,640]{1,0:T(8,128)(2,1)S(1)}, bf16[512,640]{1,0:T(8,128)(2,1)}, u32[]{:S(2)}) copy-start(bf16[512,640]{1,0:T(8,128)(2,1)} %qb_ref.3) | copy-start | bytes 1966084
  6.6 45.9 %copy-start.2 = (bf16[512,640]{1,0:T(8,128)(2,1)S(1)}, bf16[512,640]{1,0:T(8,128)(2,1)}, u32[]{:S(2)}) copy-start(bf16[512,640]{1,0:T(8,128)(2,1)} %refs_1_.1) | copy-start | bytes 1966084
  6.6 45.9 %copy-start.3 = (bf16[512,640]{1,0:T(8,128)(2,1)S(1)}, bf16[512,640]{1,0:T(8,128)(2,1)}, u32[]{:S(2)}) copy-start(bf16[512,640]{1,0:T(8,128)(2,1)} %refs_2_.1) | copy-start | bytes 1966084
  6.6 38.5 %collective-permute-start.10 = (bf16[1280,640]{1,0:T(8,128)(2,1)S(1)}, bf16[1280,640]{1,0:T(8,128)(2,1)S(1)}, u32[]{:S(2)}, u32[]{:S(2)}) collective-permute-start(bf16[1280,640]{1,0:T(8,128)(2,1)S(1)} %pad_maximum_fusion), channel_id=1, source_target_pairs={{0,17},{17,0},{1,16},{16,1},{2,19},{19,2},{3,18},{18,3},{4,21},{21... | collective-permute-start | bytes 4915208 | tf_op jit(solution)/shard_map/ppermute | solution.py:224
  9.2 36.0 %collective-permute-start.4 = (bf16[1024,640]{1,0:T(8,128)(2,1)}, bf16[1024,640]{1,0:T(8,128)(2,1)S(1)}, u32[]{:S(2)}, u32[]{:S(2)}) collective-permute-start(bf16[1024,640]{1,0:T(8,128)(2,1)} %constant_dynamic-update-slice_fusion.refs_2_.refs_1_), channel_id=1, source_target_pairs={{0,8},{8,0},{1,9},{9,1},{2,10},{10,2},{3,11},{11,3},{4,12},{12,4},... | collective-permute-start | bytes 3932168 | tf_op jit(solution)/shard_map/ppermute | solution.py:215
  9.2 26.1 %collective-permute-start.5 = (bf16[512,640]{1,0:T(8,128)(2,1)S(1)}, bf16[512,640]{1,0:T(8,128)(2,1)S(1)}, u32[]{:S(2)}, u32[]{:S(2)}) collective-permute-start(bf16[512,640]{1,0:T(8,128)(2,1)S(1)} %copy-done.1), channel_id=1, source_target_pairs={{0,64},{32,96},{64,0},{96,32},{1,65},{33,97},{65,1},{97,33},{2,66}... | collective-permute-start | bytes 1966088 | tf_op jit(solution)/shard_map/ppermute | solution.py:218
  33.9 37.8 %collective-permute-start.2 = (bf16[1024,640]{1,0:T(8,128)(2,1)S(1)}, bf16[1024,640]{1,0:T(8,128)(2,1)S(1)}, u32[]{:S(2)}, u32[]{:S(2)}) collective-permute-start(bf16[1024,640]{1,0:T(8,128)(2,1)S(1)} %collective-permute-done.1.z_ref), channel_id=1, source_target_pairs={{0,8},{8,0},{1,9},{9,1},{2,10},{10,2},{3,11},{11,3},{4,12},{12,4},... | collective-permute-start | bytes 3932168 | tf_op jit(solution)/shard_map/ppermute | solution.py:219
  33.9 25.3 %collective-permute-start.3 = (bf16[512,640]{1,0:T(8,128)(2,1)S(1)}, bf16[512,640]{1,0:T(8,128)(2,1)S(1)}, u32[]{:S(2)}, u32[]{:S(2)}) collective-permute-start(bf16[512,640]{1,0:T(8,128)(2,1)S(1)} %copy-done.1), channel_id=1, source_target_pairs={{0,32},{32,64},{64,96},{96,0},{1,33},{33,65},{65,97},{97,1},{2,34}... | collective-permute-start | bytes 1966088 | tf_op jit(solution)/shard_map/ppermute | solution.py:216
  35.4 23.8 %collective-permute-start = (bf16[512,640]{1,0:T(8,128)(2,1)S(1)}, bf16[512,640]{1,0:T(8,128)(2,1)S(1)}, u32[]{:S(2)}, u32[]{:S(2)}) collective-permute-start(bf16[512,640]{1,0:T(8,128)(2,1)S(1)} %copy-done.1), channel_id=1, source_target_pairs={{0,96},{32,0},{64,32},{96,64},{1,97},{33,1},{65,33},{97,65},{2,98}... | collective-permute-start | bytes 1966088 | tf_op jit(solution)/shard_map/ppermute | solution.py:217
  45.2 81.9 %collective-permute-start.11 = (bf16[1280,640]{1,0:T(8,128)(2,1)S(1)}, bf16[1280,640]{1,0:T(8,128)(2,1)}, u32[]{:S(2)}, u32[]{:S(2)}) collective-permute-start(bf16[1280,640]{1,0:T(8,128)(2,1)S(1)} %collective-permute-done.10.wz_ref), channel_id=1, source_target_pairs={{0,8},{8,0},{1,9},{9,1},{2,10},{10,2},{3,11},{11,3},{4,12},{12,4},... | collective-permute-start | bytes 4915208 | tf_op jit(solution)/shard_map/ppermute | solution.py:225
  78.5 27.2 %collective-permute-start.17 = (bf16[656,256]{1,0:T(8,128)(2,1)S(1)}, bf16[656,256]{1,0:T(8,128)(2,1)S(1)}, u32[]{:S(2)}, u32[]{:S(2)}) collective-permute-start(bf16[656,256]{1,0:T(8,128)(2,1)S(1)} %get-tuple-element.48), channel_id=1, source_target_pairs={{0,32},{32,64},{64,96},{96,0},{1,33},{33,65},{65,97},{97,1},{2,34}... | collective-permute-start | bytes 1007624 | tf_op jit(solution)/shard_map/ppermute | solution.py:236
  86.9 19.9 %collective-permute-start.15 = (bf16[656,256]{1,0:T(8,128)(2,1)S(1)}, bf16[656,256]{1,0:T(8,128)(2,1)S(1)}, u32[]{:S(2)}, u32[]{:S(2)}) collective-permute-start(bf16[656,256]{1,0:T(8,128)(2,1)S(1)} %get-tuple-element.46), channel_id=1, source_target_pairs={{0,96},{32,0},{64,32},{96,64},{1,97},{33,1},{65,33},{97,65},{2,98}... | collective-permute-start | bytes 1007624 | tf_op jit(solution)/shard_map/ppermute | solution.py:236
  87.5 20.8 %collective-permute-start.16 = (bf16[656,256]{1,0:T(8,128)(2,1)S(1)}, bf16[656,256]{1,0:T(8,128)(2,1)S(1)}, u32[]{:S(2)}, u32[]{:S(2)}) collective-permute-start(bf16[656,256]{1,0:T(8,128)(2,1)S(1)} %get-tuple-element.47), channel_id=1, source_target_pairs={{0,64},{32,96},{64,0},{96,32},{1,65},{33,97},{65,1},{97,33},{2,66}... | collective-permute-start | bytes 1007624 | tf_op jit(solution)/shard_map/ppermute | solution.py:236
  97.1 14.0 %collective-permute-start.8 = (bf16[656,256]{1,0:T(8,128)(2,1)}, bf16[656,256]{1,0:T(8,128)(2,1)}, u32[]{:S(2)}, u32[]{:S(2)}) collective-permute-start(bf16[656,256]{1,0:T(8,128)(2,1)} %get-tuple-element.40), channel_id=1, source_target_pairs={{0,32},{32,64},{64,96},{96,0},{1,33},{33,65},{65,97},{97,1},{2,34}... | collective-permute-start | bytes 1007624 | tf_op jit(solution)/shard_map/ppermute | solution.py:236
  105.7 10.0 %collective-permute-start.6 = (bf16[656,256]{1,0:T(8,128)(2,1)}, bf16[656,256]{1,0:T(8,128)(2,1)S(1)}, u32[]{:S(2)}, u32[]{:S(2)}) collective-permute-start(bf16[656,256]{1,0:T(8,128)(2,1)} %get-tuple-element.38), channel_id=1, source_target_pairs={{0,96},{32,0},{64,32},{96,64},{1,97},{33,1},{65,33},{97,65},{2,98}... | collective-permute-start | bytes 1007624 | tf_op jit(solution)/shard_map/ppermute | solution.py:236
  106.7 16.4 %collective-permute-start.7 = (bf16[656,256]{1,0:T(8,128)(2,1)}, bf16[656,256]{1,0:T(8,128)(2,1)}, u32[]{:S(2)}, u32[]{:S(2)}) collective-permute-start(bf16[656,256]{1,0:T(8,128)(2,1)} %get-tuple-element.39), channel_id=1, source_target_pairs={{0,64},{32,96},{64,0},{96,32},{1,65},{33,97},{65,1},{97,33},{2,66}... | collective-permute-start | bytes 1007624 | tf_op jit(solution)/shard_map/ppermute | solution.py:236
  108.6 18.5 %collective-permute-start.18 = (bf16[256,640]{1,0:T(8,128)(2,1)S(1)}, bf16[256,640]{1,0:T(8,128)(2,1)}, u32[]{:S(2)}, u32[]{:S(2)}) collective-permute-start(bf16[256,640]{1,0:T(8,128)(2,1)S(1)} %shard_map.91.att_ref), channel_id=1, source_target_pairs={{0,1},{1,0},{2,3},{3,2},{4,5},{5,4},{6,7},{7,6},{8,9},{9,8},{10,11... | collective-permute-start | bytes 983048 | tf_op jit(solution)/shard_map/ppermute | solution.py:239
  124.6 14.2 %collective-permute-start.9 = (bf16[256,640]{1,0:T(8,128)(2,1)S(1)}, bf16[256,640]{1,0:T(8,128)(2,1)S(1)}, u32[]{:S(2)}, u32[]{:S(2)}) collective-permute-start(bf16[256,640]{1,0:T(8,128)(2,1)S(1)} %shard_map.87.att_ref), channel_id=1, source_target_pairs={{0,1},{1,0},{2,3},{3,2},{4,5},{5,4},{6,7},{7,6},{8,9},{9,8},{10,11... | collective-permute-start | bytes 983048 | tf_op jit(solution)/shard_map/ppermute | solution.py:239
  127.1 2.9 %copy-start = (bf16[640,5120]{1,0:T(8,128)(2,1)S(1)}, bf16[640,5120]{1,0:T(8,128)(2,1)}, u32[]{:S(2)}) copy-start(bf16[640,5120]{1,0:T(8,128)(2,1)} %w_ref.3) | copy-start | bytes 19660804
  135.7 13.9 %collective-permute-start.19 = (bf16[256,640]{1,0:T(8,128)(2,1)S(1)}, bf16[256,640]{1,0:T(8,128)(2,1)S(1)}, u32[]{:S(2)}, u32[]{:S(2)}) collective-permute-start(bf16[256,640]{1,0:T(8,128)(2,1)S(1)} %get-tuple-element.50), channel_id=1, source_target_pairs={{0,2},{2,4},{4,6},{6,0},{1,3},{3,5},{5,7},{7,1},{8,10},{10,12},{12... | collective-permute-start | bytes 983048 | tf_op jit(solution)/shard_map/ppermute | solution.py:243
  137.1 16.3 %collective-permute-start.20 = (bf16[256,640]{1,0:T(8,128)(2,1)S(1)}, bf16[256,640]{1,0:T(8,128)(2,1)S(1)}, u32[]{:S(2)}, u32[]{:S(2)}) collective-permute-start(bf16[256,640]{1,0:T(8,128)(2,1)S(1)} %get-tuple-element.51), channel_id=1, source_target_pairs={{0,4},{2,6},{4,0},{6,2},{1,5},{3,7},{5,1},{7,3},{8,12},{10,14},{12... | collective-permute-start | bytes 983048 | tf_op jit(solution)/shard_map/ppermute | solution.py:243
  137.7 17.8 %collective-permute-start.21 = (bf16[256,640]{1,0:T(8,128)(2,1)S(1)}, bf16[256,640]{1,0:T(8,128)(2,1)S(1)}, u32[]{:S(2)}, u32[]{:S(2)}) collective-permute-start(bf16[256,640]{1,0:T(8,128)(2,1)S(1)} %get-tuple-element.52), channel_id=1, source_target_pairs={{0,6},{2,0},{4,2},{6,4},{1,7},{3,1},{5,3},{7,5},{8,14},{10,8},{12,... | collective-permute-start | bytes 983048 | tf_op jit(solution)/shard_map/ppermute | solution.py:243
  144.4 16.0 %collective-permute-start.12 = (bf16[256,640]{1,0:T(8,128)(2,1)S(1)}, bf16[256,640]{1,0:T(8,128)(2,1)S(1)}, u32[]{:S(2)}, u32[]{:S(2)}) collective-permute-start(bf16[256,640]{1,0:T(8,128)(2,1)S(1)} %get-tuple-element.42), channel_id=1, source_target_pairs={{0,2},{2,4},{4,6},{6,0},{1,3},{3,5},{5,7},{7,1},{8,10},{10,12},{12... | collective-permute-start | bytes 983048 | tf_op jit(solution)/shard_map/ppermute | solution.py:243
  145.6 19.4 %collective-permute-start.13 = (bf16[256,640]{1,0:T(8,128)(2,1)S(1)}, bf16[256,640]{1,0:T(8,128)(2,1)S(1)}, u32[]{:S(2)}, u32[]{:S(2)}) collective-permute-start(bf16[256,640]{1,0:T(8,128)(2,1)S(1)} %get-tuple-element.43), channel_id=1, source_target_pairs={{0,4},{2,6},{4,0},{6,2},{1,5},{3,7},{5,1},{7,3},{8,12},{10,14},{12... | collective-permute-start | bytes 983048 | tf_op jit(solution)/shard_map/ppermute | solution.py:243
  149.6 17.3 %collective-permute-start.14 = (bf16[256,640]{1,0:T(8,128)(2,1)S(1)}, bf16[256,640]{1,0:T(8,128)(2,1)S(1)}, u32[]{:S(2)}, u32[]{:S(2)}) collective-permute-start(bf16[256,640]{1,0:T(8,128)(2,1)S(1)} %get-tuple-element.44), channel_id=1, source_target_pairs={{0,6},{2,0},{4,2},{6,4},{1,7},{3,1},{5,3},{7,5},{8,14},{10,8},{12,... | collective-permute-start | bytes 983048 | tf_op jit(solution)/shard_map/ppermute | solution.py:243
  155.6 11.4 %copy-start.4 = (bf16[512,640]{1,0:T(8,128)(2,1)S(1)}, bf16[512,640]{1,0:T(8,128)(2,1)}, u32[]{:S(2)}) copy-start(bf16[512,640]{1,0:T(8,128)(2,1)} %param.14) | copy-start | bytes 1966084
  155.6 11.4 %copy-start.6 = (f32[640]{0:T(1024)S(1)}, f32[640]{0:T(1024)}, u32[]{:S(2)}) copy-start(f32[640]{0:T(1024)} %param.15) | copy-start | bytes 7684

commit v3 on v0

v3 whole, which is shorter than its diff:
```python
import functools
import math

import jax
import jax.numpy as jnp
from jax import lax
from jax.experimental import pallas as pl
from jax.experimental.pallas import tpu as pltpu
from jax.sharding import PartitionSpec as P


HD = 128
STAT = 16
CHUNKS = 2
TO_LOG2 = math.log2(math.e) / math.sqrt(HD)
AXES = ("x", "zl", "c", "y", "zh")
NT = (((1,), (1,)), ((), ()))
TN = (((0,), (0,)), ((), ()))


VMEM = pl.BlockSpec(memory_space=pltpu.VMEM)


def ring(n, k):
    return [(i, (i + k) % n) for i in range(n)]


def dot(a, b, dims):
    return lax.dot_general(a, b, dims, preferred_element_type=jnp.float32)


def call(kernel, out_shape, *args, limit, scratch=(), specs=None, flops=0):
    size = sum(x.size * x.dtype.itemsize for x in args)
    return pl.pallas_call(
        kernel,
        out_shape=out_shape,
        in_specs=specs or [VMEM] * len(args),
        out_specs=jax.tree.map(lambda _: VMEM, out_shape),
        scratch_shapes=scratch,
        compiler_params=pltpu.CompilerParams(vmem_limit_bytes=limit << 20),
        cost_estimate=pl.CostEstimate(flops=flops, bytes_accessed=size, transcendentals=0),
    )(*args)


def attend(q, pieces, extra=None):
    scores = [dot(k, q, NT) for k, _ in pieces]
    top = functools.reduce(jnp.maximum, [jnp.max(s, axis=0, keepdims=True) for s in scores])
    expo = [jnp.exp2((s - top) * TO_LOG2) for s in scores]
    total = functools.reduce(jnp.add, [jnp.sum(e, axis=0, keepdims=True) for e in expo])
    out = functools.reduce(
        jnp.add, [dot(v, e.astype(jnp.bfloat16), TN) for e, (_, v) in zip(expo, pieces, strict=True)]
    )
    top = top * TO_LOG2
    if extra is None:
        return out * (1.0 / total), top + jnp.log2(total)
    before, before_lse = extra
    best = jnp.maximum(top, before_lse)
    now, then = jnp.exp2(top - best), jnp.exp2(before_lse - best)
    whole = total * now + then
    inverse = 1.0 / whole
    return out * (now * inverse) + before * (then * inverse), best + jnp.log2(whole)


def head_loop(heads, step):
    def run(h, carry):
        step(h, pl.ds(pl.multiple_of(h * HD, HD), HD))
        return carry

    lax.fori_loop(0, heads, run, 0)


def early_kernel(count, *refs):
    queries, (ka, va, kb, vb), outs = refs[:count], refs[count : count + 4], refs[count + 4 :]
    n = queries[0].shape[0]

    def step(h, at):
        q = jnp.concatenate([r[:, at] for r in queries], axis=0)
        out, lse = attend(q, [(ka[:, at], va[:, at]), (kb[:, at], vb[:, at])])
        for i in range(count):
            outs[2 * i][at, :] = out[:, i * n : (i + 1) * n]
            outs[2 * i + 1][pl.ds(h, 1), :] = lse[:, i * n : (i + 1) * n]

    head_loop(queries[0].shape[1] // HD, step)


def early(queries, *kv):
    n, width = queries[0].shape
    count = len(queries)
    shapes = (jax.ShapeDtypeStruct((width, n), jnp.float32), jax.ShapeDtypeStruct((8, n), jnp.float32)) * count
    return call(
        functools.partial(early_kernel, count), shapes, *queries, *kv, limit=26, flops=count * 8 * n * n * width
    )


def late_kernel(segments, *refs):
    count = len(segments)
    queries, refs = refs[:count], refs[count:]
    before, refs = refs[: 2 * count], refs[2 * count :]
    ka, va, kb, vb = refs[:4]
    outs, stat = refs[4:-1], refs[-1]
    rows = [slice(first, first + n) for first, n in segments]
    width = queries[0].shape[1]

    def spans():
        start = 0
        for (_, n), out_ref in zip(segments, outs, strict=True):
            yield out_ref, slice(start, start + n)
            start += n

    def step(h, at):
        q = jnp.concatenate([r[s, at] for r, s in zip(queries, rows, strict=True)], axis=0)
        old = jnp.concatenate([r[at, s] for r, s in zip(before[::2], rows, strict=True)], axis=1)
        old_lse = jnp.concatenate([r[pl.ds(h, 1), s] for r, s in zip(before[1::2], rows, strict=True)], axis=1)
        out, lse = attend(q, [(ka[:, at], va[:, at]), (kb[:, at], vb[:, at])], (old, old_lse))
        for out_ref, span in spans():
            out_ref[at, :] = out[:, span].astype(jnp.bfloat16)
        stat[pl.ds(h, 1), :] = lse

    head_loop(width // HD, step)
    high = stat[...].astype(jnp.bfloat16)
    low = (stat[...] - high.astype(jnp.float32)).astype(jnp.bfloat16)
    both = jnp.concatenate([high, low], axis=0)
    for out_ref, span in spans():
        out_ref[width : width + STAT, :] = both[:, span]


def late(segments, *kv):
    whole, width = segments[0][0].shape
    spans = tuple((first, n) for _, _, first, n in segments)
    return call(
        functools.partial(late_kernel, spans),
        tuple(jax.ShapeDtypeStruct((width + STAT, n), jnp.bfloat16) for _, n in spans),
        *(q for q, _, _, _ in segments),
        *(part for _, e, _, _ in segments for part in e),
        *kv,
        limit=26,
        scratch=[pltpu.VMEM((8, sum(n for _, n in spans)), jnp.float32)],
        flops=sum(n for _, n in spans) * 8 * whole * width,
    )


def merge_kernel(first, *refs):
    *parts, out_ref = refs
    n, width = out_ref.shape
    own = slice(first, first + n)
    spans = [own] + [slice(0, n)] * (len(parts) - 1)
    stats = []
    for ref, span in zip(parts, spans, strict=True):
        both = ref[width : width + STAT, span].astype(jnp.float32)
        stats.append(both[0:8] + both[8:16])
    top = functools.reduce(jnp.maximum, stats)
    weights = [jnp.exp2(s - top) for s in stats]
    total = functools.reduce(jnp.add, weights)
    weights = [w * (1.0 / total) for w in weights]
    for h in range(width // HD):
        mixed = None
        for ref, span, w in zip(parts, spans, weights, strict=True):
            term = ref[h * HD : (h + 1) * HD, span].astype(jnp.float32) * w[h : h + 1, :]
            mixed = term if mixed is None else mixed + term
        out_ref[:, h * HD : (h + 1) * HD] = mixed.T.astype(jnp.bfloat16)


def merge(first, n, parts):
    shape = jax.ShapeDtypeStruct((n, parts[0].shape[0] - STAT), jnp.bfloat16)
    return call(functools.partial(merge_kernel, first), shape, *parts, limit=8)


def weight_columns(owner_y, owner_zh, width):
    return pl.ds(pl.multiple_of((owner_y * 2 + owner_zh) * width, HD), width)


def parcel_kernel(w_ref, out_ref, sems):
    width = w_ref.shape[0]
    zh, c = lax.axis_index("zh"), lax.axis_index("c")
    for act in ("start", "wait"):
        for i in range(2):
            at = weight_columns(2 * c + i, 1 - zh, width)
            copy = pltpu.make_async_copy(w_ref.at[:, at], out_ref.at[i * width : (i + 1) * width, :], sems.at[i])
            getattr(copy, act)()


def weight_kernel(w_ref, wz_ref, ws_ref, out_ref, sems):
    width = w_ref.shape[0]
    y, zh, c = lax.axis_index("y"), lax.axis_index("zh"), lax.axis_index("c")

    def other_rows(j, ref):
        at = pl.ds(pl.multiple_of(lax.rem(y + j, 2) * width, width), width)
        return pltpu.make_async_copy(ref.at[at, :], out_ref.at[j, width : 2 * width, :], sems.at[4 + j])

    for act in ("start", "wait"):
        for j in range(4):
            owner = lax.rem(y + j, 4)
            at = weight_columns(owner, zh, width)
            copy = pltpu.make_async_copy(w_ref.at[:, at], out_ref.at[j, 0:width, :], sems.at[j])
            getattr(copy, act)()
            mine = lax.div(owner, 2) == c

            @pl.when(mine)
            def _():
                getattr(other_rows(j, wz_ref), act)()

            @pl.when(jnp.logical_not(mine))
            def _():
                getattr(other_rows(j, ws_ref), act)()


def project_kernel(att_ref, other_ref, w_ref, *outs):
    act = jnp.concatenate([att_ref[...], other_ref[...]], axis=1)
    for j, out_ref in enumerate(outs):
        out_ref[...] = jnp.dot(act, w_ref[j], preferred_element_type=jnp.float32).astype(jnp.bfloat16)


def final_kernel(residual_ref, gate_ref, *refs):
    *pieces, out_ref = refs
    n = out_ref.shape[0] // CHUNKS
    for i in range(CHUNKS):
        rows = slice(i * n, (i + 1) * n)
        mine = [r[...].astype(jnp.float32) for r in pieces[i * 4 : (i + 1) * 4]]
        whole = functools.reduce(jnp.add, mine)
        out_ref[rows, :] = (residual_ref[rows, :].astype(jnp.float32) + gate_ref[...] * whole).astype(jnp.bfloat16)


def block(query, key_fresh, value_fresh, key_stale, value_stale, out_weight, residual, gate):
    rows, width = query.shape
    n = rows // CHUNKS
    swap = ring(2, 1)
    hbm = pl.BlockSpec(memory_space=pl.ANY)

    k_z = lax.ppermute(key_stale, "zl", swap)
    v_z = lax.ppermute(value_stale, "zl", swap)
    q1 = lax.ppermute(query, "x", ring(4, 1))
    q3 = lax.ppermute(query, "x", ring(4, 3))
    k_s = lax.ppermute(key_stale, "c", swap)
    v_s = lax.ppermute(value_stale, "c", swap)
    q2 = lax.ppermute(query, "x", ring(4, 2))
    k_zs = lax.ppermute(k_z, "c", swap)
    v_zs = lax.ppermute(v_z, "c", swap)

    parcel = call(
        parcel_kernel,
        jax.ShapeDtypeStruct((2 * width, width), jnp.bfloat16),
        out_weight,
        limit=4,
        specs=[hbm],
        scratch=[pltpu.SemaphoreType.DMA((2,))],
    )
    w_z = lax.ppermute(parcel, ("zl", "zh"), [(0, 3), (3, 0), (1, 2), (2, 1)])
    w_s = lax.ppermute(w_z, "c", swap)

    e0 = early((query,), key_fresh, value_fresh, k_s, v_s)
    e13 = early((q1, q3), key_stale, value_stale, k_s, v_s)
    e2 = early((q2,), key_stale, value_stale, k_s, v_s)
    far = (k_z, v_z, k_zs, v_zs)
    firsts = [i * n for i in range(CHUNKS)]
    pairs = [late([(q1, e13[:2], first, n), (q3, e13[2:], first, n)], *far) for first in firsts]
    middle = late([(q2, e2, first, n) for first in firsts], *far)
    (o0,) = late([(query, e0, 0, rows)], *far)
    weights = call(
        weight_kernel,
        jax.ShapeDtypeStruct((4, 2 * width, width), jnp.bfloat16),
        out_weight,
        w_z,
        w_s,
        limit=10,
        specs=[hbm] * 3,
        scratch=[pltpu.SemaphoreType.DMA((8,))],
    )

    landed = []
    for i in range(CHUNKS):
        o1, o3 = pairs[i]
        parts = (
            o0,
            lax.ppermute(o1, "x", ring(4, 3)),
            lax.ppermute(middle[i], "x", ring(4, 2)),
            lax.ppermute(o3, "x", ring(4, 1)),
        )
        attended = merge(i * n, n, parts)
        other = lax.ppermute(attended, "zh", swap)
        pieces = call(
            project_kernel,
            (jax.ShapeDtypeStruct((n, width), jnp.bfloat16),) * 4,
            attended,
            other,
            weights,
            limit=16,
            flops=16 * n * width * width,
        )
        landed += [pieces[0], *(lax.ppermute(pieces[j], "y", ring(4, j)) for j in range(1, 4))]
    shape = jax.ShapeDtypeStruct((rows, width), jnp.bfloat16)
    return call(final_kernel, shape, residual, gate, *landed, limit=8)


def solution(mesh):
    fine = jax.sharding.Mesh(mesh.devices.reshape(4, 2, 2, 4, 2), AXES)
    rows, cols = ("x", "zl", "c"), ("y", "zh")
    spec = P(rows, cols)
    in_specs = (spec, spec, spec, spec, spec, P(cols, None), spec, P(cols))
    return jax.shard_map(block, mesh=fine, in_specs=in_specs, out_specs=spec, check_vma=False)
```

time: 580 us -> 144 us (0.25)
  waiting for transfers between devices: 357 us -> 60.2 us
  local copies, waits for them, and re-layouts: 116 us -> 2.89 us
  other arithmetic: 52.1 us -> 0.01 us
  Pallas kernels: 0 us -> 50.2 us
  matrix products: 39.8 us -> 0 us
  starting transfers between devices: 0.08 us -> 29.3 us
  between operations: 13.2 us -> 0.19 us
    psum x1 -> x0, waiting for transfers between devices: 227 us -> none  [body(): lax.psum(jnp.dot(attended, out_weight, preferred_element_type=jnp.float32...]
    all_gather x2 -> x0, waiting for transfers between devices: 129 us -> none  [the longest x1 64.5 us: body(): lax.all_gather(value_stale, 'patch', axis=0, tiled=True)]
    gather x16 -> x0, local copies, waits for them, and re-layouts: 73.6 us -> none  [the longest x8 41.4 us: inner(): value_rows = jnp.where(inside[:, None], fresh_pair[1][within], value_rows)]
    ppermute x0 -> x25, waiting for transfers between devices: none -> 60.2 us  [the longest x6 16.4 us: block(): lax.ppermute(pieces[j], 'y', ring(4, j))]
    pallas_call x0 -> x14, Pallas kernels: none -> 50.2 us  [call(): pl.pallas_call(kernel, out_shape=out_shape, in_specs=specs or [VMEM] * le...]
    dot_general x17 -> x0, matrix products: 39.8 us -> none  [the longest x8 18.2 us: softmax_step(): jnp.einsum('qhk,khd->qhd', expo.astype(jnp.bfloat16), values3, preferred_...]
    select_n x16 -> x0, other arithmetic: 34.5 us -> none  [the longest x8 34.4 us: inner(): value_rows = jnp.where(inside[:, None], fresh_pair[1][within], value_rows)]
    select_n x16 -> x0, local copies, waits for them, and re-layouts: 32.8 us -> none  [the longest x8 20 us: inner(): value_rows = jnp.where(inside[:, None], fresh_pair[1][within], value_rows)]
  transfers between devices with their start and end apart: 3 -> 25, of which waited for: 3 -> 12; matrix products, arithmetic and copies ran while one was open for 0% -> 0% of each run, Pallas kernels for 0% -> 34%
where the time goes in v3:
time: 144 us; the launch traced here: 143 us
  waiting for transfers between devices  60.2 us (42%)
  Pallas kernels  50.2 us (35%)
  starting transfers between devices  29.3 us (20%)
  local copies, waits for them, and re-layouts  2.89 us (2%)
    pallas_call x14, Pallas kernels, call(): pl.pallas_call(kernel, out_shape=out_shape, in_specs=specs or [VMEM] * le...  50.2 us
    ppermute x6, waiting for transfers between devices, block(): lax.ppermute(pieces[j], 'y', ring(4, j))  16.4 us
    ppermute x1, waiting for transfers between devices, block(): k_z = lax.ppermute(key_stale, 'zl', swap)  15.3 us
    ppermute x1, waiting for transfers between devices, block(): v_z = lax.ppermute(value_stale, 'zl', swap)  10.5 us
    ppermute x6, starting transfers between devices, block(): lax.ppermute(pieces[j], 'y', ring(4, j))  7.49 us
    ppermute x2, waiting for transfers between devices, block(): other = lax.ppermute(attended, 'zh', swap)  7.09 us
    ppermute x1, waiting for transfers between devices, block(): q1 = lax.ppermute(query, 'x', ring(4, 1))  5.9 us
    ppermute x2, starting transfers between devices, block(): lax.ppermute(middle[i], 'x', ring(4, 2))  4.9 us
  transfers between devices with their start and end apart: 25, of which 12 were waited for; matrix products, arithmetic and copies ran while one was open for 0% of the time, Pallas kernels for 34%

profile of v3, /device:TPU:18, one launch (start us, length us, event | category | flops | bytes accessed | tf_op | source)
XLA Modules:
  0.0 142.8 jit_solution(9404497086616218668)
XLA Ops:
  0.0 2.9 %copy-done = bf16[640,5120]{1,0:T(8,128)(2,1)S(1)} copy-done((bf16[640,5120]{1,0:T(8,128)(2,1)S(1)}, bf16[640,5120]{1,0:T(8,128)(2,1)}, u32[]{:S(2)}) %copy-start) | copy-done | bytes 6553624
  2.9 0.2 shard_map.89
  3.1 4.1 %collective-permute-start.13 = (bf16[1280,640]{1,0:T(8,128)(2,1)S(1)}, bf16[1280,640]{1,0:T(8,128)(2,1)S(1)}, u32[]{:S(2)}, u32[]{:S(2)}) collective-permute-start(bf16[1280,640]{1,0:T(8,128)(2,1)S(1)} %shard_map.89), channel_id=1, source_target_pairs={{0,17},{17,0},{1,16},{16,1},{2,19},{19,2},{3,18},{18,3},{4,21},{21... | collective-permute-start | bytes 4915208 | tf_op jit(solution)/shard_map/ppermute | solution.py:247
  7.2 2.0 %collective-permute-start.3 = (bf16[512,640]{1,0:T(8,128)(2,1)S(1)}, bf16[512,640]{1,0:T(8,128)(2,1)S(1)}, u32[]{:S(2)}, u32[]{:S(2)}) collective-permute-start(bf16[512,640]{1,0:T(8,128)(2,1)S(1)} %copy-done.5), channel_id=1, source_target_pairs={{0,16},{16,0},{1,17},{17,1},{2,18},{18,2},{3,19},{19,3},{4,20},{20... | collective-permute-start | bytes 1966088 | tf_op jit(solution)/shard_map/ppermute | solution.py:230
  9.3 0.2 collective-permute-start.1
  9.5 15.3 %collective-permute-done.2.refs_3_.refs_6_ = bf16[512,640]{1,0:T(8,128)(2,1)S(1)} collective-permute-done((bf16[512,640]{1,0:T(8,128)(2,1)S(1)}, bf16[512,640]{1,0:T(8,128)(2,1)S(1)}, u32[]{:S(2)}, u32[]{:S(2)}) %collective-permute-start.2) | collective-permute-done | bytes 655392 | tf_op jit(solution)/shard_map/ppermute | solution.py:229
  24.8 2.1 %collective-permute-start.9 = (bf16[512,640]{1,0:T(8,128)(2,1)S(1)}, bf16[512,640]{1,0:T(8,128)(2,1)S(1)}, u32[]{:S(2)}, u32[]{:S(2)}) collective-permute-start(bf16[512,640]{1,0:T(8,128)(2,1)S(1)} %copy-done.1), channel_id=1, source_target_pairs={{0,64},{32,96},{64,0},{96,32},{1,65},{33,97},{65,1},{97,33},{2,66}... | collective-permute-start | bytes 1966088 | tf_op jit(solution)/shard_map/ppermute | solution.py:235
  27.0 0.0 collective-permute-start.6
  27.0 10.5 %collective-permute-done.3.refs_4_.refs_7_ = bf16[512,640]{1,0:T(8,128)(2,1)S(1)} collective-permute-done((bf16[512,640]{1,0:T(8,128)(2,1)S(1)}, bf16[512,640]{1,0:T(8,128)(2,1)S(1)}, u32[]{:S(2)}, u32[]{:S(2)}) %collective-permute-start.3) | collective-permute-done | bytes 655392 | tf_op jit(solution)/shard_map/ppermute | solution.py:230
  37.5 0.5 collective-permute-start.7
  38.0 0.0 collective-permute-done.1.refs_4_.refs_5_
  38.0 2.8 %collective-permute-done.9.refs_0_.refs_1_ = bf16[512,640]{1,0:T(8,128)(2,1)S(1)} collective-permute-done((bf16[512,640]{1,0:T(8,128)(2,1)S(1)}, bf16[512,640]{1,0:T(8,128)(2,1)S(1)}, u32[]{:S(2)}, u32[]{:S(2)}) %collective-permute-start.9) | collective-permute-done | bytes 655392 | tf_op jit(solution)/shard_map/ppermute | solution.py:235
  40.8 2.2 %collective-permute-done.13.wz_ref = bf16[1280,640]{1,0:T(8,128)(2,1)S(1)} collective-permute-done((bf16[1280,640]{1,0:T(8,128)(2,1)S(1)}, bf16[1280,640]{1,0:T(8,128)(2,1)S(1)}, u32[]{:S(2)}, u32[]{:S(2)}) %collective-permute-start.13) | collective-permute-done | bytes 1638432 | tf_op jit(solution)/shard_map/ppermute | solution.py:247
  43.0 5.4 %shard_map.86 = (f32[640,512]{1,0:T(8,128)S(1)}, f32[8,512]{1,0:T(8,128)S(1)}) custom-call(bf16[512,640]{1,0:T(8,128)(2,1)S(1)} %collective-permute-done.9.refs_0_.refs_1_, bf16[512,640]{1,0:T(8,128)(2,1)S(1)} %copy-done.4, bf16[512,640]{1,0:T(8,128)(2,1)S(1)} %copy-done.5, bf16[512,640]{1,0:T(8,128)(2,1)S(1)} %collective-permute-done.refs_3_.refs_4_, ...), custom_call_target="tpu_custom_call" | custom-call | flops 1342177280 | bytes 3276800 | tf_op jit(solution)/shard_map/pallas_call | solution.py:34
  48.5 5.9 %collective-permute-done.6.refs_0_ = bf16[512,640]{1,0:T(8,128)(2,1)S(1)} collective-permute-done((bf16[512,640]{1,0:T(8,128)(2,1)S(1)}, bf16[512,640]{1,0:T(8,128)(2,1)S(1)}, u32[]{:S(2)}, u32[]{:S(2)}) %collective-permute-start.6) | collective-permute-done | bytes 655392 | tf_op jit(solution)/shard_map/ppermute | solution.py:231
  54.4 9.3 %shard_map.84 = (f32[640,512]{1,0:T(8,128)S(1)}, f32[8,512]{1,0:T(8,128)S(1)}, f32[640,512]{1,0:T(8,128)S(1)}, f32[8,512]{1,0:T(8,128)S(1)}) custom-call(bf16[512,640]{1,0:T(8,128)(2,1)S(1)} %collective-permute-done.6.refs_0_, bf16[512,640]{1,0:T(8,128)(2,1)S(1)} %collective-permute-done.7.refs_1_, bf16[512,640]{1,0:T(8,128)(2,1)S(1)} %copy-done.4, ...), custom_call_target="tpu_custom_call" | custom-call | flops 2684354560 | bytes 3932160 | tf_op jit(solution)/shard_map/pallas_call | solution.py:34
  63.7 5.6 %shard_map.87 = (bf16[656,256]{1,0:T(8,128)(2,1)S(1)}, bf16[656,256]{1,0:T(8,128)(2,1)S(1)}) custom-call(bf16[512,640]{1,0:T(8,128)(2,1)S(1)} %collective-permute-done.9.refs_0_.refs_1_, bf16[512,640]{1,0:T(8,128)(2,1)S(1)} %collective-permute-done.9.refs_0_.refs_1_, f32[640,512]{1,0:T(8,128)S(1)} %get-tuple-element.34.refs_2_.refs_4_, ...), custom_call_target="tpu_custom_call" | custom-call | flops 1342177280 | bytes 6586368 | tf_op jit(solution)/shard_map/pallas_call | solution.py:34
  69.3 2.8 %collective-permute-start.19 = (bf16[656,256]{1,0:T(8,128)(2,1)S(1)}, bf16[656,256]{1,0:T(8,128)(2,1)S(1)}, u32[]{:S(2)}, u32[]{:S(2)}) collective-permute-start(bf16[656,256]{1,0:T(8,128)(2,1)S(1)} %get-tuple-element.43), channel_id=1, source_target_pairs={{0,64},{32,96},{64,0},{96,32},{1,65},{33,97},{65,1},{97,33},{2,66}... | collective-permute-start | bytes 1007624 | tf_op jit(solution)/shard_map/ppermute | solution.py:275
  72.0 5.6 %shard_map.92 = (bf16[656,256]{1,0:T(8,128)(2,1)S(1)}, bf16[656,256]{1,0:T(8,128)(2,1)S(1)}) custom-call(bf16[512,640]{1,0:T(8,128)(2,1)S(1)} %collective-permute-done.6.refs_0_, bf16[512,640]{1,0:T(8,128)(2,1)S(1)} %collective-permute-done.7.refs_1_, f32[640,512]{1,0:T(8,128)S(1)} %get-tuple-element.29.refs_2_, f32[8,512]{1,0:T(8,128)S(1)} %get-tuple-element.30.refs_3_, ...), custom_call_target="tpu_custom_call" | custom-call | flops 1342177280 | bytes 6586368 | tf_op jit(solution)/shard_map/pallas_call | solution.py:34
  77.6 0.1 collective-permute-start.18
  77.7 2.0 %collective-permute-start.20 = (bf16[656,256]{1,0:T(8,128)(2,1)S(1)}, bf16[656,256]{1,0:T(8,128)(2,1)S(1)}, u32[]{:S(2)}, u32[]{:S(2)}) collective-permute-start(bf16[656,256]{1,0:T(8,128)(2,1)S(1)} %get-tuple-element.44), channel_id=1, source_target_pairs={{0,32},{32,64},{64,96},{96,0},{1,33},{33,65},{65,97},{97,1},{2,34}... | collective-permute-start | bytes 1007624 | tf_op jit(solution)/shard_map/ppermute | solution.py:276
  79.7 5.4 %shard_map.82 = (f32[640,512]{1,0:T(8,128)S(1)}, f32[8,512]{1,0:T(8,128)S(1)}) custom-call(bf16[512,640]{1,0:T(8,128)(2,1)S(1)} %copy-done.1, bf16[512,640]{1,0:T(8,128)(2,1)S(1)} %copy-done.6, bf16[512,640]{1,0:T(8,128)(2,1)S(1)} %copy-done.7, bf16[512,640]{1,0:T(8,128)(2,1)S(1)} %collective-permute-done.refs_3_.refs_4_, ...), custom_call_target="tpu_custom_call" | custom-call | flops 1342177280 | bytes 3276800 | tf_op jit(solution)/shard_map/pallas_call | solution.py:34
  85.2 2.1 %collective-permute-start.10 = (bf16[656,256]{1,0:T(8,128)(2,1)S(1)}, bf16[656,256]{1,0:T(8,128)(2,1)S(1)}, u32[]{:S(2)}, u32[]{:S(2)}) collective-permute-start(bf16[656,256]{1,0:T(8,128)(2,1)S(1)} %get-tuple-element.36), channel_id=1, source_target_pairs={{0,64},{32,96},{64,0},{96,32},{1,65},{33,97},{65,1},{97,33},{2,66}... | collective-permute-start | bytes 1007624 | tf_op jit(solution)/shard_map/ppermute | solution.py:275
  87.3 5.6 %shard_map.85 = (bf16[656,256]{1,0:T(8,128)(2,1)S(1)}, bf16[656,256]{1,0:T(8,128)(2,1)S(1)}) custom-call(bf16[512,640]{1,0:T(8,128)(2,1)S(1)} %collective-permute-done.6.refs_0_, bf16[512,640]{1,0:T(8,128)(2,1)S(1)} %collective-permute-done.7.refs_1_, f32[640,512]{1,0:T(8,128)S(1)} %get-tuple-element.29.refs_2_, f32[8,512]{1,0:T(8,128)S(1)} %get-tuple-element.30.refs_3_, ...), custom_call_target="tpu_custom_call" | custom-call | flops 1342177280 | bytes 6586368 | tf_op jit(solution)/shard_map/pallas_call | solution.py:34
  92.9 0.1 collective-permute-start.8
  93.0 2.0 %collective-permute-start.11 = (bf16[656,256]{1,0:T(8,128)(2,1)S(1)}, bf16[656,256]{1,0:T(8,128)(2,1)S(1)}, u32[]{:S(2)}, u32[]{:S(2)}) collective-permute-start(bf16[656,256]{1,0:T(8,128)(2,1)S(1)} %get-tuple-element.37), channel_id=1, source_target_pairs={{0,32},{32,64},{64,96},{96,0},{1,33},{33,65},{65,97},{97,1},{2,34}... | collective-permute-start | bytes 1007624 | tf_op jit(solution)/shard_map/ppermute | solution.py:276
  95.0 5.7 %shard_map.83.refs_0_ = bf16[656,512]{1,0:T(8,128)(2,1)S(1)} custom-call(bf16[512,640]{1,0:T(8,128)(2,1)S(1)} %copy-done.1, f32[640,512]{1,0:T(8,128)S(1)} %get-tuple-element.27.refs_1_, f32[8,512]{1,0:T(8,128)S(1)} %get-tuple-element.28.refs_2_, bf16[512,640]{1,0:T(8,128)(2,1)S(1)} %collective-permute-done.2.refs_3_.refs_6_, ...), custom_call_target="tpu_custom_call" | custom-call | flops 1342177280 | bytes 4603904 | tf_op jit(solution)/shard_map/pallas_call | solution.py:34
  100.7 0.4 shard_map.93.att_ref
  101.0 1.2 collective-permute-start.21
  102.3 0.4 shard_map.88.att_ref
  102.7 2.4 %collective-permute-start.12 = (bf16[256,640]{1,0:T(8,128)(2,1)S(1)}, bf16[256,640]{1,0:T(8,128)(2,1)S(1)}, u32[]{:S(2)}, u32[]{:S(2)}) collective-permute-start(bf16[256,640]{1,0:T(8,128)(2,1)S(1)} %shard_map.88.att_ref), channel_id=1, source_target_pairs={{0,1},{1,0},{2,3},{3,2},{4,5},{5,4},{6,7},{7,6},{8,9},{9,8},{10,11... | collective-permute-start | bytes 983048 | tf_op jit(solution)/shard_map/ppermute | solution.py:279
  105.1 1.0 shard_map.90.w_ref
  106.1 7.1 %collective-permute-done.21.other_ref = bf16[256,640]{1,0:T(8,128)(2,1)S(1)} collective-permute-done((bf16[256,640]{1,0:T(8,128)(2,1)S(1)}, bf16[256,640]{1,0:T(8,128)(2,1)S(1)}, u32[]{:S(2)}, u32[]{:S(2)}) %collective-permute-start.21) | collective-permute-done | bytes 327712 | tf_op jit(solution)/shard_map/ppermute | solution.py:279
  113.2 2.2 %shard_map.94 = (bf16[256,640]{1,0:T(8,128)(2,1)S(1)}, bf16[256,640]{1,0:T(8,128)(2,1)S(1)}, bf16[256,640]{1,0:T(8,128)(2,1)S(1)}, bf16[256,640]{1,0:T(8,128)(2,1)S(1)}) custom-call(bf16[256,640]{1,0:T(8,128)(2,1)S(1)} %shard_map.93.att_ref, bf16[256,640]{1,0:T(8,128)(2,1)S(1)} %collective-permute-done.21.other_ref, bf16[4,1280,640]{2,1,0:T(8,128)(2,1)S(1)} %shard_map.90.w_ref), custom_call_target="tpu_custom_call" | custom-call | flops 1677721600 | bytes 7208960 | tf_op jit(solution)/shard_map/pallas_call | solution.py:34
  115.4 1.4 collective-permute-start.22
  116.8 0.6 collective-permute-start.23
  117.4 1.1 collective-permute-start.24
  118.5 2.2 %shard_map.91 = (bf16[256,640]{1,0:T(8,128)(2,1)S(1)}, bf16[256,640]{1,0:T(8,128)(2,1)S(1)}, bf16[256,640]{1,0:T(8,128)(2,1)S(1)}, bf16[256,640]{1,0:T(8,128)(2,1)S(1)}) custom-call(bf16[256,640]{1,0:T(8,128)(2,1)S(1)} %shard_map.88.att_ref, bf16[256,640]{1,0:T(8,128)(2,1)S(1)} %collective-permute-done.12.other_ref, bf16[4,1280,640]{2,1,0:T(8,128)(2,1)S(1)} %shard_map.90.w_ref), custom_call_target="tpu_custom_call" | custom-call | flops 1677721600 | bytes 7208960 | tf_op jit(solution)/shard_map/pallas_call | solution.py:34
  120.7 1.2 collective-permute-start.15
  121.9 2.7 %collective-permute-start.16 = (bf16[256,640]{1,0:T(8,128)(2,1)S(1)}, bf16[256,640]{1,0:T(8,128)(2,1)S(1)}, u32[]{:S(2)}, u32[]{:S(2)}) collective-permute-start(bf16[256,640]{1,0:T(8,128)(2,1)S(1)} %get-tuple-element.40), channel_id=1, source_target_pairs={{0,4},{2,6},{4,0},{6,2},{1,5},{3,7},{5,1},{7,3},{8,12},{10,14},{12... | collective-permute-start | bytes 983048 | tf_op jit(solution)/shard_map/ppermute | solution.py:289
  124.6 1.4 %collective-permute-done.22.refs_5_ = bf16[256,640]{1,0:T(8,128)(2,1)S(1)} collective-permute-done((bf16[256,640]{1,0:T(8,128)(2,1)S(1)}, bf16[256,640]{1,0:T(8,128)(2,1)S(1)}, u32[]{:S(2)}, u32[]{:S(2)}) %collective-permute-start.22) | collective-permute-done | bytes 327712 | tf_op jit(solution)/shard_map/ppermute | solution.py:289
  126.1 0.5 collective-permute-start.17
  126.6 6.0 %collective-permute-done.23.refs_6_ = bf16[256,640]{1,0:T(8,128)(2,1)S(1)} collective-permute-done((bf16[256,640]{1,0:T(8,128)(2,1)S(1)}, bf16[256,640]{1,0:T(8,128)(2,1)S(1)}, u32[]{:S(2)}, u32[]{:S(2)}) %collective-permute-start.23) | collective-permute-done | bytes 327712 | tf_op jit(solution)/shard_map/ppermute | solution.py:289
  132.6 1.9 %collective-permute-done.24.refs_7_ = bf16[256,640]{1,0:T(8,128)(2,1)S(1)} collective-permute-done((bf16[256,640]{1,0:T(8,128)(2,1)S(1)}, bf16[256,640]{1,0:T(8,128)(2,1)S(1)}, u32[]{:S(2)}, u32[]{:S(2)}) %collective-permute-start.24) | collective-permute-done | bytes 327712 | tf_op jit(solution)/shard_map/ppermute | solution.py:289
  134.4 1.6 %collective-permute-done.15.refs_1_ = bf16[256,640]{1,0:T(8,128)(2,1)S(1)} collective-permute-done((bf16[256,640]{1,0:T(8,128)(2,1)S(1)}, bf16[256,640]{1,0:T(8,128)(2,1)S(1)}, u32[]{:S(2)}, u32[]{:S(2)}) %collective-permute-start.15) | collective-permute-done | bytes 327712 | tf_op jit(solution)/shard_map/ppermute | solution.py:289
  136.1 3.5 %collective-permute-done.16.refs_2_ = bf16[256,640]{1,0:T(8,128)(2,1)S(1)} collective-permute-done((bf16[256,640]{1,0:T(8,128)(2,1)S(1)}, bf16[256,640]{1,0:T(8,128)(2,1)S(1)}, u32[]{:S(2)}, u32[]{:S(2)}) %collective-permute-start.16) | collective-permute-done | bytes 327712 | tf_op jit(solution)/shard_map/ppermute | solution.py:289
  139.6 1.9 %collective-permute-done.17.refs_3_ = bf16[256,640]{1,0:T(8,128)(2,1)S(1)} collective-permute-done((bf16[256,640]{1,0:T(8,128)(2,1)S(1)}, bf16[256,640]{1,0:T(8,128)(2,1)S(1)}, u32[]{:S(2)}, u32[]{:S(2)}) %collective-permute-start.17) | collective-permute-done | bytes 327712 | tf_op jit(solution)/shard_map/ppermute | solution.py:289
  141.5 1.3 shard_map.95
  (37 shorter events, 0.1 us)
Async XLA Ops:
  0.0 2.9 %copy-start = (bf16[640,5120]{1,0:T(8,128)(2,1)S(1)}, bf16[640,5120]{1,0:T(8,128)(2,1)}, u32[]{:S(2)}) copy-start(bf16[640,5120]{1,0:T(8,128)(2,1)} %w_ref.3) | copy-start | bytes 19660804
  2.9 4.4 %copy-start.4 = (bf16[512,640]{1,0:T(8,128)(2,1)S(1)}, bf16[512,640]{1,0:T(8,128)(2,1)}, u32[]{:S(2)}) copy-start(bf16[512,640]{1,0:T(8,128)(2,1)} %refs_1_.3) | copy-start | bytes 1966084
  2.9 4.4 %copy-start.5 = (bf16[512,640]{1,0:T(8,128)(2,1)S(1)}, bf16[512,640]{1,0:T(8,128)(2,1)}, u32[]{:S(2)}) copy-start(bf16[512,640]{1,0:T(8,128)(2,1)} %refs_2_.5) | copy-start | bytes 1966084
  2.9 22.0 %copy-start.1 = (bf16[512,640]{1,0:T(8,128)(2,1)S(1)}, bf16[512,640]{1,0:T(8,128)(2,1)}, u32[]{:S(2)}) copy-start(bf16[512,640]{1,0:T(8,128)(2,1)} %refs_0_.3) | copy-start | bytes 1966084
  3.1 39.9 %collective-permute-start.13 = (bf16[1280,640]{1,0:T(8,128)(2,1)S(1)}, bf16[1280,640]{1,0:T(8,128)(2,1)S(1)}, u32[]{:S(2)}, u32[]{:S(2)}) collective-permute-start(bf16[1280,640]{1,0:T(8,128)(2,1)S(1)} %shard_map.89), channel_id=1, source_target_pairs={{0,17},{17,0},{1,16},{16,1},{2,19},{19,2},{3,18},{18,3},{4,21},{21... | collective-permute-start | bytes 4915208 | tf_op jit(solution)/shard_map/ppermute | solution.py:247
  7.2 17.6 %collective-permute-start.2 = (bf16[512,640]{1,0:T(8,128)(2,1)S(1)}, bf16[512,640]{1,0:T(8,128)(2,1)S(1)}, u32[]{:S(2)}, u32[]{:S(2)}) collective-permute-start(bf16[512,640]{1,0:T(8,128)(2,1)S(1)} %copy-done.4), channel_id=1, source_target_pairs={{0,16},{16,0},{1,17},{17,1},{2,18},{18,2},{3,19},{19,3},{4,20},{20... | collective-permute-start | bytes 1966088 | tf_op jit(solution)/shard_map/ppermute | solution.py:229
  7.2 19.7 %collective-permute-start = (bf16[512,640]{1,0:T(8,128)(2,1)S(1)}, bf16[512,640]{1,0:T(8,128)(2,1)S(1)}, u32[]{:S(2)}, u32[]{:S(2)}) collective-permute-start(bf16[512,640]{1,0:T(8,128)(2,1)S(1)} %copy-done.4), channel_id=1, source_target_pairs={{0,8},{8,0},{1,9},{9,1},{2,10},{10,2},{3,11},{11,3},{4,12},{12,4},... | collective-permute-start | bytes 1966088 | tf_op jit(solution)/shard_map/ppermute | solution.py:233
  7.2 30.2 %collective-permute-start.3 = (bf16[512,640]{1,0:T(8,128)(2,1)S(1)}, bf16[512,640]{1,0:T(8,128)(2,1)S(1)}, u32[]{:S(2)}, u32[]{:S(2)}) collective-permute-start(bf16[512,640]{1,0:T(8,128)(2,1)S(1)} %copy-done.5), channel_id=1, source_target_pairs={{0,16},{16,0},{1,17},{17,1},{2,18},{18,2},{3,19},{19,3},{4,20},{20... | collective-permute-start | bytes 1966088 | tf_op jit(solution)/shard_map/ppermute | solution.py:230
  9.3 28.7 %collective-permute-start.1 = (bf16[512,640]{1,0:T(8,128)(2,1)S(1)}, bf16[512,640]{1,0:T(8,128)(2,1)S(1)}, u32[]{:S(2)}, u32[]{:S(2)}) collective-permute-start(bf16[512,640]{1,0:T(8,128)(2,1)S(1)} %copy-done.5), channel_id=1, source_target_pairs={{0,8},{8,0},{1,9},{9,1},{2,10},{10,2},{3,11},{11,3},{4,12},{12,4},... | collective-permute-start | bytes 1966088 | tf_op jit(solution)/shard_map/ppermute | solution.py:234
  24.8 16.0 %collective-permute-start.9 = (bf16[512,640]{1,0:T(8,128)(2,1)S(1)}, bf16[512,640]{1,0:T(8,128)(2,1)S(1)}, u32[]{:S(2)}, u32[]{:S(2)}) collective-permute-start(bf16[512,640]{1,0:T(8,128)(2,1)S(1)} %copy-done.1), channel_id=1, source_target_pairs={{0,64},{32,96},{64,0},{96,32},{1,65},{33,97},{65,1},{97,33},{2,66}... | collective-permute-start | bytes 1966088 | tf_op jit(solution)/shard_map/ppermute | solution.py:235
  27.0 27.4 %collective-permute-start.6 = (bf16[512,640]{1,0:T(8,128)(2,1)S(1)}, bf16[512,640]{1,0:T(8,128)(2,1)S(1)}, u32[]{:S(2)}, u32[]{:S(2)}) collective-permute-start(bf16[512,640]{1,0:T(8,128)(2,1)S(1)} %copy-done.1), channel_id=1, source_target_pairs={{0,32},{32,64},{64,96},{96,0},{1,33},{33,65},{65,97},{97,1},{2,34}... | collective-permute-start | bytes 1966088 | tf_op jit(solution)/shard_map/ppermute | solution.py:231
  37.5 16.9 %collective-permute-start.7 = (bf16[512,640]{1,0:T(8,128)(2,1)S(1)}, bf16[512,640]{1,0:T(8,128)(2,1)S(1)}, u32[]{:S(2)}, u32[]{:S(2)}) collective-permute-start(bf16[512,640]{1,0:T(8,128)(2,1)S(1)} %copy-done.1), channel_id=1, source_target_pairs={{0,96},{32,0},{64,32},{96,64},{1,97},{33,1},{65,33},{97,65},{2,98}... | collective-permute-start | bytes 1966088 | tf_op jit(solution)/shard_map/ppermute | solution.py:232
  38.0 25.7 %collective-permute-start.4 = (bf16[512,640]{1,0:T(8,128)(2,1)S(1)}, bf16[512,640]{1,0:T(8,128)(2,1)S(1)}, u32[]{:S(2)}, u32[]{:S(2)}) collective-permute-start(bf16[512,640]{1,0:T(8,128)(2,1)S(1)} %collective-permute-done.2.refs_3_.refs_6_), channel_id=1, source_target_pairs={{0,8},{8,0},{1,9},{9,1},{2,10},{10,2},{3,11},{11,3},{4,12},{12,4},... | collective-permute-start | bytes 1966088 | tf_op jit(solution)/shard_map/ppermute | solution.py:236
  40.8 22.8 %collective-permute-start.5 = (bf16[512,640]{1,0:T(8,128)(2,1)S(1)}, bf16[512,640]{1,0:T(8,128)(2,1)S(1)}, u32[]{:S(2)}, u32[]{:S(2)}) collective-permute-start(bf16[512,640]{1,0:T(8,128)(2,1)S(1)} %collective-permute-done.3.refs_4_.refs_7_), channel_id=1, source_target_pairs={{0,8},{8,0},{1,9},{9,1},{2,10},{10,2},{3,11},{11,3},{4,12},{12,4},... | collective-permute-start | bytes 1966088 | tf_op jit(solution)/shard_map/ppermute | solution.py:237
  43.0 62.1 %collective-permute-start.14 = (bf16[1280,640]{1,0:T(8,128)(2,1)S(1)}, bf16[1280,640]{1,0:T(8,128)(2,1)S(1)}, u32[]{:S(2)}, u32[]{:S(2)}) collective-permute-start(bf16[1280,640]{1,0:T(8,128)(2,1)S(1)} %collective-permute-done.13.wz_ref), channel_id=1, source_target_pairs={{0,8},{8,0},{1,9},{9,1},{2,10},{10,2},{3,11},{11,3},{4,12},{12,4},... | collective-permute-start | bytes 4915208 | tf_op jit(solution)/shard_map/ppermute | solution.py:248
  69.3 23.6 %collective-permute-start.19 = (bf16[656,256]{1,0:T(8,128)(2,1)S(1)}, bf16[656,256]{1,0:T(8,128)(2,1)S(1)}, u32[]{:S(2)}, u32[]{:S(2)}) collective-permute-start(bf16[656,256]{1,0:T(8,128)(2,1)S(1)} %get-tuple-element.43), channel_id=1, source_target_pairs={{0,64},{32,96},{64,0},{96,32},{1,65},{33,97},{65,1},{97,33},{2,66}... | collective-permute-start | bytes 1007624 | tf_op jit(solution)/shard_map/ppermute | solution.py:275
  72.0 7.7 %copy-start.6 = (bf16[512,640]{1,0:T(8,128)(2,1)S(1)}, bf16[512,640]{1,0:T(8,128)(2,1)}, u32[]{:S(2)}) copy-start(bf16[512,640]{1,0:T(8,128)(2,1)} %refs_1_.2) | copy-start | bytes 1966084
  72.0 7.7 %copy-start.7 = (bf16[512,640]{1,0:T(8,128)(2,1)S(1)}, bf16[512,640]{1,0:T(8,128)(2,1)}, u32[]{:S(2)}) copy-start(bf16[512,640]{1,0:T(8,128)(2,1)} %refs_2_.3) | copy-start | bytes 1966084
  77.6 15.4 %collective-permute-start.18 = (bf16[656,256]{1,0:T(8,128)(2,1)S(1)}, bf16[656,256]{1,0:T(8,128)(2,1)S(1)}, u32[]{:S(2)}, u32[]{:S(2)}) collective-permute-start(bf16[656,256]{1,0:T(8,128)(2,1)S(1)} %get-tuple-element.42), channel_id=1, source_target_pairs={{0,96},{32,0},{64,32},{96,64},{1,97},{33,1},{65,33},{97,65},{2,98}... | collective-permute-start | bytes 1007624 | tf_op jit(solution)/shard_map/ppermute | solution.py:274
  77.7 23.0 %collective-permute-start.20 = (bf16[656,256]{1,0:T(8,128)(2,1)S(1)}, bf16[656,256]{1,0:T(8,128)(2,1)S(1)}, u32[]{:S(2)}, u32[]{:S(2)}) collective-permute-start(bf16[656,256]{1,0:T(8,128)(2,1)S(1)} %get-tuple-element.44), channel_id=1, source_target_pairs={{0,32},{32,64},{64,96},{96,0},{1,33},{33,65},{65,97},{97,1},{2,34}... | collective-permute-start | bytes 1007624 | tf_op jit(solution)/shard_map/ppermute | solution.py:276
  85.2 17.1 %collective-permute-start.10 = (bf16[656,256]{1,0:T(8,128)(2,1)S(1)}, bf16[656,256]{1,0:T(8,128)(2,1)S(1)}, u32[]{:S(2)}, u32[]{:S(2)}) collective-permute-start(bf16[656,256]{1,0:T(8,128)(2,1)S(1)} %get-tuple-element.36), channel_id=1, source_target_pairs={{0,64},{32,96},{64,0},{96,32},{1,65},{33,97},{65,1},{97,33},{2,66}... | collective-permute-start | bytes 1007624 | tf_op jit(solution)/shard_map/ppermute | solution.py:275
  87.3 17.8 %slice-start = ((s8[6553600]{0:T(1024)(128)(4,1)}), s8[2359296]{0:T(1024)(128)(4,1)S(1)}, s32[]{:S(2)}) async-start(s8[6553600]{0:T(1024)(128)(4,1)} %bitcast), calls=%async_computation | async-start | bytes 4718592
  92.9 9.4 %collective-permute-start.8 = (bf16[656,256]{1,0:T(8,128)(2,1)S(1)}, bf16[656,256]{1,0:T(8,128)(2,1)S(1)}, u32[]{:S(2)}, u32[]{:S(2)}) collective-permute-start(bf16[656,256]{1,0:T(8,128)(2,1)S(1)} %get-tuple-element.33), channel_id=1, source_target_pairs={{0,96},{32,0},{64,32},{96,64},{1,97},{33,1},{65,33},{97,65},{2,98}... | collective-permute-start | bytes 1007624 | tf_op jit(solution)/shard_map/ppermute | solution.py:274
  93.0 9.3 %collective-permute-start.11 = (bf16[656,256]{1,0:T(8,128)(2,1)S(1)}, bf16[656,256]{1,0:T(8,128)(2,1)S(1)}, u32[]{:S(2)}, u32[]{:S(2)}) collective-permute-start(bf16[656,256]{1,0:T(8,128)(2,1)S(1)} %get-tuple-element.37), channel_id=1, source_target_pairs={{0,32},{32,64},{64,96},{96,0},{1,33},{33,65},{65,97},{97,1},{2,34}... | collective-permute-start | bytes 1007624 | tf_op jit(solution)/shard_map/ppermute | solution.py:276
  95.0 10.2 %slice-start.1 = ((s8[6553600]{0:T(1024)(128)(4,1)}), s8[4194304]{0:T(1024)(128)(4,1)S(1)}, s32[]{:S(2)}) async-start(s8[6553600]{0:T(1024)(128)(4,1)} %bitcast), calls=%async_computation.1 | async-start | bytes 8388608
  101.0 12.2 %collective-permute-start.21 = (bf16[256,640]{1,0:T(8,128)(2,1)S(1)}, bf16[256,640]{1,0:T(8,128)(2,1)S(1)}, u32[]{:S(2)}, u32[]{:S(2)}) collective-permute-start(bf16[256,640]{1,0:T(8,128)(2,1)S(1)} %shard_map.93.att_ref), channel_id=1, source_target_pairs={{0,1},{1,0},{2,3},{3,2},{4,5},{5,4},{6,7},{7,6},{8,9},{9,8},{10,11... | collective-permute-start | bytes 983048 | tf_op jit(solution)/shard_map/ppermute | solution.py:279
  102.7 15.8 %collective-permute-start.12 = (bf16[256,640]{1,0:T(8,128)(2,1)S(1)}, bf16[256,640]{1,0:T(8,128)(2,1)S(1)}, u32[]{:S(2)}, u32[]{:S(2)}) collective-permute-start(bf16[256,640]{1,0:T(8,128)(2,1)S(1)} %shard_map.88.att_ref), channel_id=1, source_target_pairs={{0,1},{1,0},{2,3},{3,2},{4,5},{5,4},{6,7},{7,6},{8,9},{9,8},{10,11... | collective-permute-start | bytes 983048 | tf_op jit(solution)/shard_map/ppermute | solution.py:279
  115.4 10.6 %collective-permute-start.22 = (bf16[256,640]{1,0:T(8,128)(2,1)S(1)}, bf16[256,640]{1,0:T(8,128)(2,1)S(1)}, u32[]{:S(2)}, u32[]{:S(2)}) collective-permute-start(bf16[256,640]{1,0:T(8,128)(2,1)S(1)} %get-tuple-element.46), channel_id=1, source_target_pairs={{0,2},{2,4},{4,6},{6,0},{1,3},{3,5},{5,7},{7,1},{8,10},{10,12},{12... | collective-permute-start | bytes 983048 | tf_op jit(solution)/shard_map/ppermute | solution.py:289
  116.8 15.8 %collective-permute-start.23 = (bf16[256,640]{1,0:T(8,128)(2,1)S(1)}, bf16[256,640]{1,0:T(8,128)(2,1)S(1)}, u32[]{:S(2)}, u32[]{:S(2)}) collective-permute-start(bf16[256,640]{1,0:T(8,128)(2,1)S(1)} %get-tuple-element.47), channel_id=1, source_target_pairs={{0,4},{2,6},{4,0},{6,2},{1,5},{3,7},{5,1},{7,3},{8,12},{10,14},{12... | collective-permute-start | bytes 983048 | tf_op jit(solution)/shard_map/ppermute | solution.py:289
  117.4 24.1 %copy-start.2 = (bf16[512,640]{1,0:T(8,128)(2,1)S(1)}, bf16[512,640]{1,0:T(8,128)(2,1)}, u32[]{:S(2)}) copy-start(bf16[512,640]{1,0:T(8,128)(2,1)} %residual_ref.1) | copy-start | bytes 1966084
  117.4 24.1 %copy-start.3 = (f32[640]{0:T(1024)S(1)}, f32[640]{0:T(1024)}, u32[]{:S(2)}) copy-start(f32[640]{0:T(1024)} %gate_ref.1) | copy-start | bytes 7684
  117.4 17.0 %collective-permute-start.24 = (bf16[256,640]{1,0:T(8,128)(2,1)S(1)}, bf16[256,640]{1,0:T(8,128)(2,1)S(1)}, u32[]{:S(2)}, u32[]{:S(2)}) collective-permute-start(bf16[256,640]{1,0:T(8,128)(2,1)S(1)} %get-tuple-element.48), channel_id=1, source_target_pairs={{0,6},{2,0},{4,2},{6,4},{1,7},{3,1},{5,3},{7,5},{8,14},{10,8},{12,... | collective-permute-start | bytes 983048 | tf_op jit(solution)/shard_map/ppermute | solution.py:289
  120.7 15.4 %collective-permute-start.15 = (bf16[256,640]{1,0:T(8,128)(2,1)S(1)}, bf16[256,640]{1,0:T(8,128)(2,1)S(1)}, u32[]{:S(2)}, u32[]{:S(2)}) collective-permute-start(bf16[256,640]{1,0:T(8,128)(2,1)S(1)} %get-tuple-element.39), channel_id=1, source_target_pairs={{0,2},{2,4},{4,6},{6,0},{1,3},{3,5},{5,7},{7,1},{8,10},{10,12},{12... | collective-permute-start | bytes 983048 | tf_op jit(solution)/shard_map/ppermute | solution.py:289
  121.9 17.7 %collective-permute-start.16 = (bf16[256,640]{1,0:T(8,128)(2,1)S(1)}, bf16[256,640]{1,0:T(8,128)(2,1)S(1)}, u32[]{:S(2)}, u32[]{:S(2)}) collective-permute-start(bf16[256,640]{1,0:T(8,128)(2,1)S(1)} %get-tuple-element.40), channel_id=1, source_target_pairs={{0,4},{2,6},{4,0},{6,2},{1,5},{3,7},{5,1},{7,3},{8,12},{10,14},{12... | collective-permute-start | bytes 983048 | tf_op jit(solution)/shard_map/ppermute | solution.py:289
  126.1 15.4 %collective-permute-start.17 = (bf16[256,640]{1,0:T(8,128)(2,1)S(1)}, bf16[256,640]{1,0:T(8,128)(2,1)S(1)}, u32[]{:S(2)}, u32[]{:S(2)}) collective-permute-start(bf16[256,640]{1,0:T(8,128)(2,1)S(1)} %get-tuple-element.41), channel_id=1, source_target_pairs={{0,6},{2,0},{4,2},{6,4},{1,7},{3,1},{5,3},{7,5},{8,14},{10,8},{12,... | collective-permute-start | bytes 983048 | tf_op jit(solution)/shard_map/ppermute | solution.py:289

commit v4 on v3

--- a/solution.py
+++ b/solution.py
@@ -29,8 +29,8 @@
     return lax.dot_general(a, b, dims, preferred_element_type=jnp.float32)
 
 
-def call(kernel, out_shape, *args, limit, scratch=(), specs=None, flops=0):
-    size = sum(x.size * x.dtype.itemsize for x in args)
+def call(kernel, out_shape, *args, limit, scratch=(), specs=None, flops=0, size=None):
+    size = sum(x.size * x.dtype.itemsize for x in args) if size is None else size
     return pl.pallas_call(
         kernel,
         out_shape=out_shape,
@@ -69,27 +69,49 @@
     lax.fori_loop(0, heads, run, 0)
 
 
+def early_own_kernel(*refs):
+    q, k, v, *rest, q_in, k_in, v_in, sems = refs
+    copies = [pltpu.make_async_copy(a, b, sems.at[i]) for i, (a, b) in enumerate(((q, q_in), (k, k_in), (v, v_in)))]
+    for copy in copies:
+        copy.start()
+    for copy in copies:
+        copy.wait()
+    early_kernel(1, q_in, k_in, v_in, *rest)
+
+
 def early_kernel(count, *refs):
     queries, (ka, va, kb, vb), outs = refs[:count], refs[count : count + 4], refs[count + 4 :]
-    n = queries[0].shape[0]
+    ends = [sum(r.shape[0] for r in queries[: i + 1]) for i in range(count)]
 
     def step(h, at):
         q = jnp.concatenate([r[:, at] for r in queries], axis=0)
         out, lse = attend(q, [(ka[:, at], va[:, at]), (kb[:, at], vb[:, at])])
         for i in range(count):
-            outs[2 * i][at, :] = out[:, i * n : (i + 1) * n]
-            outs[2 * i + 1][pl.ds(h, 1), :] = lse[:, i * n : (i + 1) * n]
+            span = slice(ends[i] - queries[i].shape[0], ends[i])
+            outs[2 * i][at, :] = out[:, span]
+            outs[2 * i + 1][pl.ds(h, 1), :] = lse[:, span]
 
     head_loop(queries[0].shape[1] // HD, step)
 
 
-def early(queries, *kv):
-    n, width = queries[0].shape
-    count = len(queries)
-    shapes = (jax.ShapeDtypeStruct((width, n), jnp.float32), jax.ShapeDtypeStruct((8, n), jnp.float32)) * count
-    return call(
-        functools.partial(early_kernel, count), shapes, *queries, *kv, limit=26, flops=count * 8 * n * n * width
-    )
+def early(queries, *kv, load=False):
+    keys, width = kv[0].shape
+    shapes = [
+        (jax.ShapeDtypeStruct((width, q.shape[0]), jnp.float32), jax.ShapeDtypeStruct((8, q.shape[0]), jnp.float32))
+        for q in queries
+    ]
+    parts = call(
+        early_own_kernel if load else functools.partial(early_kernel, len(queries)),
+        tuple(shape for pair in shapes for shape in pair),
+        *queries,
+        *kv,
+        limit=26,
+        specs=[pl.BlockSpec(memory_space=pltpu.HBM)] * 3 + [VMEM] * 2 if load else None,
+        scratch=[pltpu.VMEM((keys, width), jnp.bfloat16)] * 3 + [pltpu.SemaphoreType.DMA((3,))] if load else (),
+        size=0 if load else None,
+        flops=sum(q.shape[0] for q in queries) * 8 * keys * width,
+    )
+    return [tuple(parts[2 * i : 2 * i + 2]) for i in range(len(queries))]
 
 
 def late_kernel(segments, *refs):
@@ -125,7 +147,7 @@
 
 
 def late(segments, *kv):
-    whole, width = segments[0][0].shape
+    whole, width = kv[0].shape
     spans = tuple((first, n) for _, _, first, n in segments)
     return call(
         functools.partial(late_kernel, spans),
@@ -204,10 +226,37 @@
                 getattr(other_rows(j, ws_ref), act)()
 
 
-def project_kernel(att_ref, other_ref, w_ref, *outs):
-    act = jnp.concatenate([att_ref[...], other_ref[...]], axis=1)
-    for j, out_ref in enumerate(outs):
-        out_ref[...] = jnp.dot(act, w_ref[j], preferred_element_type=jnp.float32).astype(jnp.bfloat16)
+def relay_kernel(*refs):
+    n = refs[0].shape[0] // CHUNKS
+    for i in range(CHUNKS):
+        refs[CHUNKS + i][...] = refs[i][i * n : (i + 1) * n, :]
+
+
+def project_own_kernel(att_ref, w_ref, out_ref):
+    width = att_ref.shape[1]
+    for j in range(4):
+        out_ref[j] = jnp.dot(att_ref[...], w_ref[j, 0:width, :], preferred_element_type=jnp.float32)
+
+
+def project_other_kernel(targets, own_ref, other_ref, w_ref, *outs):
+    width = other_ref.shape[1]
+    for j, out_ref in zip(targets, outs, strict=True):
+        rest = jnp.dot(other_ref[...], w_ref[j, width : 2 * width, :], preferred_element_type=jnp.float32)
+        out_ref[...] = (own_ref[j] + rest).astype(jnp.bfloat16)
+
+
+def project(attended, other, weights):
+    n, width = attended.shape
+    shape = jax.ShapeDtypeStruct((4, n, width), jnp.float32)
+    own = call(project_own_kernel, shape, attended, weights, limit=16, flops=8 * n * width * width)
+    pieces = {}
+    for targets in ((1, 3), (2, 0)):
+        shapes = (jax.ShapeDtypeStruct((n, width), jnp.bfloat16),) * len(targets)
+        kernel = functools.partial(project_other_kernel, targets)
+        flops = len(targets) * 2 * n * width * width
+        outs = call(kernel, shapes, own, other, weights, limit=16, flops=flops)
+        pieces.update(zip(targets, outs, strict=True))
+    return pieces
 
 
 def final_kernel(residual_ref, gate_ref, *refs):
@@ -224,68 +273,64 @@
     rows, width = query.shape
     n = rows // CHUNKS
     swap = ring(2, 1)
-    hbm = pl.BlockSpec(memory_space=pl.ANY)
-
+    hbm = pl.BlockSpec(memory_space=pltpu.HBM)
+
+    query_at, key_at, value_at, weight_at = (
+        pltpu.with_memory_space_constraint(x, pltpu.HBM) for x in (query, key_fresh, value_fresh, out_weight)
+    )
+    k_s = lax.ppermute(key_stale, "c", swap)
+    v_s = lax.ppermute(value_stale, "c", swap)
     k_z = lax.ppermute(key_stale, "zl", swap)
     v_z = lax.ppermute(value_stale, "zl", swap)
     q1 = lax.ppermute(query, "x", ring(4, 1))
     q3 = lax.ppermute(query, "x", ring(4, 3))
-    k_s = lax.ppermute(key_stale, "c", swap)
-    v_s = lax.ppermute(value_stale, "c", swap)
-    q2 = lax.ppermute(query, "x", ring(4, 2))
     k_zs = lax.ppermute(k_z, "c", swap)
     v_zs = lax.ppermute(v_z, "c", swap)
+    relayed = call(relay_kernel, (jax.ShapeDtypeStruct((n, width), jnp.bfloat16),) * CHUNKS, q1, q3, limit=4)
+    q2 = [lax.ppermute(relayed[i], "x", ring(4, 1 + 2 * i)) for i in range(CHUNKS)]
 
     parcel = call(
         parcel_kernel,
         jax.ShapeDtypeStruct((2 * width, width), jnp.bfloat16),
-        out_weight,
+        weight_at,
         limit=4,
         specs=[hbm],
         scratch=[pltpu.SemaphoreType.DMA((2,))],
+        size=0,
     )
     w_z = lax.ppermute(parcel, ("zl", "zh"), [(0, 3), (3, 0), (1, 2), (2, 1)])
     w_s = lax.ppermute(w_z, "c", swap)
 
-    e0 = early((query,), key_fresh, value_fresh, k_s, v_s)
-    e13 = early((q1, q3), key_stale, value_stale, k_s, v_s)
-    e2 = early((q2,), key_stale, value_stale, k_s, v_s)
+    (e0,) = early((query_at,), key_at, value_at, k_s, v_s, load=True)
+    e1, e3 = early((q1, q3), key_stale, value_stale, k_s, v_s)
+    e2 = early(q2, key_stale, value_stale, k_s, v_s)
     far = (k_z, v_z, k_zs, v_zs)
-    firsts = [i * n for i in range(CHUNKS)]
-    pairs = [late([(q1, e13[:2], first, n), (q3, e13[2:], first, n)], *far) for first in firsts]
-    middle = late([(q2, e2, first, n) for first in firsts], *far)
-    (o0,) = late([(query, e0, 0, rows)], *far)
+    sent = [late([(q1, e1, i * n, n), (q2[i], e2[i], 0, n), (q3, e3, i * n, n)], *far) for i in range(CHUNKS)]
+    own = [late([(query, e0, i * n, n)], *far)[0] for i in range(CHUNKS)]
     weights = call(
         weight_kernel,
         jax.ShapeDtypeStruct((4, 2 * width, width), jnp.bfloat16),
-        out_weight,
+        weight_at,
         w_z,
         w_s,
         limit=10,
-        specs=[hbm] * 3,
+        specs=[hbm, pl.BlockSpec(memory_space=pl.ANY), pl.BlockSpec(memory_space=pl.ANY)],
         scratch=[pltpu.SemaphoreType.DMA((8,))],
+        size=0,
     )
 
     landed = []
     for i in range(CHUNKS):
-        o1, o3 = pairs[i]
+        o1, o2, o3 = sent[i]
         parts = (
-            o0,
+            own[i],
             lax.ppermute(o1, "x", ring(4, 3)),
-            lax.ppermute(middle[i], "x", ring(4, 2)),
+            lax.ppermute(o2, "x", ring(4, 2)),
             lax.ppermute(o3, "x", ring(4, 1)),
         )
-        attended = merge(i * n, n, parts)
+        attended = merge(0, n, parts)
         other = lax.ppermute(attended, "zh", swap)
-        pieces = call(
-            project_kernel,
-            (jax.ShapeDtypeStruct((n, width), jnp.bfloat16),) * 4,
-            attended,
-            other,
-            weights,
-            limit=16,
-            flops=16 * n * width * width,
-        )
+        pieces = project(attended, other, weights)
         landed += [pieces[0], *(lax.ppermute(pieces[j], "y", ring(4, j)) for j in range(1, 4))]
     shape = jax.ShapeDtypeStruct((rows, width), jnp.bfloat16)
     return call(final_kernel, shape, residual, gate, *landed, limit=8)

time: 144 us -> 143 us (level)
  the two profiles are of different devices: /device:TPU:18 before, /device:TPU:32 now
where the time goes in v4:
time: 143 us; the launch traced here: 142 us
  Pallas kernels  55.6 us (39%)
  starting transfers between devices  44.2 us (31%)
  waiting for transfers between devices  42.3 us (30%)
    pallas_call x19, Pallas kernels, call(): pl.pallas_call(kernel, out_shape=out_shape, in_specs=specs or [VMEM] * le...  55.6 us
    ppermute x6, starting transfers between devices, block(): lax.ppermute(pieces[j], 'y', ring(4, j))  16.6 us
    ppermute x1, waiting for transfers between devices, block(): v_z = lax.ppermute(value_stale, 'zl', swap)  12.9 us
    ppermute x1, waiting for transfers between devices, block(): k_z = lax.ppermute(key_stale, 'zl', swap)  12.3 us
    ppermute x6, waiting for transfers between devices, block(): lax.ppermute(pieces[j], 'y', ring(4, j))  12 us
    ppermute x2, starting transfers between devices, block(): lax.ppermute(o3, 'x', ring(4, 1))  5.47 us
    ppermute x1, waiting for transfers between devices, block(): w_z = lax.ppermute(parcel, ('zl', 'zh'), [(0, 3), (3, 0), (1, 2), (2, 1)])  5.07 us
    ppermute x2, starting transfers between devices, block(): other = lax.ppermute(attended, 'zh', swap)  4.2 us
  transfers between devices with their start and end apart: 26, of which 6 were waited for; matrix products, arithmetic and copies ran while one was open for 0% of the time, Pallas kernels for 37%

profile of v4, /device:TPU:32, one launch (start us, length us, event | category | flops | bytes accessed | tf_op | source)
XLA Modules:
  0.0 142.4 jit_solution(15306265408179067616)
XLA Ops:
  0.0 1.6 %shard_map.89 = bf16[1280,640]{1,0:T(8,128)(2,1)S(1)} custom-call(bf16[640,5120]{1,0:T(8,128)(2,1)} %w_ref.3), custom_call_target="tpu_custom_call" | custom-call | tf_op jit(solution)/shard_map/pallas_call | solution.py:34
  1.6 2.0 %collective-permute-start.13 = (bf16[1280,640]{1,0:T(8,128)(2,1)S(1)}, bf16[1280,640]{1,0:T(8,128)(2,1)S(1)}, u32[]{:S(2)}, u32[]{:S(2)}) collective-permute-start(bf16[1280,640]{1,0:T(8,128)(2,1)S(1)} %shard_map.89), channel_id=1, source_target_pairs={{0,17},{17,0},{1,16},{16,1},{2,19},{19,2},{3,18},{18,3},{4,21},{21... | collective-permute-start | bytes 4915208 | tf_op jit(solution)/shard_map/ppermute | solution.py:301
  3.6 2.2 %collective-permute-start.2 = (bf16[512,640]{1,0:T(8,128)(2,1)S(1)}, bf16[512,640]{1,0:T(8,128)(2,1)S(1)}, u32[]{:S(2)}, u32[]{:S(2)}) collective-permute-start(bf16[512,640]{1,0:T(8,128)(2,1)S(1)} %copy-done.4), channel_id=1, source_target_pairs={{0,16},{16,0},{1,17},{17,1},{2,18},{18,2},{3,19},{19,3},{4,20},{20... | collective-permute-start | bytes 1966088 | tf_op jit(solution)/shard_map/ppermute | solution.py:283
  5.8 0.1 collective-permute-start.3
  5.9 1.5 %collective-permute-start.6 = (bf16[512,640]{1,0:T(8,128)(2,1)S(1)}, bf16[512,640]{1,0:T(8,128)(2,1)S(1)}, u32[]{:S(2)}, u32[]{:S(2)}) collective-permute-start(bf16[512,640]{1,0:T(8,128)(2,1)S(1)} %copy-done), channel_id=1, source_target_pairs={{0,32},{32,64},{64,96},{96,0},{1,33},{33,65},{65,97},{97,1},{2,34}... | collective-permute-start | bytes 1966088 | tf_op jit(solution)/shard_map/ppermute | solution.py:285
  7.4 1.7 %collective-permute-start.7 = (bf16[512,640]{1,0:T(8,128)(2,1)S(1)}, bf16[512,640]{1,0:T(8,128)(2,1)S(1)}, u32[]{:S(2)}, u32[]{:S(2)}) collective-permute-start(bf16[512,640]{1,0:T(8,128)(2,1)S(1)} %copy-done), channel_id=1, source_target_pairs={{0,96},{32,0},{64,32},{96,64},{1,97},{33,1},{65,33},{97,65},{2,98}... | collective-permute-start | bytes 1966088 | tf_op jit(solution)/shard_map/ppermute | solution.py:286
  9.1 12.3 %collective-permute-done.2.refs_3_.refs_9_ = bf16[512,640]{1,0:T(8,128)(2,1)S(1)} collective-permute-done((bf16[512,640]{1,0:T(8,128)(2,1)S(1)}, bf16[512,640]{1,0:T(8,128)(2,1)S(1)}, u32[]{:S(2)}, u32[]{:S(2)}) %collective-permute-start.2) | collective-permute-done | bytes 655392 | tf_op jit(solution)/shard_map/ppermute | solution.py:283
  21.4 12.9 %collective-permute-done.3.refs_4_.refs_10_ = bf16[512,640]{1,0:T(8,128)(2,1)S(1)} collective-permute-done((bf16[512,640]{1,0:T(8,128)(2,1)S(1)}, bf16[512,640]{1,0:T(8,128)(2,1)S(1)}, u32[]{:S(2)}, u32[]{:S(2)}) %collective-permute-start.3) | collective-permute-done | bytes 655392 | tf_op jit(solution)/shard_map/ppermute | solution.py:284
  34.3 5.1 %collective-permute-done.13.wz_ref = bf16[1280,640]{1,0:T(8,128)(2,1)S(1)} collective-permute-done((bf16[1280,640]{1,0:T(8,128)(2,1)S(1)}, bf16[1280,640]{1,0:T(8,128)(2,1)S(1)}, u32[]{:S(2)}, u32[]{:S(2)}) %collective-permute-start.13) | collective-permute-done | bytes 1638432 | tf_op jit(solution)/shard_map/ppermute | solution.py:301
  39.4 0.5 collective-permute-start.4
  39.9 0.1 collective-permute-start.5
  40.0 0.1 shard_map.84
  40.0 1.6 %collective-permute-start.8 = (bf16[256,640]{1,0:T(8,128)(2,1)S(1)}, bf16[256,640]{1,0:T(8,128)(2,1)S(1)}, u32[]{:S(2)}, u32[]{:S(2)}) collective-permute-start(bf16[256,640]{1,0:T(8,128)(2,1)S(1)} %get-tuple-element.33), channel_id=1, source_target_pairs={{0,32},{32,64},{64,96},{96,0},{1,33},{33,65},{65,97},{97,1},{2,34}... | collective-permute-start | bytes 983048 | tf_op jit(solution)/shard_map/ppermute | solution.py:290
  41.6 1.7 %collective-permute-start.9 = (bf16[256,640]{1,0:T(8,128)(2,1)S(1)}, bf16[256,640]{1,0:T(8,128)(2,1)S(1)}, u32[]{:S(2)}, u32[]{:S(2)}) collective-permute-start(bf16[256,640]{1,0:T(8,128)(2,1)S(1)} %get-tuple-element.36), channel_id=1, source_target_pairs={{0,96},{32,0},{64,32},{96,64},{1,97},{33,1},{65,33},{97,65},{2,98}... | collective-permute-start | bytes 983048 | tf_op jit(solution)/shard_map/ppermute | solution.py:290
  43.4 9.3 %shard_map.85 = (f32[640,512]{1,0:T(8,128)S(1)}, f32[8,512]{1,0:T(8,128)S(1)}, f32[640,512]{1,0:T(8,128)S(1)}, f32[8,512]{1,0:T(8,128)S(1)}) custom-call(bf16[512,640]{1,0:T(8,128)(2,1)S(1)} %collective-permute-done.6.refs_0_, bf16[512,640]{1,0:T(8,128)(2,1)S(1)} %collective-permute-done.7.refs_1_.refs_2_, bf16[512,640]{1,0:T(8,128)(2,1)S(1)} %copy-done.4, ...), custom_call_target="tpu_custom_call" | custom-call | flops 2684354560 | bytes 3932160 | tf_op jit(solution)/shard_map/pallas_call | solution.py:34
  52.7 5.4 %shard_map.86 = (f32[640,256]{1,0:T(8,128)S(1)}, f32[8,256]{1,0:T(8,128)S(1)}, f32[640,256]{1,0:T(8,128)S(1)}, f32[8,256]{1,0:T(8,128)S(1)}) custom-call(bf16[256,640]{1,0:T(8,128)(2,1)S(1)} %collective-permute-done.8.refs_0_.refs_1_, bf16[256,640]{1,0:T(8,128)(2,1)S(1)} %collective-permute-done.9.refs_1_, bf16[512,640]{1,0:T(8,128)(2,1)S(1)} %copy-done.4, ...), custom_call_target="tpu_custom_call" | custom-call | flops 1342177280 | bytes 3276800 | tf_op jit(solution)/shard_map/pallas_call | solution.py:34
  58.1 7.4 %shard_map.95 = (bf16[656,256]{1,0:T(8,128)(2,1)S(1)}, bf16[656,256]{1,0:T(8,128)(2,1)S(1)}, bf16[656,256]{1,0:T(8,128)(2,1)S(1)}) custom-call(bf16[512,640]{1,0:T(8,128)(2,1)S(1)} %collective-permute-done.6.refs_0_, bf16[256,640]{1,0:T(8,128)(2,1)S(1)} %collective-permute-done.9.refs_1_, bf16[512,640]{1,0:T(8,128)(2,1)S(1)} %collective-permute-done.7.refs_1_.refs_2_, ...), custom_call_target="tpu_custom_call" | custom-call | flops 2013265920 | bytes 7577600 | tf_op jit(solution)/shard_map/pallas_call | solution.py:34
  65.5 1.7 %collective-permute-start.19 = (bf16[656,256]{1,0:T(8,128)(2,1)S(1)}, bf16[656,256]{1,0:T(8,128)(2,1)S(1)}, u32[]{:S(2)}, u32[]{:S(2)}) collective-permute-start(bf16[656,256]{1,0:T(8,128)(2,1)S(1)} %get-tuple-element.50), channel_id=1, source_target_pairs={{0,96},{32,0},{64,32},{96,64},{1,97},{33,1},{65,33},{97,65},{2,98}... | collective-permute-start | bytes 1007624 | tf_op jit(solution)/shard_map/ppermute | solution.py:327
  67.2 0.7 collective-permute-start.20
  67.9 0.9 collective-permute-start.21
  68.8 7.3 %shard_map.87 = (bf16[656,256]{1,0:T(8,128)(2,1)S(1)}, bf16[656,256]{1,0:T(8,128)(2,1)S(1)}, bf16[656,256]{1,0:T(8,128)(2,1)S(1)}) custom-call(bf16[512,640]{1,0:T(8,128)(2,1)S(1)} %collective-permute-done.6.refs_0_, bf16[256,640]{1,0:T(8,128)(2,1)S(1)} %collective-permute-done.8.refs_0_.refs_1_, ...), custom_call_target="tpu_custom_call" | custom-call | flops 2013265920 | bytes 7577600 | tf_op jit(solution)/shard_map/pallas_call | solution.py:34
  76.1 2.4 %collective-permute-start.10 = (bf16[656,256]{1,0:T(8,128)(2,1)S(1)}, bf16[656,256]{1,0:T(8,128)(2,1)S(1)}, u32[]{:S(2)}, u32[]{:S(2)}) collective-permute-start(bf16[656,256]{1,0:T(8,128)(2,1)S(1)} %get-tuple-element.41), channel_id=1, source_target_pairs={{0,96},{32,0},{64,32},{96,64},{1,97},{33,1},{65,33},{97,65},{2,98}... | collective-permute-start | bytes 1007624 | tf_op jit(solution)/shard_map/ppermute | solution.py:327
  78.5 1.6 %collective-permute-start.11 = (bf16[656,256]{1,0:T(8,128)(2,1)S(1)}, bf16[656,256]{1,0:T(8,128)(2,1)S(1)}, u32[]{:S(2)}, u32[]{:S(2)}) collective-permute-start(bf16[656,256]{1,0:T(8,128)(2,1)S(1)} %get-tuple-element.42), channel_id=1, source_target_pairs={{0,64},{32,96},{64,0},{96,32},{1,65},{33,97},{65,1},{97,33},{2,66}... | collective-permute-start | bytes 1007624 | tf_op jit(solution)/shard_map/ppermute | solution.py:328
  80.2 4.6 %collective-permute-start.12 = (bf16[656,256]{1,0:T(8,128)(2,1)S(1)}, bf16[656,256]{1,0:T(8,128)(2,1)S(1)}, u32[]{:S(2)}, u32[]{:S(2)}) collective-permute-start(bf16[656,256]{1,0:T(8,128)(2,1)S(1)} %get-tuple-element.43), channel_id=1, source_target_pairs={{0,32},{32,64},{64,96},{96,0},{1,33},{33,65},{65,97},{97,1},{2,34}... | collective-permute-start | bytes 1007624 | tf_op jit(solution)/shard_map/ppermute | solution.py:329
  84.8 7.0 %shard_map.82 = (f32[640,512]{1,0:T(8,128)S(1)}, f32[8,512]{1,0:T(8,128)S(1)}) custom-call(bf16[512,640]{1,0:T(8,128)(2,1)} %refs_0_.5, bf16[512,640]{1,0:T(8,128)(2,1)} %refs_1_.1, bf16[512,640]{1,0:T(8,128)(2,1)} %refs_2_.3, bf16[512,640]{1,0:T(8,128)(2,1)S(1)} %collective-permute-done.refs_3_.refs_4_, ...), custom_call_target="tpu_custom_call" | custom-call | flops 1342177280 | tf_op jit(solution)/shard_map/pallas_call | solution.py:34
  91.7 4.0 %shard_map.94.refs_0_ = bf16[656,256]{1,0:T(8,128)(2,1)S(1)} custom-call(bf16[512,640]{1,0:T(8,128)(2,1)S(1)} %copy-done.1, f32[640,512]{1,0:T(8,128)S(1)} %get-tuple-element.31.refs_1_, f32[8,512]{1,0:T(8,128)S(1)} %get-tuple-element.32.refs_2_, bf16[512,640]{1,0:T(8,128)(2,1)S(1)} %collective-permute-done.2.refs_3_.refs_9_, ...), custom_call_target="tpu_custom_call" | custom-call | flops 671088640 | bytes 4603904 | tf_op jit(solution)/shard_map/pallas_call | solution.py:34
  95.7 0.4 shard_map.96.att_ref
  96.1 4.1 %collective-permute-start.22 = (bf16[256,640]{1,0:T(8,128)(2,1)S(1)}, bf16[256,640]{1,0:T(8,128)(2,1)S(1)}, u32[]{:S(2)}, u32[]{:S(2)}) collective-permute-start(bf16[256,640]{1,0:T(8,128)(2,1)S(1)} %shard_map.96.att_ref), channel_id=1, source_target_pairs={{0,1},{1,0},{2,3},{3,2},{4,5},{5,4},{6,7},{7,6},{8,9},{9,8},{10,11... | collective-permute-start | bytes 983048 | tf_op jit(solution)/shard_map/ppermute | solution.py:332
  100.2 4.0 %shard_map.83.refs_0_ = bf16[656,256]{1,0:T(8,128)(2,1)S(1)} custom-call(bf16[512,640]{1,0:T(8,128)(2,1)S(1)} %copy-done.1, f32[640,512]{1,0:T(8,128)S(1)} %get-tuple-element.31.refs_1_, f32[8,512]{1,0:T(8,128)S(1)} %get-tuple-element.32.refs_2_, bf16[512,640]{1,0:T(8,128)(2,1)S(1)} %collective-permute-done.2.refs_3_.refs_9_, ...), custom_call_target="tpu_custom_call" | custom-call | flops 671088640 | bytes 4603904 | tf_op jit(solution)/shard_map/pallas_call | solution.py:34
  104.2 0.4 shard_map.88.att_ref
  104.6 0.1 collective-permute-start.15
  104.7 2.1 %shard_map.90.w_ref = bf16[4,1280,640]{2,1,0:T(8,128)(2,1)S(1)} custom-call(bf16[640,5120]{1,0:T(8,128)(2,1)} %w_ref.3, bf16[1280,640]{1,0:T(8,128)(2,1)S(1)} %collective-permute-done.13.wz_ref, bf16[1280,640]{1,0:T(8,128)(2,1)S(1)} %collective-permute-done.14.ws_ref), custom_call_target="tpu_custom_call" | custom-call | tf_op jit(solution)/shard_map/pallas_call | solution.py:34
  106.8 1.3 shard_map.97.own_ref
  108.1 0.7 shard_map.99
  108.9 1.6 %collective-permute-start.23 = (bf16[256,640]{1,0:T(8,128)(2,1)S(1)}, bf16[256,640]{1,0:T(8,128)(2,1)S(1)}, u32[]{:S(2)}, u32[]{:S(2)}) collective-permute-start(bf16[256,640]{1,0:T(8,128)(2,1)S(1)} %get-tuple-element.54), channel_id=1, source_target_pairs={{0,2},{2,4},{4,6},{6,0},{1,3},{3,5},{5,7},{7,1},{8,10},{10,12},{12... | collective-permute-start | bytes 983048 | tf_op jit(solution)/shard_map/ppermute | solution.py:334
  110.5 1.7 %collective-permute-start.25 = (bf16[256,640]{1,0:T(8,128)(2,1)S(1)}, bf16[256,640]{1,0:T(8,128)(2,1)S(1)}, u32[]{:S(2)}, u32[]{:S(2)}) collective-permute-start(bf16[256,640]{1,0:T(8,128)(2,1)S(1)} %get-tuple-element.56), channel_id=1, source_target_pairs={{0,6},{2,0},{4,2},{6,4},{1,7},{3,1},{5,3},{7,5},{8,14},{10,8},{12,... | collective-permute-start | bytes 983048 | tf_op jit(solution)/shard_map/ppermute | solution.py:334
  112.2 0.7 shard_map.98
  112.9 2.1 %collective-permute-start.24 = (bf16[256,640]{1,0:T(8,128)(2,1)S(1)}, bf16[256,640]{1,0:T(8,128)(2,1)S(1)}, u32[]{:S(2)}, u32[]{:S(2)}) collective-permute-start(bf16[256,640]{1,0:T(8,128)(2,1)S(1)} %get-tuple-element.55), channel_id=1, source_target_pairs={{0,4},{2,6},{4,0},{6,2},{1,5},{3,7},{5,1},{7,3},{8,12},{10,14},{12... | collective-permute-start | bytes 983048 | tf_op jit(solution)/shard_map/ppermute | solution.py:334
  115.0 1.3 shard_map.91.own_ref
  116.3 0.7 shard_map.93
  117.1 0.7 collective-permute-start.16
  117.8 2.6 %collective-permute-start.18 = (bf16[256,640]{1,0:T(8,128)(2,1)S(1)}, bf16[256,640]{1,0:T(8,128)(2,1)S(1)}, u32[]{:S(2)}, u32[]{:S(2)}) collective-permute-start(bf16[256,640]{1,0:T(8,128)(2,1)S(1)} %get-tuple-element.47), channel_id=1, source_target_pairs={{0,6},{2,0},{4,2},{6,4},{1,7},{3,1},{5,3},{7,5},{8,14},{10,8},{12,... | collective-permute-start | bytes 983048 | tf_op jit(solution)/shard_map/ppermute | solution.py:334
  120.4 0.7 shard_map.92
  121.1 7.9 %collective-permute-start.17 = (bf16[256,640]{1,0:T(8,128)(2,1)S(1)}, bf16[256,640]{1,0:T(8,128)(2,1)S(1)}, u32[]{:S(2)}, u32[]{:S(2)}) collective-permute-start(bf16[256,640]{1,0:T(8,128)(2,1)S(1)} %get-tuple-element.46), channel_id=1, source_target_pairs={{0,4},{2,6},{4,0},{6,2},{1,5},{3,7},{5,1},{7,3},{8,12},{10,14},{12... | collective-permute-start | bytes 983048 | tf_op jit(solution)/shard_map/ppermute | solution.py:334
  129.1 4.5 %collective-permute-done.16.refs_1_ = bf16[256,640]{1,0:T(8,128)(2,1)S(1)} collective-permute-done((bf16[256,640]{1,0:T(8,128)(2,1)S(1)}, bf16[256,640]{1,0:T(8,128)(2,1)S(1)}, u32[]{:S(2)}, u32[]{:S(2)}) %collective-permute-start.16) | collective-permute-done | bytes 327712 | tf_op jit(solution)/shard_map/ppermute | solution.py:334
  133.6 5.6 %collective-permute-done.18.refs_3_ = bf16[256,640]{1,0:T(8,128)(2,1)S(1)} collective-permute-done((bf16[256,640]{1,0:T(8,128)(2,1)S(1)}, bf16[256,640]{1,0:T(8,128)(2,1)S(1)}, u32[]{:S(2)}, u32[]{:S(2)}) %collective-permute-start.18) | collective-permute-done | bytes 327712 | tf_op jit(solution)/shard_map/ppermute | solution.py:334
  139.2 1.8 %collective-permute-done.17.refs_2_ = bf16[256,640]{1,0:T(8,128)(2,1)S(1)} collective-permute-done((bf16[256,640]{1,0:T(8,128)(2,1)S(1)}, bf16[256,640]{1,0:T(8,128)(2,1)S(1)}, u32[]{:S(2)}, u32[]{:S(2)}) %collective-permute-start.17) | collective-permute-done | bytes 327712 | tf_op jit(solution)/shard_map/ppermute | solution.py:334
  141.1 1.3 shard_map.100
  (35 shorter events, 0.1 us)
Async XLA Ops:
  0.0 3.6 %copy-start.4 = (bf16[512,640]{1,0:T(8,128)(2,1)S(1)}, bf16[512,640]{1,0:T(8,128)(2,1)}, u32[]{:S(2)}) copy-start(bf16[512,640]{1,0:T(8,128)(2,1)} %refs_2_.5) | copy-start | bytes 1966084
  0.0 5.8 %copy-start.5 = (bf16[512,640]{1,0:T(8,128)(2,1)S(1)}, bf16[512,640]{1,0:T(8,128)(2,1)}, u32[]{:S(2)}) copy-start(bf16[512,640]{1,0:T(8,128)(2,1)} %refs_3_.3) | copy-start | bytes 1966084
  0.0 5.9 %copy-start = (bf16[512,640]{1,0:T(8,128)(2,1)S(1)}, bf16[512,640]{1,0:T(8,128)(2,1)}, u32[]{:S(2)}) copy-start(bf16[512,640]{1,0:T(8,128)(2,1)} %refs_0_.5) | copy-start | bytes 1966084
  1.6 37.8 %collective-permute-start.13 = (bf16[1280,640]{1,0:T(8,128)(2,1)S(1)}, bf16[1280,640]{1,0:T(8,128)(2,1)S(1)}, u32[]{:S(2)}, u32[]{:S(2)}) collective-permute-start(bf16[1280,640]{1,0:T(8,128)(2,1)S(1)} %shard_map.89), channel_id=1, source_target_pairs={{0,17},{17,0},{1,16},{16,1},{2,19},{19,2},{3,18},{18,3},{4,21},{21... | collective-permute-start | bytes 4915208 | tf_op jit(solution)/shard_map/ppermute | solution.py:301
  3.6 17.8 %collective-permute-start.2 = (bf16[512,640]{1,0:T(8,128)(2,1)S(1)}, bf16[512,640]{1,0:T(8,128)(2,1)S(1)}, u32[]{:S(2)}, u32[]{:S(2)}) collective-permute-start(bf16[512,640]{1,0:T(8,128)(2,1)S(1)} %copy-done.4), channel_id=1, source_target_pairs={{0,16},{16,0},{1,17},{17,1},{2,18},{18,2},{3,19},{19,3},{4,20},{20... | collective-permute-start | bytes 1966088 | tf_op jit(solution)/shard_map/ppermute | solution.py:283
  5.8 28.5 %collective-permute-start.3 = (bf16[512,640]{1,0:T(8,128)(2,1)S(1)}, bf16[512,640]{1,0:T(8,128)(2,1)S(1)}, u32[]{:S(2)}, u32[]{:S(2)}) collective-permute-start(bf16[512,640]{1,0:T(8,128)(2,1)S(1)} %copy-done.5), channel_id=1, source_target_pairs={{0,16},{16,0},{1,17},{17,1},{2,18},{18,2},{3,19},{19,3},{4,20},{20... | collective-permute-start | bytes 1966088 | tf_op jit(solution)/shard_map/ppermute | solution.py:284
  5.9 33.5 %collective-permute-start.6 = (bf16[512,640]{1,0:T(8,128)(2,1)S(1)}, bf16[512,640]{1,0:T(8,128)(2,1)S(1)}, u32[]{:S(2)}, u32[]{:S(2)}) collective-permute-start(bf16[512,640]{1,0:T(8,128)(2,1)S(1)} %copy-done), channel_id=1, source_target_pairs={{0,32},{32,64},{64,96},{96,0},{1,33},{33,65},{65,97},{97,1},{2,34}... | collective-permute-start | bytes 1966088 | tf_op jit(solution)/shard_map/ppermute | solution.py:285
  7.4 32.5 %collective-permute-start.7 = (bf16[512,640]{1,0:T(8,128)(2,1)S(1)}, bf16[512,640]{1,0:T(8,128)(2,1)S(1)}, u32[]{:S(2)}, u32[]{:S(2)}) collective-permute-start(bf16[512,640]{1,0:T(8,128)(2,1)S(1)} %copy-done), channel_id=1, source_target_pairs={{0,96},{32,0},{64,32},{96,64},{1,97},{33,1},{65,33},{97,65},{2,98}... | collective-permute-start | bytes 1966088 | tf_op jit(solution)/shard_map/ppermute | solution.py:286
  21.4 18.6 %collective-permute-start = (bf16[512,640]{1,0:T(8,128)(2,1)S(1)}, bf16[512,640]{1,0:T(8,128)(2,1)S(1)}, u32[]{:S(2)}, u32[]{:S(2)}) collective-permute-start(bf16[512,640]{1,0:T(8,128)(2,1)S(1)} %copy-done.4), channel_id=1, source_target_pairs={{0,8},{8,0},{1,9},{9,1},{2,10},{10,2},{3,11},{11,3},{4,12},{12,4},... | collective-permute-start | bytes 1966088 | tf_op jit(solution)/shard_map/ppermute | solution.py:281
  34.3 7.3 %collective-permute-start.1 = (bf16[512,640]{1,0:T(8,128)(2,1)S(1)}, bf16[512,640]{1,0:T(8,128)(2,1)S(1)}, u32[]{:S(2)}, u32[]{:S(2)}) collective-permute-start(bf16[512,640]{1,0:T(8,128)(2,1)S(1)} %copy-done.5), channel_id=1, source_target_pairs={{0,8},{8,0},{1,9},{9,1},{2,10},{10,2},{3,11},{11,3},{4,12},{12,4},... | collective-permute-start | bytes 1966088 | tf_op jit(solution)/shard_map/ppermute | solution.py:282
  39.4 65.3 %collective-permute-start.14 = (bf16[1280,640]{1,0:T(8,128)(2,1)S(1)}, bf16[1280,640]{1,0:T(8,128)(2,1)S(1)}, u32[]{:S(2)}, u32[]{:S(2)}) collective-permute-start(bf16[1280,640]{1,0:T(8,128)(2,1)S(1)} %collective-permute-done.13.wz_ref), channel_id=1, source_target_pairs={{0,8},{8,0},{1,9},{9,1},{2,10},{10,2},{3,11},{11,3},{4,12},{12,4},... | collective-permute-start | bytes 4915208 | tf_op jit(solution)/shard_map/ppermute | solution.py:302
  39.4 18.7 %collective-permute-start.4 = (bf16[512,640]{1,0:T(8,128)(2,1)S(1)}, bf16[512,640]{1,0:T(8,128)(2,1)S(1)}, u32[]{:S(2)}, u32[]{:S(2)}) collective-permute-start(bf16[512,640]{1,0:T(8,128)(2,1)S(1)} %collective-permute-done.2.refs_3_.refs_9_), channel_id=1, source_target_pairs={{0,8},{8,0},{1,9},{9,1},{2,10},{10,2},{3,11},{11,3},{4,12},{12,4},... | collective-permute-start | bytes 1966088 | tf_op jit(solution)/shard_map/ppermute | solution.py:287
  39.9 18.2 %collective-permute-start.5 = (bf16[512,640]{1,0:T(8,128)(2,1)S(1)}, bf16[512,640]{1,0:T(8,128)(2,1)S(1)}, u32[]{:S(2)}, u32[]{:S(2)}) collective-permute-start(bf16[512,640]{1,0:T(8,128)(2,1)S(1)} %collective-permute-done.3.refs_4_.refs_10_), channel_id=1, source_target_pairs={{0,8},{8,0},{1,9},{9,1},{2,10},{10,2},{3,11},{11,3},{4,12},{12,4},... | collective-permute-start | bytes 1966088 | tf_op jit(solution)/shard_map/ppermute | solution.py:288
  40.0 12.6 %collective-permute-start.8 = (bf16[256,640]{1,0:T(8,128)(2,1)S(1)}, bf16[256,640]{1,0:T(8,128)(2,1)S(1)}, u32[]{:S(2)}, u32[]{:S(2)}) collective-permute-start(bf16[256,640]{1,0:T(8,128)(2,1)S(1)} %get-tuple-element.33), channel_id=1, source_target_pairs={{0,32},{32,64},{64,96},{96,0},{1,33},{33,65},{65,97},{97,1},{2,34}... | collective-permute-start | bytes 983048 | tf_op jit(solution)/shard_map/ppermute | solution.py:290
  41.6 11.1 %collective-permute-start.9 = (bf16[256,640]{1,0:T(8,128)(2,1)S(1)}, bf16[256,640]{1,0:T(8,128)(2,1)S(1)}, u32[]{:S(2)}, u32[]{:S(2)}) collective-permute-start(bf16[256,640]{1,0:T(8,128)(2,1)S(1)} %get-tuple-element.36), channel_id=1, source_target_pairs={{0,96},{32,0},{64,32},{96,64},{1,97},{33,1},{65,33},{97,65},{2,98}... | collective-permute-start | bytes 983048 | tf_op jit(solution)/shard_map/ppermute | solution.py:290
  65.5 13.1 %collective-permute-start.19 = (bf16[656,256]{1,0:T(8,128)(2,1)S(1)}, bf16[656,256]{1,0:T(8,128)(2,1)S(1)}, u32[]{:S(2)}, u32[]{:S(2)}) collective-permute-start(bf16[656,256]{1,0:T(8,128)(2,1)S(1)} %get-tuple-element.50), channel_id=1, source_target_pairs={{0,96},{32,0},{64,32},{96,64},{1,97},{33,1},{65,33},{97,65},{2,98}... | collective-permute-start | bytes 1007624 | tf_op jit(solution)/shard_map/ppermute | solution.py:327
  67.2 13.0 %collective-permute-start.20 = (bf16[656,256]{1,0:T(8,128)(2,1)S(1)}, bf16[656,256]{1,0:T(8,128)(2,1)S(1)}, u32[]{:S(2)}, u32[]{:S(2)}) collective-permute-start(bf16[656,256]{1,0:T(8,128)(2,1)S(1)} %get-tuple-element.51), channel_id=1, source_target_pairs={{0,64},{32,96},{64,0},{96,32},{1,65},{33,97},{65,1},{97,33},{2,66}... | collective-permute-start | bytes 1007624 | tf_op jit(solution)/shard_map/ppermute | solution.py:328
  67.9 27.8 %collective-permute-start.21 = (bf16[656,256]{1,0:T(8,128)(2,1)S(1)}, bf16[656,256]{1,0:T(8,128)(2,1)S(1)}, u32[]{:S(2)}, u32[]{:S(2)}) collective-permute-start(bf16[656,256]{1,0:T(8,128)(2,1)S(1)} %get-tuple-element.52), channel_id=1, source_target_pairs={{0,32},{32,64},{64,96},{96,0},{1,33},{33,65},{65,97},{97,1},{2,34}... | collective-permute-start | bytes 1007624 | tf_op jit(solution)/shard_map/ppermute | solution.py:329
  76.1 28.1 %collective-permute-start.10 = (bf16[656,256]{1,0:T(8,128)(2,1)S(1)}, bf16[656,256]{1,0:T(8,128)(2,1)S(1)}, u32[]{:S(2)}, u32[]{:S(2)}) collective-permute-start(bf16[656,256]{1,0:T(8,128)(2,1)S(1)} %get-tuple-element.41), channel_id=1, source_target_pairs={{0,96},{32,0},{64,32},{96,64},{1,97},{33,1},{65,33},{97,65},{2,98}... | collective-permute-start | bytes 1007624 | tf_op jit(solution)/shard_map/ppermute | solution.py:327
  78.5 25.7 %collective-permute-start.11 = (bf16[656,256]{1,0:T(8,128)(2,1)S(1)}, bf16[656,256]{1,0:T(8,128)(2,1)S(1)}, u32[]{:S(2)}, u32[]{:S(2)}) collective-permute-start(bf16[656,256]{1,0:T(8,128)(2,1)S(1)} %get-tuple-element.42), channel_id=1, source_target_pairs={{0,64},{32,96},{64,0},{96,32},{1,65},{33,97},{65,1},{97,33},{2,66}... | collective-permute-start | bytes 1007624 | tf_op jit(solution)/shard_map/ppermute | solution.py:328
  80.2 11.6 %copy-start.1 = (bf16[512,640]{1,0:T(8,128)(2,1)S(1)}, bf16[512,640]{1,0:T(8,128)(2,1)}, u32[]{:S(2)}) copy-start(bf16[512,640]{1,0:T(8,128)(2,1)} %refs_0_.5) | copy-start | bytes 1966084
  80.2 24.1 %collective-permute-start.12 = (bf16[656,256]{1,0:T(8,128)(2,1)S(1)}, bf16[656,256]{1,0:T(8,128)(2,1)S(1)}, u32[]{:S(2)}, u32[]{:S(2)}) collective-permute-start(bf16[656,256]{1,0:T(8,128)(2,1)S(1)} %get-tuple-element.43), channel_id=1, source_target_pairs={{0,32},{32,64},{64,96},{96,0},{1,33},{33,65},{65,97},{97,1},{2,34}... | collective-permute-start | bytes 1007624 | tf_op jit(solution)/shard_map/ppermute | solution.py:329
  96.1 12.0 %collective-permute-start.22 = (bf16[256,640]{1,0:T(8,128)(2,1)S(1)}, bf16[256,640]{1,0:T(8,128)(2,1)S(1)}, u32[]{:S(2)}, u32[]{:S(2)}) collective-permute-start(bf16[256,640]{1,0:T(8,128)(2,1)S(1)} %shard_map.96.att_ref), channel_id=1, source_target_pairs={{0,1},{1,0},{2,3},{3,2},{4,5},{5,4},{6,7},{7,6},{8,9},{9,8},{10,11... | collective-permute-start | bytes 983048 | tf_op jit(solution)/shard_map/ppermute | solution.py:332
  104.6 11.7 %collective-permute-start.15 = (bf16[256,640]{1,0:T(8,128)(2,1)S(1)}, bf16[256,640]{1,0:T(8,128)(2,1)S(1)}, u32[]{:S(2)}, u32[]{:S(2)}) collective-permute-start(bf16[256,640]{1,0:T(8,128)(2,1)S(1)} %shard_map.88.att_ref), channel_id=1, source_target_pairs={{0,1},{1,0},{2,3},{3,2},{4,5},{5,4},{6,7},{7,6},{8,9},{9,8},{10,11... | collective-permute-start | bytes 983048 | tf_op jit(solution)/shard_map/ppermute | solution.py:332
  108.9 12.3 %collective-permute-start.23 = (bf16[256,640]{1,0:T(8,128)(2,1)S(1)}, bf16[256,640]{1,0:T(8,128)(2,1)S(1)}, u32[]{:S(2)}, u32[]{:S(2)}) collective-permute-start(bf16[256,640]{1,0:T(8,128)(2,1)S(1)} %get-tuple-element.54), channel_id=1, source_target_pairs={{0,2},{2,4},{4,6},{6,0},{1,3},{3,5},{5,7},{7,1},{8,10},{10,12},{12... | collective-permute-start | bytes 983048 | tf_op jit(solution)/shard_map/ppermute | solution.py:334
  110.5 18.6 %collective-permute-start.25 = (bf16[256,640]{1,0:T(8,128)(2,1)S(1)}, bf16[256,640]{1,0:T(8,128)(2,1)S(1)}, u32[]{:S(2)}, u32[]{:S(2)}) collective-permute-start(bf16[256,640]{1,0:T(8,128)(2,1)S(1)} %get-tuple-element.56), channel_id=1, source_target_pairs={{0,6},{2,0},{4,2},{6,4},{1,7},{3,1},{5,3},{7,5},{8,14},{10,8},{12,... | collective-permute-start | bytes 983048 | tf_op jit(solution)/shard_map/ppermute | solution.py:334
  112.9 16.2 %collective-permute-start.24 = (bf16[256,640]{1,0:T(8,128)(2,1)S(1)}, bf16[256,640]{1,0:T(8,128)(2,1)S(1)}, u32[]{:S(2)}, u32[]{:S(2)}) collective-permute-start(bf16[256,640]{1,0:T(8,128)(2,1)S(1)} %get-tuple-element.55), channel_id=1, source_target_pairs={{0,4},{2,6},{4,0},{6,2},{1,5},{3,7},{5,1},{7,3},{8,12},{10,14},{12... | collective-permute-start | bytes 983048 | tf_op jit(solution)/shard_map/ppermute | solution.py:334
  117.1 16.5 %collective-permute-start.16 = (bf16[256,640]{1,0:T(8,128)(2,1)S(1)}, bf16[256,640]{1,0:T(8,128)(2,1)S(1)}, u32[]{:S(2)}, u32[]{:S(2)}) collective-permute-start(bf16[256,640]{1,0:T(8,128)(2,1)S(1)} %get-tuple-element.45), channel_id=1, source_target_pairs={{0,2},{2,4},{4,6},{6,0},{1,3},{3,5},{5,7},{7,1},{8,10},{10,12},{12... | collective-permute-start | bytes 983048 | tf_op jit(solution)/shard_map/ppermute | solution.py:334
  117.8 23.3 %copy-start.2 = (bf16[512,640]{1,0:T(8,128)(2,1)S(1)}, bf16[512,640]{1,0:T(8,128)(2,1)}, u32[]{:S(2)}) copy-start(bf16[512,640]{1,0:T(8,128)(2,1)} %residual_ref.1) | copy-start | bytes 1966084
  117.8 23.3 %copy-start.3 = (f32[640]{0:T(1024)S(1)}, f32[640]{0:T(1024)}, u32[]{:S(2)}) copy-start(f32[640]{0:T(1024)} %gate_ref.1) | copy-start | bytes 7684
  117.8 21.4 %collective-permute-start.18 = (bf16[256,640]{1,0:T(8,128)(2,1)S(1)}, bf16[256,640]{1,0:T(8,128)(2,1)S(1)}, u32[]{:S(2)}, u32[]{:S(2)}) collective-permute-start(bf16[256,640]{1,0:T(8,128)(2,1)S(1)} %get-tuple-element.47), channel_id=1, source_target_pairs={{0,6},{2,0},{4,2},{6,4},{1,7},{3,1},{5,3},{7,5},{8,14},{10,8},{12,... | collective-permute-start | bytes 983048 | tf_op jit(solution)/shard_map/ppermute | solution.py:334
  121.1 20.0 %collective-permute-start.17 = (bf16[256,640]{1,0:T(8,128)(2,1)S(1)}, bf16[256,640]{1,0:T(8,128)(2,1)S(1)}, u32[]{:S(2)}, u32[]{:S(2)}) collective-permute-start(bf16[256,640]{1,0:T(8,128)(2,1)S(1)} %get-tuple-element.46), channel_id=1, source_target_pairs={{0,4},{2,6},{4,0},{6,2},{1,5},{3,7},{5,1},{7,3},{8,12},{10,14},{12... | collective-permute-start | bytes 983048 | tf_op jit(solution)/shard_map/ppermute | solution.py:334
